TPU v7x, 32 devices: a whole 2x2x4 slice. The times are simulated.
32 devices in a mesh: dp: 4 (over y, x), expert: 8 (over z, core).
Axes of the slice: x: 2, y: 2, z: 4, core: 2. Of those that a mesh axis runs over, the one named last changes fastest.
Arguments:
- tokens: bfloat16 [3, 8192, 768], P(None, ('dp', 'expert')), may hold values from -6 to 6
- cotangent: bfloat16 [3, 8192, 768], P(None, ('dp', 'expert')), may hold values from -6 to 6
- routes: int32 [3, 8192, 2], P(None, ('dp', 'expert')), may hold values from 0 to 7, all different within a row; in each aligned block of 256 rows (0 to 255, 256 to 511, ..., all dimensions but the last counted through in order) at most 128 rows name the same one
- attn_norm: bfloat16 [768], P('dp'), may hold values from 0.099609375 to 1.8984375
- query_weight: bfloat16 [768, 768], P('dp'), may hold values from -0.3125 to 0.3125
- key_weight: bfloat16 [768, 768], P('dp'), may hold values from -0.3125 to 0.3125
- value_weight: bfloat16 [768, 768], P('dp'), may hold values from -0.21875 to 0.21875
- out_weight: bfloat16 [768, 768], P('dp'), may hold values from -0.875 to 0.875
- ffn_norm: bfloat16 [768], P('dp'), may hold values from 0.099609375 to 1.8984375
- router_weight: bfloat16 [768, 8], P('dp'), may hold values from -0.15625 to 0.15625
- shared_gate: bfloat16 [768, 2048], P('dp'), may hold values from -0.21875 to 0.21875
- shared_up: bfloat16 [768, 2048], P('dp'), may hold values from -0.21875 to 0.21875
- shared_down: bfloat16 [2048, 768], P('dp'), may hold values from -0.125 to 0.125
- expert_gate: bfloat16 [8, 768, 2048], P('expert', 'dp'), may hold values from -0.21875 to 0.21875
- expert_up: bfloat16 [8, 768, 2048], P('expert', 'dp'), may hold values from -0.21875 to 0.21875
- expert_down: bfloat16 [8, 2048, 768], P('expert', 'dp'), may hold values from -1 to 1
Outputs:
- output: bfloat16 [3, 8192, 768], P(None, ('dp', 'expert'))
- input_grad: bfloat16 [3, 8192, 768], P(None, ('dp', 'expert'))
- attn_norm_grad: float32 [768], P('dp')
- query_grad: float32 [768, 768], P('dp')
- key_grad: float32 [768, 768], P('dp')
- value_grad: float32 [768, 768], P('dp')
- out_grad: float32 [768, 768], P('dp')
- ffn_norm_grad: float32 [768], P('dp')
- router_grad: float32 [768, 8], P('dp')
- shared_gate_grad: float32 [768, 2048], P('dp')
- shared_up_grad: float32 [768, 2048], P('dp')
- shared_down_grad: float32 [2048, 768], P('dp')
- expert_gate_grad: float32 [8, 768, 2048], P('expert', 'dp')
- expert_up_grad: float32 [8, 768, 2048], P('expert', 'dp')
- expert_down_grad: float32 [8, 2048, 768], P('expert', 'dp')
Inputs may be any that keep to these rules, and one draw needn't show every extreme that they name: `routes`: each row names two different experts. In each aligned block of 256 rows (the rows of one device in one micro-batch) no expert is named by more than 128 rows.
All inputs are finite; a program needn't handle non-finite values.
Results may differ from a plain program's by a relative error of at most 0.025.
Values may be sent and summed in bfloat16 or wider, within the bound.
A program may use at most 384 MiB of HBM per device.

v0:
```python
import math

import jax
import jax.numpy as jnp
from jax import lax
from jax.sharding import PartitionSpec as P

HEADS = 12
HD = 64
PROMPT = 1024
CLEN = 128


epsilon = 1e-05
neg_large = -1e30
highest = lax.Precision.HIGHEST


def from_root(value, axis, source):
    kept = jnp.where(lax.axis_index(axis) == source, value, 0).astype(value.dtype)
    return lax.psum(kept, axis)


def matmul(left_side, right_side):
    return jnp.dot(left_side, right_side, preferred_element_type=jnp.float32)


def contract_rows(left_side, right_side):
    return lax.dot_general(
        left_side, right_side, (((0,), (0,)), ((), ())), preferred_element_type=jnp.float32
    )


def times_transpose(left_side, right_side):
    return lax.dot_general(
        left_side, right_side, (((1,), (1,)), ((), ())), preferred_element_type=jnp.float32
    )


def silu_parts(pre_act):
    sigma_val = jax.nn.sigmoid(pre_act)
    return (pre_act * sigma_val, sigma_val * (1.0 + pre_act * (1.0 - sigma_val)))


def rotary(positions):
    middle = HD // 2
    frequency = jnp.exp(jnp.arange(middle).astype(jnp.float32) * (-2.0 * math.log(10000.0) / HD))
    angles = positions.astype(jnp.float32)[:, None] * frequency[None, :]
    return (jnp.cos(angles), jnp.sin(angles))


def turn_heads(values, cos_table, sine_table, direction):
    layout = values.shape
    by_head = values.reshape(layout[:-1] + (HEADS, HD))
    middle = HD // 2
    leading = by_head[..., :middle]
    trailing = by_head[..., middle:]
    cos_heads = cos_table[:, None, :]
    sine_heads = sine_table[:, None, :] * direction
    turned = jnp.concatenate(
        [leading * cos_heads - trailing * sine_heads, trailing * cos_heads + leading * sine_heads],
        axis=-1,
    )
    return turned.reshape(layout)


def key_mask(query_pos, key_pos, own_flags):
    is_later = query_pos[:, None] >= PROMPT
    before = key_pos[None, :] <= query_pos[:, None]
    same_doc = (key_pos[None, :] - PROMPT) // CLEN == (query_pos[:, None] - PROMPT) // CLEN
    return jnp.where(own_flags[None, :], is_later & before & same_doc, is_later | before)


def head_scores(queries, key_rows, allowed):
    tok_rows = queries.shape[0]
    scores = jnp.einsum(
        "qhd,khd->hqk",
        queries.reshape(tok_rows, HEADS, HD),
        key_rows.reshape(-1, HEADS, HD),
        preferred_element_type=jnp.float32,
    ) * (1.0 / math.sqrt(HD))
    return jnp.where(allowed[None], scores, neg_large)


def forward_pass(gathered, token_rows, route_ids):
    (
        attn_norm,
        query_weight,
        key_weight,
        value_weight,
        out_weight,
        ffn_norm,
        router_weight,
        shared_gate,
        shared_up,
        shared_down,
        expert_gate,
        expert_up,
        expert_down,
    ) = gathered
    tok_rows = token_rows.shape[0]
    model_width = token_rows.shape[1]
    experts = router_weight.shape[1]
    capacity = 4 * tok_rows // experts
    hidden_in = token_rows.astype(jnp.float32)
    inverse_one = lax.rsqrt(jnp.mean(hidden_in * hidden_in, axis=-1, keepdims=True) + epsilon)
    normed = (hidden_in * inverse_one * attn_norm.astype(jnp.float32)).astype(jnp.bfloat16)
    offset = lax.axis_index("expert") * tok_rows
    query_pos = offset + jnp.arange(tok_rows, dtype=jnp.int32)
    rope_pos = jnp.where(query_pos < PROMPT, query_pos, PROMPT + (query_pos - PROMPT) % CLEN)
    cos_table, sine_table = rotary(rope_pos)
    queries = turn_heads(matmul(normed, query_weight), cos_table, sine_table, 1.0).astype(
        jnp.bfloat16
    )
    own_keys = turn_heads(matmul(normed, key_weight), cos_table, sine_table, 1.0).astype(
        jnp.bfloat16
    )
    own_values = matmul(normed, value_weight).astype(jnp.bfloat16)
    own_pairs = jnp.concatenate([own_keys, own_values], axis=1)
    prompt_parts = []
    for prompt_root in range(PROMPT // tok_rows):
        prompt_parts.append(from_root(own_pairs, "expert", prompt_root))
    key_value = jnp.concatenate(prompt_parts + [own_pairs], axis=0)
    key_rows = key_value[:, :model_width]
    value_rows = key_value[:, model_width:]
    key_pos = jnp.concatenate([jnp.arange(PROMPT, dtype=jnp.int32), query_pos])
    own_flags = jnp.arange(PROMPT + tok_rows) >= PROMPT
    allowed = key_mask(query_pos, key_pos, own_flags)
    scores = head_scores(queries, key_rows, allowed)
    row_top = jnp.max(scores, axis=-1, keepdims=True)
    row_exp = jnp.exp(scores - row_top)
    row_total = jnp.sum(row_exp, axis=-1, keepdims=True)
    log_total = row_top + jnp.log(row_total)
    attn_probs = row_exp / row_total
    attended = jnp.einsum(
        "hqk,khd->qhd",
        attn_probs.astype(jnp.bfloat16),
        value_rows.reshape(-1, HEADS, HD),
        preferred_element_type=jnp.float32,
    )
    attended = attended.reshape(tok_rows, model_width).astype(jnp.bfloat16)
    residual = hidden_in + matmul(attended, out_weight)
    inverse_two = lax.rsqrt(jnp.mean(residual * residual, axis=-1, keepdims=True) + epsilon)
    mixed_in = (residual * inverse_two * ffn_norm.astype(jnp.float32)).astype(jnp.bfloat16)
    router_probs = jax.nn.softmax(matmul(mixed_in, router_weight), axis=-1)
    chosen = (route_ids[:, :, None] == jnp.arange(experts, dtype=jnp.int32)[None, None, :]).astype(
        jnp.float32
    )
    gate_values = jnp.sum(router_probs[:, None, :] * chosen, axis=-1)
    pair_expert = route_ids.reshape(-1)
    member = (pair_expert[:, None] == jnp.arange(experts, dtype=jnp.int32)[None, :]).astype(
        jnp.int32
    )
    rank_ids = jnp.sum((jnp.cumsum(member, axis=0) - member) * member, axis=1)
    slot_ids = pair_expert * capacity + rank_ids
    placing = (
        slot_ids[:, None] == jnp.arange(experts * capacity, dtype=jnp.int32)[None, :]
    ).astype(jnp.bfloat16)
    token_place = jnp.sum(placing.reshape(tok_rows, 2, experts * capacity), axis=1)
    outbound = (
        contract_rows(token_place, mixed_in)
        .astype(jnp.bfloat16)
        .reshape(experts, capacity, model_width)
    )
    received = lax.all_to_all(outbound, "expert", split_axis=0, concat_axis=0, tiled=True)
    sources = received.shape[0]
    count_items = received.shape[1]
    flat_rows = received.reshape(-1, model_width)
    gate_pre = matmul(flat_rows, expert_gate[0])
    up_pre = matmul(flat_rows, expert_up[0])
    hidden_rows = (jax.nn.silu(gate_pre) * up_pre).astype(jnp.bfloat16)
    produced = (
        matmul(hidden_rows, expert_down[0])
        .astype(jnp.bfloat16)
        .reshape(sources, count_items, model_width)
    )
    returned = lax.all_to_all(produced, "expert", split_axis=0, concat_axis=0, tiled=True)
    kept_gate = gate_pre.reshape(sources, count_items, -1)
    kept_up = up_pre.reshape(sources, count_items, -1)
    kept_hidden = hidden_rows.reshape(sources, count_items, -1)
    pair_out = matmul(placing, returned.reshape(-1, model_width)).reshape(tok_rows, 2, model_width)
    moe_out = jnp.sum(gate_values[:, :, None] * pair_out, axis=1)
    shared_g = matmul(mixed_in, shared_gate)
    shared_u = matmul(mixed_in, shared_up)
    shared_h = (jax.nn.silu(shared_g) * shared_u).astype(jnp.bfloat16)
    output_rows = residual + matmul(shared_h, shared_down) + moe_out
    kept_state = {
        "hidden_in": hidden_in,
        "inverse_one": inverse_one,
        "normed": normed,
        "offset": offset,
        "cos_table": cos_table,
        "sine_table": sine_table,
        "queries": queries,
        "key_rows": key_rows,
        "value_rows": value_rows,
        "allowed": allowed,
        "log_total": log_total,
        "attended": attended,
        "residual": residual,
        "inverse_two": inverse_two,
        "mixed_in": mixed_in,
        "router_probs": router_probs,
        "chosen": chosen,
        "gate_values": gate_values,
        "placing": placing,
        "token_place": token_place,
        "pair_out": pair_out,
        "kept_in": received,
        "kept_gate": kept_gate,
        "kept_up": kept_up,
        "kept_hidden": kept_hidden,
        "shared_g": shared_g,
        "shared_u": shared_u,
        "shared_h": shared_h,
    }
    return (output_rows.astype(jnp.bfloat16), kept_state)


def backward_pass(gathered, kept_state, cot_rows):
    (
        attn_norm,
        query_weight,
        key_weight,
        value_weight,
        out_weight,
        ffn_norm,
        router_weight,
        shared_gate,
        shared_up,
        shared_down,
        expert_gate,
        expert_up,
        expert_down,
    ) = gathered
    tok_rows = cot_rows.shape[0]
    model_width = cot_rows.shape[1]
    experts = router_weight.shape[1]
    capacity = 4 * tok_rows // experts
    mixed_in = kept_state["mixed_in"]
    grad_out = cot_rows.astype(jnp.float32)
    shared_down_grad = contract_rows(kept_state["shared_h"], cot_rows)
    shared_dh = times_transpose(cot_rows, shared_down)
    shared_act, shared_slope = silu_parts(kept_state["shared_g"])
    shared_dg = (shared_dh * kept_state["shared_u"] * shared_slope).astype(jnp.bfloat16)
    shared_du = (shared_dh * shared_act).astype(jnp.bfloat16)
    shared_gate_grad = contract_rows(mixed_in, shared_dg)
    shared_up_grad = contract_rows(mixed_in, shared_du)
    mixed_grad = times_transpose(shared_dg, shared_gate) + times_transpose(shared_du, shared_up)
    router_probs = kept_state["router_probs"]
    gate_grad = jnp.sum(grad_out[:, None, :] * kept_state["pair_out"], axis=-1)
    prob_grad = jnp.sum(gate_grad[:, :, None] * kept_state["chosen"], axis=1)
    logit_grad = router_probs * (
        prob_grad - jnp.sum(router_probs * prob_grad, axis=-1, keepdims=True)
    )
    router_grad = lax.dot_general(
        mixed_in.astype(jnp.float32),
        logit_grad,
        (((0,), (0,)), ((), ())),
        precision=highest,
        preferred_element_type=jnp.float32,
    )
    mixed_grad = mixed_grad + lax.dot_general(
        logit_grad,
        router_weight.astype(jnp.float32),
        (((1,), (1,)), ((), ())),
        precision=highest,
        preferred_element_type=jnp.float32,
    )
    pair_grad = (
        (kept_state["gate_values"][:, :, None] * grad_out[:, None, :])
        .reshape(-1, model_width)
        .astype(jnp.bfloat16)
    )
    outbound = (
        contract_rows(kept_state["placing"], pair_grad)
        .astype(jnp.bfloat16)
        .reshape(experts, capacity, model_width)
    )
    arrived = lax.all_to_all(outbound, "expert", split_axis=0, concat_axis=0, tiled=True).reshape(
        -1, model_width
    )
    expert_hidden = kept_state["kept_hidden"].reshape(-1, kept_state["kept_hidden"].shape[2])
    expert_gate_pre = kept_state["kept_gate"].reshape(expert_hidden.shape)
    expert_up_pre = kept_state["kept_up"].reshape(expert_hidden.shape)
    expert_rows = kept_state["kept_in"].reshape(-1, model_width)
    expert_down_grad = contract_rows(expert_hidden, arrived)[None]
    hidden_grad = times_transpose(arrived, expert_down[0])
    expert_act, expert_slope = silu_parts(expert_gate_pre)
    expert_dg = (hidden_grad * expert_up_pre * expert_slope).astype(jnp.bfloat16)
    expert_du = (hidden_grad * expert_act).astype(jnp.bfloat16)
    expert_gate_grad = contract_rows(expert_rows, expert_dg)[None]
    expert_up_grad = contract_rows(expert_rows, expert_du)[None]
    sent_back = (
        (times_transpose(expert_dg, expert_gate[0]) + times_transpose(expert_du, expert_up[0]))
        .astype(jnp.bfloat16)
        .reshape(experts, capacity, model_width)
    )
    came_back = lax.all_to_all(
        sent_back, "expert", split_axis=0, concat_axis=0, tiled=True
    ).reshape(-1, model_width)
    mixed_grad = mixed_grad + matmul(kept_state["token_place"], came_back)
    residual = kept_state["residual"]
    inverse_two = kept_state["inverse_two"]
    hat_two = residual * inverse_two
    ffn_norm_grad = jnp.sum(mixed_grad * hat_two, axis=0)
    scaled_two = mixed_grad * ffn_norm.astype(jnp.float32)
    residual_grad = grad_out + inverse_two * (
        scaled_two - hat_two * jnp.mean(scaled_two * hat_two, axis=-1, keepdims=True)
    )
    attn_grad = residual_grad.astype(jnp.bfloat16)
    out_grad = contract_rows(kept_state["attended"], attn_grad)
    attended_grad = times_transpose(attn_grad, out_weight).astype(jnp.bfloat16)
    queries = kept_state["queries"]
    key_rows = kept_state["key_rows"]
    value_rows = kept_state["value_rows"]
    scores = head_scores(queries, key_rows, kept_state["allowed"])
    attn_probs = jnp.exp(scores - kept_state["log_total"])
    grad_heads = attended_grad.reshape(tok_rows, HEADS, HD)
    prob_grad_attn = jnp.einsum(
        "qhd,khd->hqk",
        grad_heads,
        value_rows.reshape(-1, HEADS, HD),
        preferred_element_type=jnp.float32,
    )
    row_delta = jnp.sum(attn_probs * prob_grad_attn, axis=-1, keepdims=True)
    score_grad = (attn_probs * (prob_grad_attn - row_delta)).astype(jnp.bfloat16)
    score_scale = 1.0 / math.sqrt(HD)
    query_side = (
        jnp.einsum(
            "hqk,khd->qhd",
            score_grad,
            key_rows.reshape(-1, HEADS, HD),
            preferred_element_type=jnp.float32,
        ).reshape(tok_rows, model_width)
        * score_scale
    )
    key_side = (
        jnp.einsum(
            "hqk,qhd->khd",
            score_grad,
            queries.reshape(tok_rows, HEADS, HD),
            preferred_element_type=jnp.float32,
        ).reshape(-1, model_width)
        * score_scale
    )
    value_side = jnp.einsum(
        "hqk,qhd->khd",
        attn_probs.astype(jnp.bfloat16),
        grad_heads,
        preferred_element_type=jnp.float32,
    ).reshape(-1, model_width)
    pair_grads = jnp.concatenate([key_side, value_side], axis=1)
    group_rows = lax.axis_size("expert") * tok_rows
    padded_grads = jnp.concatenate(
        [pair_grads[:PROMPT], jnp.zeros((group_rows - PROMPT, 2 * model_width), jnp.float32)],
        axis=0,
    )
    own_share = lax.psum_scatter(
        padded_grads.astype(jnp.bfloat16), "expert", scatter_dimension=0, tiled=True
    ).astype(jnp.float32)
    own_grads = pair_grads[PROMPT:] + own_share
    cos_table = kept_state["cos_table"]
    sine_table = kept_state["sine_table"]
    query_pre_grad = turn_heads(query_side, cos_table, sine_table, -1.0).astype(jnp.bfloat16)
    key_pre_grad = turn_heads(own_grads[:, :model_width], cos_table, sine_table, -1.0).astype(
        jnp.bfloat16
    )
    value_pre_grad = own_grads[:, model_width:].astype(jnp.bfloat16)
    normed = kept_state["normed"]
    query_grad = contract_rows(normed, query_pre_grad)
    key_grad = contract_rows(normed, key_pre_grad)
    value_grad = contract_rows(normed, value_pre_grad)
    normed_grad = (
        times_transpose(query_pre_grad, query_weight)
        + times_transpose(key_pre_grad, key_weight)
        + times_transpose(value_pre_grad, value_weight)
    )
    hidden_in = kept_state["hidden_in"]
    inverse_one = kept_state["inverse_one"]
    hat_one = hidden_in * inverse_one
    attn_norm_grad = jnp.sum(normed_grad * hat_one, axis=0)
    scaled_one = normed_grad * attn_norm.astype(jnp.float32)
    input_rows = residual_grad + inverse_one * (
        scaled_one - hat_one * jnp.mean(scaled_one * hat_one, axis=-1, keepdims=True)
    )
    gradients = (
        attn_norm_grad,
        query_grad,
        key_grad,
        value_grad,
        out_grad,
        ffn_norm_grad,
        router_grad,
        shared_gate_grad,
        shared_up_grad,
        shared_down_grad,
        expert_gate_grad,
        expert_up_grad,
        expert_down_grad,
    )
    return (gradients, input_rows.astype(jnp.bfloat16))


def share_each(gradients):
    pieces = (
        lax.psum_scatter(
            gradients[0].astype(jnp.bfloat16), "dp", scatter_dimension=0, tiled=True
        ).astype(jnp.float32),
        lax.psum_scatter(
            gradients[1].astype(jnp.bfloat16), "dp", scatter_dimension=0, tiled=True
        ).astype(jnp.float32),
        lax.psum_scatter(
            gradients[2].astype(jnp.bfloat16), "dp", scatter_dimension=0, tiled=True
        ).astype(jnp.float32),
        lax.psum_scatter(
            gradients[3].astype(jnp.bfloat16), "dp", scatter_dimension=0, tiled=True
        ).astype(jnp.float32),
        lax.psum_scatter(
            gradients[4].astype(jnp.bfloat16), "dp", scatter_dimension=0, tiled=True
        ).astype(jnp.float32),
        lax.psum_scatter(
            gradients[5].astype(jnp.bfloat16), "dp", scatter_dimension=0, tiled=True
        ).astype(jnp.float32),
        lax.psum_scatter(
            gradients[6].astype(jnp.bfloat16), "dp", scatter_dimension=0, tiled=True
        ).astype(jnp.float32),
        lax.psum_scatter(
            gradients[7].astype(jnp.bfloat16), "dp", scatter_dimension=0, tiled=True
        ).astype(jnp.float32),
        lax.psum_scatter(
            gradients[8].astype(jnp.bfloat16), "dp", scatter_dimension=0, tiled=True
        ).astype(jnp.float32),
        lax.psum_scatter(
            gradients[9].astype(jnp.bfloat16), "dp", scatter_dimension=0, tiled=True
        ).astype(jnp.float32),
        lax.psum_scatter(
            gradients[10].astype(jnp.bfloat16), "dp", scatter_dimension=1, tiled=True
        ).astype(jnp.float32),
        lax.psum_scatter(
            gradients[11].astype(jnp.bfloat16), "dp", scatter_dimension=1, tiled=True
        ).astype(jnp.float32),
        lax.psum_scatter(
            gradients[12].astype(jnp.bfloat16), "dp", scatter_dimension=1, tiled=True
        ).astype(jnp.float32),
    )
    dense_sum = (
        lax.psum(pieces[0].astype(jnp.bfloat16), "expert").astype(jnp.float32),
        lax.psum(pieces[1].astype(jnp.bfloat16), "expert").astype(jnp.float32),
        lax.psum(pieces[2].astype(jnp.bfloat16), "expert").astype(jnp.float32),
        lax.psum(pieces[3].astype(jnp.bfloat16), "expert").astype(jnp.float32),
        lax.psum(pieces[4].astype(jnp.bfloat16), "expert").astype(jnp.float32),
        lax.psum(pieces[5].astype(jnp.bfloat16), "expert").astype(jnp.float32),
        lax.psum(pieces[6].astype(jnp.bfloat16), "expert").astype(jnp.float32),
        lax.psum(pieces[7].astype(jnp.bfloat16), "expert").astype(jnp.float32),
        lax.psum(pieces[8].astype(jnp.bfloat16), "expert").astype(jnp.float32),
        lax.psum(pieces[9].astype(jnp.bfloat16), "expert").astype(jnp.float32),
    )
    return (
        dense_sum[0],
        dense_sum[1],
        dense_sum[2],
        dense_sum[3],
        dense_sum[4],
        dense_sum[5],
        dense_sum[6],
        dense_sum[7],
        dense_sum[8],
        dense_sum[9],
        pieces[10],
        pieces[11],
        pieces[12],
    )


def per_device(
    tokens,
    cotangent,
    routes,
    attn_norm,
    query_weight,
    key_weight,
    value_weight,
    out_weight,
    ffn_norm,
    router_weight,
    shared_gate,
    shared_up,
    shared_down,
    expert_gate,
    expert_up,
    expert_down,
):
    gathered = (
        lax.all_gather(attn_norm, "dp", axis=0, tiled=True),
        lax.all_gather(query_weight, "dp", axis=0, tiled=True),
        lax.all_gather(key_weight, "dp", axis=0, tiled=True),
        lax.all_gather(value_weight, "dp", axis=0, tiled=True),
        lax.all_gather(out_weight, "dp", axis=0, tiled=True),
        lax.all_gather(ffn_norm, "dp", axis=0, tiled=True),
        lax.all_gather(router_weight, "dp", axis=0, tiled=True),
        lax.all_gather(shared_gate, "dp", axis=0, tiled=True),
        lax.all_gather(shared_up, "dp", axis=0, tiled=True),
        lax.all_gather(shared_down, "dp", axis=0, tiled=True),
        lax.all_gather(expert_gate, "dp", axis=1, tiled=True),
        lax.all_gather(expert_up, "dp", axis=1, tiled=True),
        lax.all_gather(expert_down, "dp", axis=1, tiled=True),
    )
    outputs_all = []
    inputs_all = []
    summed = None
    for micro_step in range(tokens.shape[0]):
        produced, kept_state = forward_pass(gathered, tokens[micro_step], routes[micro_step])
        gradients, input_rows = backward_pass(gathered, kept_state, cotangent[micro_step])
        outputs_all.append(produced)
        inputs_all.append(input_rows)
        shares = share_each(gradients)
        if summed is None:
            summed = shares
        else:
            summed = tuple((earlier + latest for earlier, latest in zip(summed, shares)))
    return (jnp.stack(outputs_all), jnp.stack(inputs_all)) + tuple(summed)


def solution(mesh):
    return jax.shard_map(
        per_device,
        mesh=mesh,
        in_specs=(
            P(None, ("dp", "expert"), None),
            P(None, ("dp", "expert"), None),
            P(None, ("dp", "expert"), None),
            P("dp"),
            P("dp", None),
            P("dp", None),
            P("dp", None),
            P("dp", None),
            P("dp"),
            P("dp", None),
            P("dp", None),
            P("dp", None),
            P("dp", None),
            P("expert", "dp", None),
            P("expert", "dp", None),
            P("expert", "dp", None),
        ),
        out_specs=(
            P(None, ("dp", "expert"), None),
            P(None, ("dp", "expert"), None),
            P("dp"),
            P("dp", None),
            P("dp", None),
            P("dp", None),
            P("dp", None),
            P("dp"),
            P("dp", None),
            P("dp", None),
            P("dp", None),
            P("dp", None),
            P("expert", "dp", None),
            P("expert", "dp", None),
            P("expert", "dp", None),
        ),
        check_vma=False,
    )
```

profile of v0, /device:TPU:0, one launch (start us, length us, event | category | flops | bytes accessed | tf_op | source)
XLA Modules:
  0.0 2805.4 jit_solution(12393656146510331009)
XLA Ops:
  143.2 161.3 %all-reduce.21.cloned.1.call-done = (bf16[256,1536]{1,0:T(8,128)(2,1)}, bf16[256,1536]{1,0:T(8,128)(2,1)}, bf16[256,1536]{1,0:T(8,128)(2,1)}, bf16[256,1536]{1,0...) async-done(((bf16[256,1536]{1,0:T(8,128)(2,1)}, ...) | async-done | bytes 9437200 | tf_op jit(solution)/shard_map/psum | solution.py:21
  525.9 36.5 %all-gather.30.cloned.1.call-done = bf16[1,2048,768]{2,1,0:T(8,128)(2,1)} async-done(((bf16[1,512,768]{2,1,0:T(8,128)(2,1)}), bf16[1,2048,768]{2,1,0:T(8,128)(2,1)}) %all-gather.30.cloned.1.call-update) | async-done | bytes 3145744 | tf_op jit(solution)/shard_map/all_gather | solution.py:507
  576.1 32.1 %all-gather.26.cloned.1.call-done = bf16[1,768,2048]{2,1,0:T(8,128)(2,1)} async-done(((bf16[1,192,2048]{2,1,0:T(8,128)(2,1)}), bf16[1,768,2048]{2,1,0:T(8,128)(2,1)}) %all-gather.26.cloned.1.call-update) | async-done | bytes 3145744 | tf_op jit(solution)/shard_map/all_gather | solution.py:505
  1341.8 45.3 %reduce-scatter.97.cloned.1.call-done = bf16[1,192,2048]{2,1,0:T(8,128)(2,1)} async-done(((bf16[1,768,2048]{2,1,0:T(8,128)(2,1)}), bf16[1,192,2048]{2,1,0:T(8,128)(2,1)}) %reduce-scatter.97.cloned.1.call-update) | async-done | bytes 786448 | tf_op jit(solution)/shard_map/reduce_scatter | solution.py:440
  1387.1 46.9 %reduce-scatter.99.cloned.1.call-done = bf16[1,192,2048]{2,1,0:T(8,128)(2,1)} async-done(((bf16[1,768,2048]{2,1,0:T(8,128)(2,1)}), bf16[1,192,2048]{2,1,0:T(8,128)(2,1)}) %reduce-scatter.99.cloned.1.call-update) | async-done | bytes 786448 | tf_op jit(solution)/shard_map/reduce_scatter | solution.py:440
  1434.0 46.8 %reduce-scatter.101.cloned.1.call-done = bf16[1,192,2048]{2,1,0:T(8,128)(2,1)} async-done(((bf16[1,768,2048]{2,1,0:T(8,128)(2,1)}), bf16[1,192,2048]{2,1,0:T(8,128)(2,1)}) %reduce-scatter.101.cloned.1.call-update) | async-done | bytes 786448 | tf_op jit(solution)/shard_map/reduce_scatter | solution.py:440
  1483.9 43.8 %reduce-scatter.79.cloned.1.call-done = bf16[192,2048]{1,0:T(8,128)(2,1)} async-done(((bf16[768,2048]{1,0:T(8,128)(2,1)}), bf16[192,2048]{1,0:T(8,128)(2,1)}) %reduce-scatter.79.cloned.1.call-update) | async-done | bytes 786448 | tf_op jit(solution)/shard_map/reduce_scatter | solution.py:431
  1527.7 46.9 %reduce-scatter.73.cloned.1.call-done = bf16[192,2048]{1,0:T(8,128)(2,1)} async-done(((bf16[768,2048]{1,0:T(8,128)(2,1)}), bf16[192,2048]{1,0:T(8,128)(2,1)}) %reduce-scatter.73.cloned.1.call-update) | async-done | bytes 786448 | tf_op jit(solution)/shard_map/reduce_scatter | solution.py:428
  1574.7 46.9 %reduce-scatter.81.cloned.1.call-done = bf16[192,2048]{1,0:T(8,128)(2,1)} async-done(((bf16[768,2048]{1,0:T(8,128)(2,1)}), bf16[192,2048]{1,0:T(8,128)(2,1)}) %reduce-scatter.81.cloned.1.call-update) | async-done | bytes 786448 | tf_op jit(solution)/shard_map/reduce_scatter | solution.py:431
  1621.6 46.8 %reduce-scatter.75.cloned.1.call-done = bf16[192,2048]{1,0:T(8,128)(2,1)} async-done(((bf16[768,2048]{1,0:T(8,128)(2,1)}), bf16[192,2048]{1,0:T(8,128)(2,1)}) %reduce-scatter.75.cloned.1.call-update) | async-done | bytes 786448 | tf_op jit(solution)/shard_map/reduce_scatter | solution.py:428
  1668.4 46.9 %reduce-scatter.87.cloned.1.call-done = bf16[512,768]{1,0:T(8,128)(2,1)} async-done(((bf16[2048,768]{1,0:T(8,128)(2,1)}), bf16[512,768]{1,0:T(8,128)(2,1)}) %reduce-scatter.87.cloned.1.call-update) | async-done | bytes 786448 | tf_op jit(solution)/shard_map/reduce_scatter | solution.py:434
  1715.3 46.8 %reduce-scatter.85.cloned.1.call-done = bf16[512,768]{1,0:T(8,128)(2,1)} async-done(((bf16[2048,768]{1,0:T(8,128)(2,1)}), bf16[512,768]{1,0:T(8,128)(2,1)}) %reduce-scatter.85.cloned.1.call-update) | async-done | bytes 786448 | tf_op jit(solution)/shard_map/reduce_scatter | solution.py:434
  1762.1 46.8 %reduce-scatter.83.cloned.1.call-done = bf16[192,2048]{1,0:T(8,128)(2,1)} async-done(((bf16[768,2048]{1,0:T(8,128)(2,1)}), bf16[192,2048]{1,0:T(8,128)(2,1)}) %reduce-scatter.83.cloned.1.call-update) | async-done | bytes 786448 | tf_op jit(solution)/shard_map/reduce_scatter | solution.py:431
  1808.9 46.9 %reduce-scatter.77.cloned.1.call-done = bf16[192,2048]{1,0:T(8,128)(2,1)} async-done(((bf16[768,2048]{1,0:T(8,128)(2,1)}), bf16[192,2048]{1,0:T(8,128)(2,1)}) %reduce-scatter.77.cloned.1.call-update) | async-done | bytes 786448 | tf_op jit(solution)/shard_map/reduce_scatter | solution.py:428
  1855.8 46.9 %reduce-scatter.89.cloned.1.call-done = bf16[512,768]{1,0:T(8,128)(2,1)} async-done(((bf16[2048,768]{1,0:T(8,128)(2,1)}), bf16[512,768]{1,0:T(8,128)(2,1)}) %reduce-scatter.89.cloned.1.call-update) | async-done | bytes 786448 | tf_op jit(solution)/shard_map/reduce_scatter | solution.py:434
  2060.7 32.2 %reduce-scatter.53.cloned.1.call-done = bf16[192,768]{1,0:T(8,128)(2,1)} async-done(((bf16[768,768]{1,0:T(8,128)(2,1)}), bf16[192,768]{1,0:T(8,128)(2,1)}) %reduce-scatter.53.cloned.1.call-update) | async-done | bytes 294928 | tf_op jit(solution)/shard_map/reduce_scatter | solution.py:410
  2124.4 32.1 %reduce-scatter.51.cloned.1.call-done = bf16[192,768]{1,0:T(8,128)(2,1)} async-done(((bf16[768,768]{1,0:T(8,128)(2,1)}), bf16[192,768]{1,0:T(8,128)(2,1)}) %reduce-scatter.51.cloned.1.call-update) | async-done | bytes 294928 | tf_op jit(solution)/shard_map/reduce_scatter | solution.py:410
  2283.0 46.9 %reduce-scatter.103.cloned.1.call-done = bf16[1,512,768]{2,1,0:T(8,128)(2,1)} async-done(((bf16[1,2048,768]{2,1,0:T(8,128)(2,1)}), bf16[1,512,768]{2,1,0:T(8,128)(2,1)}) %reduce-scatter.103.cloned.1.call-update) | async-done | bytes 786448 | tf_op jit(solution)/shard_map/reduce_scatter | solution.py:443
  2330.0 46.8 %reduce-scatter.105.cloned.1.call-done = bf16[1,512,768]{2,1,0:T(8,128)(2,1)} async-done(((bf16[1,2048,768]{2,1,0:T(8,128)(2,1)}), bf16[1,512,768]{2,1,0:T(8,128)(2,1)}) %reduce-scatter.105.cloned.1.call-update) | async-done | bytes 786448 | tf_op jit(solution)/shard_map/reduce_scatter | solution.py:443
  2376.7 46.9 %reduce-scatter.107.cloned.1.call-done = bf16[1,512,768]{2,1,0:T(8,128)(2,1)} async-done(((bf16[1,2048,768]{2,1,0:T(8,128)(2,1)}), bf16[1,512,768]{2,1,0:T(8,128)(2,1)}) %reduce-scatter.107.cloned.1.call-update) | async-done | bytes 786448 | tf_op jit(solution)/shard_map/reduce_scatter | solution.py:443
  2426.7 43.8 %reduce-scatter.91.cloned.1.call-done = bf16[1,192,2048]{2,1,0:T(8,128)(2,1)} async-done(((bf16[1,768,2048]{2,1,0:T(8,128)(2,1)}), bf16[1,192,2048]{2,1,0:T(8,128)(2,1)}) %reduce-scatter.91.cloned.1.call-update) | async-done | bytes 786448 | tf_op jit(solution)/shard_map/reduce_scatter | solution.py:437
  2470.4 46.8 %reduce-scatter.93.cloned.1.call-done = bf16[1,192,2048]{2,1,0:T(8,128)(2,1)} async-done(((bf16[1,768,2048]{2,1,0:T(8,128)(2,1)}), bf16[1,192,2048]{2,1,0:T(8,128)(2,1)}) %reduce-scatter.93.cloned.1.call-update) | async-done | bytes 786448 | tf_op jit(solution)/shard_map/reduce_scatter | solution.py:437
  2517.2 46.8 %reduce-scatter.95.cloned.1.call-done = bf16[1,192,2048]{2,1,0:T(8,128)(2,1)} async-done(((bf16[1,768,2048]{2,1,0:T(8,128)(2,1)}), bf16[1,192,2048]{2,1,0:T(8,128)(2,1)}) %reduce-scatter.95.cloned.1.call-update) | async-done | bytes 786448 | tf_op jit(solution)/shard_map/reduce_scatter | solution.py:437
  2635.2 151.5 %all-reduce.19.cloned.1.call-done = (bf16[192,768]{1,0:T(8,128)(2,1)}, bf16[192,768]{1,0:T(8,128)(2,1)}, bf16[192,768]{1,0:T(8,128)(2,1)}, bf16[192,768]{1,0:T(8...) async-done(((bf16[192,768]{1,0:T(8,128)(2,1)}, ...) | async-done | bytes 10616848 | tf_op jit(solution)/shard_map/psum | solution.py:449
  (1036 shorter events, 1504.4 us)
Async XLA Ops:
  1177.1 538.2 %reduce-scatter.87.cloned.1.call-start = ((), (), s32[]{:S(2)}) async-start(), calls=%async_computation.80 | async-start | bytes 3932160 | tf_op jit(solution)/shard_map/reduce_scatter | solution.py:434
  1182.3 579.8 %reduce-scatter.85.cloned.1.call-start = ((), (), s32[]{:S(2)}) async-start(), calls=%async_computation.79 | async-start | bytes 3932160 | tf_op jit(solution)/shard_map/reduce_scatter | solution.py:434
  1186.7 622.2 %reduce-scatter.83.cloned.1.call-start = ((), (), s32[]{:S(2)}) async-start(), calls=%async_computation.78 | async-start | bytes 3932160 | tf_op jit(solution)/shard_map/reduce_scatter | solution.py:431
  1190.7 665.1 %reduce-scatter.77.cloned.1.call-start = ((), (), s32[]{:S(2)}) async-start(), calls=%async_computation.75 | async-start | bytes 3932160 | tf_op jit(solution)/shard_map/reduce_scatter | solution.py:428
  1194.6 708.1 %reduce-scatter.89.cloned.1.call-start = ((), (), s32[]{:S(2)}) async-start(), calls=%async_computation.81 | async-start | bytes 3932160 | tf_op jit(solution)/shard_map/reduce_scatter | solution.py:434
  1198.5 735.7 %reduce-scatter.69.cloned.1.call-start = ((), (), s32[]{:S(2)}) async-start(), calls=%async_computation.71 | async-start | bytes 1474560 | tf_op jit(solution)/shard_map/reduce_scatter | solution.py:419
  1201.3 764.6 %reduce-scatter.71.cloned.1.call-start = ((), (), s32[]{:S(2)}) async-start(), calls=%async_computation.72 | async-start | bytes 1474560 | tf_op jit(solution)/shard_map/reduce_scatter | solution.py:419
  1203.9 793.6 %reduce-scatter.67.cloned.1.call-start = ((), (), s32[]{:S(2)}) async-start(), calls=%async_computation.70 | async-start | bytes 1474560 | tf_op jit(solution)/shard_map/reduce_scatter | solution.py:419
  1205.5 823.5 %reduce-scatter.63.cloned.1.call-start = ((), (), s32[]{:S(2)}) async-start(), calls=%async_computation.68 | async-start | bytes 1474560 | tf_op jit(solution)/shard_map/reduce_scatter | solution.py:416
  1210.4 850.3 %reduce-scatter.61.cloned.1.call-start = ((), (), s32[]{:S(2)}) async-start(), calls=%async_computation.67 | async-start | bytes 1474560 | tf_op jit(solution)/shard_map/reduce_scatter | solution.py:416
  1215.1 877.8 %reduce-scatter.53.cloned.1.call-start = ((), (), s32[]{:S(2)}) async-start(), calls=%async_computation.63 | async-start | bytes 1474560 | tf_op jit(solution)/shard_map/reduce_scatter | solution.py:410
  1231.1 893.4 %reduce-scatter.57.cloned.1.call-start = ((), (), s32[]{:S(2)}) async-start(), calls=%async_computation.65 | async-start | bytes 1474560 | tf_op jit(solution)/shard_map/reduce_scatter | solution.py:413
  1232.8 923.7 %reduce-scatter.51.cloned.1.call-start = ((), (), s32[]{:S(2)}) async-start(), calls=%async_computation.62 | async-start | bytes 1474560 | tf_op jit(solution)/shard_map/reduce_scatter | solution.py:410
  1234.6 953.6 %reduce-scatter.55.cloned.1.call-start = ((), (), s32[]{:S(2)}) async-start(), calls=%async_computation.64 | async-start | bytes 1474560 | tf_op jit(solution)/shard_map/reduce_scatter | solution.py:413
  1236.5 983.2 %reduce-scatter.65.cloned.1.call-start = ((), (), s32[]{:S(2)}) async-start(), calls=%async_computation.69 | async-start | bytes 1474560 | tf_op jit(solution)/shard_map/reduce_scatter | solution.py:416
  1265.9 985.5 %reduce-scatter.59.cloned.1.call-start = ((), (), s32[]{:S(2)}) async-start(), calls=%async_computation.66 | async-start | bytes 1474560 | tf_op jit(solution)/shard_map/reduce_scatter | solution.py:413
  1273.8 1009.2 %reduce-scatter.49.cloned.1.call-start = ((), (), s32[]{:S(2)}) async-start(), calls=%async_computation.61 | async-start | bytes 1474560 | tf_op jit(solution)/shard_map/reduce_scatter | solution.py:410
  1275.5 1054.4 %reduce-scatter.103.cloned.1.call-start = ((), (), s32[]{:S(2)}) async-start(), calls=%async_computation.88 | async-start | bytes 3932160 | tf_op jit(solution)/shard_map/reduce_scatter | solution.py:443
  1283.5 1093.2 %reduce-scatter.105.cloned.1.call-start = ((), (), s32[]{:S(2)}) async-start(), calls=%async_computation.89 | async-start | bytes 3932160 | tf_op jit(solution)/shard_map/reduce_scatter | solution.py:443
  1291.6 1132.1 %reduce-scatter.107.cloned.1.call-start = ((), (), s32[]{:S(2)}) async-start(), calls=%async_computation.90 | async-start | bytes 3932160 | tf_op jit(solution)/shard_map/reduce_scatter | solution.py:443
  1299.8 1170.7 %reduce-scatter.91.cloned.1.call-start = ((), (), s32[]{:S(2)}) async-start(), calls=%async_computation.82 | async-start | bytes 3932160 | tf_op jit(solution)/shard_map/reduce_scatter | solution.py:437
  1307.7 1209.6 %reduce-scatter.93.cloned.1.call-start = ((), (), s32[]{:S(2)}) async-start(), calls=%async_computation.83 | async-start | bytes 3932160 | tf_op jit(solution)/shard_map/reduce_scatter | solution.py:437
  1315.6 1248.4 %reduce-scatter.95.cloned.1.call-start = ((), (), s32[]{:S(2)}) async-start(), calls=%async_computation.84 | async-start | bytes 3932160 | tf_op jit(solution)/shard_map/reduce_scatter | solution.py:437
  1323.9 1462.9 %all-reduce.19.cloned.1.call-start = ((), (), s32[]{:S(2)}) async-start(), calls=%async_computation.94 | async-start | bytes 21233664 | tf_op jit(solution)/shard_map/psum | solution.py:449
  (314 other events, 11501.5 us)
Sparse Core Ops, SparseCore 0:
  108.9 195.5 all-reduce.20
  335.9 43.8 all-gather.21
  1052.6 67.6 reduce-scatter.44
  1122.6 68.1 reduce-scatter.42
  1193.0 68.1 reduce-scatter.46
  1343.2 43.8 reduce-scatter.96
  1390.1 43.8 reduce-scatter.98
  1436.9 43.8 reduce-scatter.100
  1483.8 43.8 reduce-scatter.78
  1530.7 43.8 reduce-scatter.72
  1577.7 43.8 reduce-scatter.80
  1624.4 43.8 reduce-scatter.74
  1671.4 43.8 reduce-scatter.86
  1718.1 43.9 reduce-scatter.84
  1764.9 43.8 reduce-scatter.82
  1811.9 43.8 reduce-scatter.76
  1858.8 43.8 reduce-scatter.88
  2286.0 43.9 reduce-scatter.102
  2332.8 43.8 reduce-scatter.104
  2379.7 43.8 reduce-scatter.106
  2426.5 43.8 reduce-scatter.90
  2473.3 43.8 reduce-scatter.92
  2520.1 43.8 reduce-scatter.94
  2568.0 218.6 all-reduce.18
  (24 shorter events, 746.9 us)
where the time goes:
time: 2820 us; the launch traced here: 2810 us
  waiting for transfers between devices  1920 us (68%)
  matrix products  505 us (18%)
  local copies, waits for them, and re-layouts  131 us (5%)
  other arithmetic  108 us (4%)
  blocking collectives  65.5 us (2%)
  starting transfers between devices  57 us (2%)
    psum x1, waiting for transfers between devices, from_root(): return lax.psum(kept, axis)  161 us
    psum x1, waiting for transfers between devices, share_each(): lax.psum(pieces[1].astype(jnp.bfloat16), 'expert').astype(jnp.float32)  152 us
    dot_general x39, matrix products, matmul(): return jnp.dot(left_side, right_side, preferred_element_type=jnp.float32)  142 us
    reduce_scatter x3, waiting for transfers between devices, share_each(): lax.psum_scatter(gradients[9].astype(jnp.bfloat16), 'dp', scatter_dimensi...  141 us
    reduce_scatter x3, waiting for transfers between devices, share_each(): lax.psum_scatter(gradients[12].astype(jnp.bfloat16), 'dp', scatter_dimens...  141 us
    reduce_scatter x3, waiting for transfers between devices, share_each(): lax.psum_scatter(gradients[7].astype(jnp.bfloat16), 'dp', scatter_dimensi...  141 us
    reduce_scatter x3, waiting for transfers between devices, share_each(): lax.psum_scatter(gradients[11].astype(jnp.bfloat16), 'dp', scatter_dimens...  139 us
    reduce_scatter x3, waiting for transfers between devices, share_each(): lax.psum_scatter(gradients[8].astype(jnp.bfloat16), 'dp', scatter_dimensi...  137 us
  transfers between devices with their start and end apart: 60, of which 50 were waited for; matrix products, arithmetic and copies ran while one was open for 21% of the time, Pallas kernels for 0%

commit v1 on v0

--- a/solution.py
+++ b/solution.py
@@ -403,73 +403,57 @@
 
 
 def share_each(gradients):
-    pieces = (
-        lax.psum_scatter(
-            gradients[0].astype(jnp.bfloat16), "dp", scatter_dimension=0, tiled=True
-        ).astype(jnp.float32),
-        lax.psum_scatter(
-            gradients[1].astype(jnp.bfloat16), "dp", scatter_dimension=0, tiled=True
-        ).astype(jnp.float32),
-        lax.psum_scatter(
-            gradients[2].astype(jnp.bfloat16), "dp", scatter_dimension=0, tiled=True
-        ).astype(jnp.float32),
-        lax.psum_scatter(
-            gradients[3].astype(jnp.bfloat16), "dp", scatter_dimension=0, tiled=True
-        ).astype(jnp.float32),
-        lax.psum_scatter(
-            gradients[4].astype(jnp.bfloat16), "dp", scatter_dimension=0, tiled=True
-        ).astype(jnp.float32),
-        lax.psum_scatter(
-            gradients[5].astype(jnp.bfloat16), "dp", scatter_dimension=0, tiled=True
-        ).astype(jnp.float32),
-        lax.psum_scatter(
-            gradients[6].astype(jnp.bfloat16), "dp", scatter_dimension=0, tiled=True
-        ).astype(jnp.float32),
-        lax.psum_scatter(
-            gradients[7].astype(jnp.bfloat16), "dp", scatter_dimension=0, tiled=True
-        ).astype(jnp.float32),
-        lax.psum_scatter(
-            gradients[8].astype(jnp.bfloat16), "dp", scatter_dimension=0, tiled=True
-        ).astype(jnp.float32),
-        lax.psum_scatter(
-            gradients[9].astype(jnp.bfloat16), "dp", scatter_dimension=0, tiled=True
-        ).astype(jnp.float32),
-        lax.psum_scatter(
-            gradients[10].astype(jnp.bfloat16), "dp", scatter_dimension=1, tiled=True
-        ).astype(jnp.float32),
-        lax.psum_scatter(
-            gradients[11].astype(jnp.bfloat16), "dp", scatter_dimension=1, tiled=True
-        ).astype(jnp.float32),
-        lax.psum_scatter(
-            gradients[12].astype(jnp.bfloat16), "dp", scatter_dimension=1, tiled=True
-        ).astype(jnp.float32),
-    )
-    dense_sum = (
-        lax.psum(pieces[0].astype(jnp.bfloat16), "expert").astype(jnp.float32),
-        lax.psum(pieces[1].astype(jnp.bfloat16), "expert").astype(jnp.float32),
-        lax.psum(pieces[2].astype(jnp.bfloat16), "expert").astype(jnp.float32),
-        lax.psum(pieces[3].astype(jnp.bfloat16), "expert").astype(jnp.float32),
-        lax.psum(pieces[4].astype(jnp.bfloat16), "expert").astype(jnp.float32),
-        lax.psum(pieces[5].astype(jnp.bfloat16), "expert").astype(jnp.float32),
-        lax.psum(pieces[6].astype(jnp.bfloat16), "expert").astype(jnp.float32),
-        lax.psum(pieces[7].astype(jnp.bfloat16), "expert").astype(jnp.float32),
-        lax.psum(pieces[8].astype(jnp.bfloat16), "expert").astype(jnp.float32),
-        lax.psum(pieces[9].astype(jnp.bfloat16), "expert").astype(jnp.float32),
-    )
+    (
+        attn_norm_grad,
+        query_grad,
+        key_grad,
+        value_grad,
+        out_grad,
+        ffn_norm_grad,
+        router_grad,
+        shared_gate_grad,
+        shared_up_grad,
+        shared_down_grad,
+        expert_gate_grad,
+        expert_up_grad,
+        expert_down_grad,
+    ) = gradients
+    low = jnp.bfloat16
+
+    def scatter(value, dimension):
+        return lax.psum_scatter(value.astype(low), "dp", scatter_dimension=dimension, tiled=True)
+
+    expert_wide = scatter(
+        jnp.concatenate([expert_gate_grad[0], expert_up_grad[0]], axis=1), 0
+    ).astype(jnp.float32)
+    expert_deep = scatter(expert_down_grad[0], 0).astype(jnp.float32)
+    ff = expert_gate_grad.shape[2]
+    width = query_grad.shape[1]
+    experts = router_grad.shape[1]
+    dense_wide = jnp.concatenate(
+        [query_grad, key_grad, value_grad, out_grad, shared_gate_grad, shared_up_grad], axis=1
+    )
+    lanes = 128
+    small = jnp.concatenate([attn_norm_grad[:, None], ffn_norm_grad[:, None], router_grad], axis=1)
+    small = jnp.pad(small, ((0, 0), (0, lanes - small.shape[1])))
+    dense_wide = lax.psum(scatter(jnp.concatenate([dense_wide, small], axis=1), 0), "expert")
+    dense_wide = dense_wide.astype(jnp.float32)
+    dense_deep = lax.psum(scatter(shared_down_grad, 0), "expert").astype(jnp.float32)
+    tail = 4 * width + 2 * ff
     return (
-        dense_sum[0],
-        dense_sum[1],
-        dense_sum[2],
-        dense_sum[3],
-        dense_sum[4],
-        dense_sum[5],
-        dense_sum[6],
-        dense_sum[7],
-        dense_sum[8],
-        dense_sum[9],
-        pieces[10],
-        pieces[11],
-        pieces[12],
+        dense_wide[:, tail],
+        dense_wide[:, :width],
+        dense_wide[:, width : 2 * width],
+        dense_wide[:, 2 * width : 3 * width],
+        dense_wide[:, 3 * width : 4 * width],
+        dense_wide[:, tail + 1],
+        dense_wide[:, tail + 2 : tail + 2 + experts],
+        dense_wide[:, 4 * width : 4 * width + ff],
+        dense_wide[:, 4 * width + ff : tail],
+        dense_deep,
+        expert_wide[None, :, :ff],
+        expert_wide[None, :, ff:],
+        expert_deep[None],
     )
 
 
@@ -491,20 +475,52 @@
     expert_up,
     expert_down,
 ):
+    width = query_weight.shape[1]
+    experts = router_weight.shape[1]
+    ff = shared_gate.shape[1]
+    attn_all = lax.all_gather(
+        jnp.concatenate(
+            [
+                query_weight,
+                key_weight,
+                value_weight,
+                out_weight,
+                jnp.pad(
+                    jnp.concatenate(
+                        [attn_norm[:, None], ffn_norm[:, None], router_weight], axis=1
+                    ),
+                    ((0, 0), (0, 126 - experts)),
+                ),
+            ],
+            axis=1,
+        ),
+        "dp",
+        axis=0,
+        tiled=True,
+    )
+    wide_all = lax.all_gather(
+        jnp.concatenate([shared_gate, shared_up, expert_gate[0], expert_up[0]], axis=1),
+        "dp",
+        axis=0,
+        tiled=True,
+    )
+    deep_all = lax.all_gather(
+        jnp.concatenate([shared_down, expert_down[0]], axis=1), "dp", axis=0, tiled=True
+    )
     gathered = (
-        lax.all_gather(attn_norm, "dp", axis=0, tiled=True),
-        lax.all_gather(query_weight, "dp", axis=0, tiled=True),
-        lax.all_gather(key_weight, "dp", axis=0, tiled=True),
-        lax.all_gather(value_weight, "dp", axis=0, tiled=True),
-        lax.all_gather(out_weight, "dp", axis=0, tiled=True),
-        lax.all_gather(ffn_norm, "dp", axis=0, tiled=True),
-        lax.all_gather(router_weight, "dp", axis=0, tiled=True),
-        lax.all_gather(shared_gate, "dp", axis=0, tiled=True),
-        lax.all_gather(shared_up, "dp", axis=0, tiled=True),
-        lax.all_gather(shared_down, "dp", axis=0, tiled=True),
-        lax.all_gather(expert_gate, "dp", axis=1, tiled=True),
-        lax.all_gather(expert_up, "dp", axis=1, tiled=True),
-        lax.all_gather(expert_down, "dp", axis=1, tiled=True),
+        attn_all[:, 4 * width],
+        attn_all[:, :width],
+        attn_all[:, width : 2 * width],
+        attn_all[:, 2 * width : 3 * width],
+        attn_all[:, 3 * width : 4 * width],
+        attn_all[:, 4 * width + 1],
+        attn_all[:, 4 * width + 2 : 4 * width + 2 + experts],
+        wide_all[:, :ff],
+        wide_all[:, ff : 2 * ff],
+        deep_all[:, :width],
+        wide_all[None, :, 2 * ff : 3 * ff],
+        wide_all[None, :, 3 * ff :],
+        deep_all[None, :, width:],
     )
     outputs_all = []
     inputs_all = []
@@ -514,12 +530,11 @@
         gradients, input_rows = backward_pass(gathered, kept_state, cotangent[micro_step])
         outputs_all.append(produced)
         inputs_all.append(input_rows)
-        shares = share_each(gradients)
         if summed is None:
-            summed = shares
+            summed = gradients
         else:
-            summed = tuple((earlier + latest for earlier, latest in zip(summed, shares)))
-    return (jnp.stack(outputs_all), jnp.stack(inputs_all)) + tuple(summed)
+            summed = tuple((earlier + latest for earlier, latest in zip(summed, gradients)))
+    return (jnp.stack(outputs_all), jnp.stack(inputs_all)) + share_each(summed)
 
 
 def solution(mesh):

time: 2820 us -> 1610 us (0.57)
  waiting for transfers between devices: 1920 us -> 763 us
  blocking collectives: 65.5 us -> 0 us
    reduce_scatter x30 -> x4, waiting for transfers between devices: 1220 us -> 154 us  [scatter(): lax.psum_scatter(value.astype(low), 'dp', scatter_dimension=dimension, ti...]
    psum x1, waiting for transfers between devices: 152 us -> 80.8 us  [share_each(): lax.psum(scatter(jnp.concatenate([dense_wide, small], axis=1), 0), 'expert')]
    all_gather x10 -> x3, waiting for transfers between devices: 147 us -> 78.1 us  [the longest x1 57.1 us: per_device(): lax.all_gather(jnp.concatenate([query_weight, key_weight, value_weight, o...]
    reduce_scatter x3, waiting for transfers between devices: 24.7 us -> 74 us  [backward_pass(): lax.psum_scatter(padded_grads.astype(jnp.bfloat16), 'expert', scatter_dim...]
    psum x1, waiting for transfers between devices: 161 us -> 196 us  [from_root(): return lax.psum(kept, axis)]
    dot_general x30, matrix products: 88.6 us -> 117 us  [times_transpose(): lax.dot_general(left_side, right_side, (((1,), (1,)), ((), ())), preferre...]
    psum x1 -> x0, blocking collectives: 28.8 us -> none  [share_each(): lax.psum(pieces[0].astype(jnp.bfloat16), 'expert').astype(jnp.float32)]
    unnamed x2 -> x0, blocking collectives: 28.3 us -> none
  transfers between devices with their start and end apart: 60 -> 24, of which waited for: 50 -> 20; matrix products, arithmetic and copies ran while one was open for 21% -> 40% of each run, Pallas kernels for 0% -> 0%
where the time goes in v1:
time: 1610 us; the launch traced here: 1600 us
  waiting for transfers between devices  763 us (47%)
  matrix products  510 us (32%)
  local copies, waits for them, and re-layouts  153 us (10%)
  other arithmetic  106 us (7%)
  starting transfers between devices  53.1 us (3%)
  between operations  18.6 us (1%)
    psum x1, waiting for transfers between devices, from_root(): return lax.psum(kept, axis)  196 us
    reduce_scatter x4, waiting for transfers between devices, scatter(): lax.psum_scatter(value.astype(low), 'dp', scatter_dimension=dimension, ti...  154 us
    dot_general x39, matrix products, matmul(): return jnp.dot(left_side, right_side, preferred_element_type=jnp.float32)  145 us
    dot_general x30, matrix products, times_transpose(): lax.dot_general(left_side, right_side, (((1,), (1,)), ((), ())), preferre...  117 us
    dot_general x36, matrix products, contract_rows(): lax.dot_general(left_side, right_side, (((0,), (0,)), ((), ())), preferre...  110 us
    psum x1, waiting for transfers between devices, share_each(): lax.psum(scatter(jnp.concatenate([dense_wide, small], axis=1), 0), 'expert')  80.8 us
    reduce_scatter x3, waiting for transfers between devices, backward_pass(): lax.psum_scatter(padded_grads.astype(jnp.bfloat16), 'expert', scatter_dim...  74 us
    unnamed x643, local copies, waits for them, and re-layouts  64.1 us
  transfers between devices with their start and end apart: 24, of which 20 were waited for; matrix products, arithmetic and copies ran while one was open for 40% of the time, Pallas kernels for 0%

profile of v1, /device:TPU:0, one launch (start us, length us, event | category | flops | bytes accessed | tf_op | source)
XLA Modules:
  0.0 1603.5 jit_solution(17689576251780737663)
XLA Ops:
  18.8 57.1 %all-gather.4.cloned.1.call-done = bf16[768,3200]{1,0:T(8,128)(2,1)} async-done(((bf16[192,3200]{1,0:T(8,128)(2,1)}), bf16[768,3200]{1,0:T(8,128)(2,1)}) %all-gather.4.cloned.1.call-update) | async-done | bytes 4915216 | tf_op jit(solution)/shard_map/all_gather | solution.py:481
  127.5 20.9 %all-gather.8.cloned.1.call-done = bf16[2048,1536]{1,0:T(8,128)(2,1)} async-done(((bf16[512,1536]{1,0:T(8,128)(2,1)}), bf16[2048,1536]{1,0:T(8,128)(2,1)}) %all-gather.8.cloned.1.call-update) | async-done | bytes 6291472 | tf_op jit(solution)/shard_map/all_gather | solution.py:507
  152.7 195.9 %all-reduce.12.cloned.1.call-done = (bf16[256,1536]{1,0:T(8,128)(2,1)}, bf16[256,1536]{1,0:T(8,128)(2,1)}, bf16[256,1536]{1,0:T(8,128)(2,1)}, bf16[256,1536]{1,0...) async-done(((bf16[256,1536]{1,0:T(8,128)(2,1)}, ...) | async-done | bytes 9437200 | tf_op jit(solution)/shard_map/psum | solution.py:21
  498.8 12.0 all-to-all-done.6
  510.8 14.1 multiply_convert_fusion.7
  553.8 21.4 %all-to-all-done.1 = bf16[8,128,768]{2,1,0:T(8,128)(2,1)} async-done(((bf16[8,128,768]{2,1,0:T(8,128)(2,1)}), bf16[8,128,768]{2,1,0:T(8,128)(2,1)}, u32[]{:S(2)}, u32[]{:S(2)}) %all-to-all-start.1) | async-done | bytes 1572896 | tf_op jit(solution)/shard_map/all_to_all | solution.py:177
  597.9 19.5 %all-to-all-done.7 = bf16[8,128,768]{2,1,0:T(8,128)(2,1)} async-done(((bf16[8,128,768]{2,1,0:T(8,128)(2,1)}), bf16[8,128,768]{2,1,0:T(8,128)(2,1)}, u32[]{:S(2)}, u32[]{:S(2)}) %all-to-all-start.7) | async-done | bytes 1572896 | tf_op jit(solution)/shard_map/all_to_all | solution.py:299
  646.9 18.8 %all-to-all-done.4 = bf16[8,128,768]{2,1,0:T(8,128)(2,1)} async-done(((bf16[8,128,768]{2,1,0:T(8,128)(2,1)}), bf16[8,128,768]{2,1,0:T(8,128)(2,1)}, u32[]{:S(2)}, u32[]{:S(2)}) %all-to-all-start.4) | async-done | bytes 1572896 | tf_op jit(solution)/shard_map/all_to_all | solution.py:165
  690.4 16.6 %all-to-all-done.2 = bf16[8,128,768]{2,1,0:T(8,128)(2,1)S(1)} async-done(((bf16[8,128,768]{2,1,0:T(8,128)(2,1)}), bf16[8,128,768]{2,1,0:T(8,128)(2,1)S(1)}, u32[]{:S(2)}, u32[]{:S(2)}) %all-to-all-start.2) | async-done | bytes 1572896 | tf_op jit(solution)/shard_map/all_to_all | solution.py:165
  752.9 14.1 multiply_convert_fusion.3
  775.3 15.3 all-to-all-done.8
  795.1 12.6 multiply_convert_fusion.5
  816.1 16.8 %all-to-all-done.5 = bf16[8,128,768]{2,1,0:T(8,128)(2,1)} async-done(((bf16[8,128,768]{2,1,0:T(8,128)(2,1)}), bf16[8,128,768]{2,1,0:T(8,128)(2,1)}, u32[]{:S(2)}, u32[]{:S(2)}) %all-to-all-start.5) | async-done | bytes 1572896 | tf_op jit(solution)/shard_map/all_to_all | solution.py:177
  856.9 17.3 %all-to-all-done.3 = bf16[8,128,768]{2,1,0:T(8,128)(2,1)S(1)} async-done(((bf16[8,128,768]{2,1,0:T(8,128)(2,1)}), bf16[8,128,768]{2,1,0:T(8,128)(2,1)S(1)}, u32[]{:S(2)}, u32[]{:S(2)}) %all-to-all-start.3) | async-done | bytes 1572896 | tf_op jit(solution)/shard_map/all_to_all | solution.py:177
  901.0 14.9 all-to-all-done.11
  938.7 19.4 %all-to-all-done.9 = bf16[8,128,768]{2,1,0:T(8,128)(2,1)} async-done(((bf16[8,128,768]{2,1,0:T(8,128)(2,1)}), bf16[8,128,768]{2,1,0:T(8,128)(2,1)}, u32[]{:S(2)}, u32[]{:S(2)}) %all-to-all-start.9) | async-done | bytes 1572896 | tf_op jit(solution)/shard_map/all_to_all | solution.py:299
  966.1 13.1 multiply_reduce_fusion
  1010.9 14.8 multiply_reduce_fusion.2
  1051.4 14.8 multiply_reduce_fusion.1
  1149.5 66.7 %reduce-scatter.10.cloned.1.call-done = bf16[256,1536]{0,1:T(8,128)(2,1)} async-done(((bf16[2048,1536]{0,1:T(8,128)(2,1)}), bf16[256,1536]{0,1:T(8,128)(2,1)}) %reduce-scatter.10.cloned.1.call-update) | async-done | bytes 786448 | tf_op jit(solution)/shard_map/reduce_scatter | solution.py:359
  1343.2 36.8 %reduce-scatter.14.cloned.1.call-done = bf16[192,7296]{1,0:T(8,128)(2,1)} async-done(((bf16[768,7296]{1,0:T(8,128)(2,1)}), bf16[192,7296]{1,0:T(8,128)(2,1)}) %reduce-scatter.14.cloned.1.call-update) | async-done | bytes 2801680 | tf_op jit(solution)/shard_map/reduce_scatter | solution.py:424
  1380.0 46.7 %reduce-scatter.20.cloned.1.call-done = bf16[512,768]{1,0:T(8,128)(2,1)} async-done(((bf16[2048,768]{1,0:T(8,128)(2,1)}), bf16[512,768]{1,0:T(8,128)(2,1)}) %reduce-scatter.20.cloned.1.call-update) | async-done | bytes 786448 | tf_op jit(solution)/shard_map/reduce_scatter | solution.py:424
  1429.1 70.7 %reduce-scatter.18.cloned.1.call-done = bf16[192,4096]{1,0:T(8,128)(2,1)} async-done(((bf16[768,4096]{1,0:T(8,128)(2,1)}), bf16[192,4096]{1,0:T(8,128)(2,1)}) %reduce-scatter.18.cloned.1.call-update) | async-done | bytes 1572880 | tf_op jit(solution)/shard_map/reduce_scatter | solution.py:424
  1506.6 80.8 %all-reduce.10.cloned.1.call-done = (bf16[192,7296]{1,0:T(8,128)(2,1)}, bf16[512,768]{1,0:T(8,128)(2,1)}) async-done(((bf16[192,7296]{1,0:T(8,128)(2,1)}, bf16[512,768]{1,0:T(8,128)(2,1)}), (bf16[192,7296]{1,0:T(8,128)(2,1)}, bf16[512,768]{1,0:T(8,128)(2,1)})) %all-reduce.10.cloned.1.call-update) | async-done | bytes 3588112 | tf_op jit(solution)/shard_map/psum | solution.py:439
  (1002 shorter events, 753.8 us)
Async XLA Ops:
  7.2 68.8 %all-gather.4.cloned.1.call-start = ((), (), s32[]{:S(2)}) async-start(), calls=%async_computation.19 | async-start | bytes 6144000 | tf_op jit(solution)/shard_map/all_gather | solution.py:481
  14.5 133.9 %all-gather.8.cloned.1.call-start = ((), (), s32[]{:S(2)}) async-start(), calls=%async_computation.21 | async-start | bytes 7864320 | tf_op jit(solution)/shard_map/all_gather | solution.py:507
  17.0 331.6 %all-reduce.12.cloned.1.call-start = ((), (), s32[]{:S(2)}) async-start(), calls=%async_computation.30 | async-start | bytes 18874368 | tf_op jit(solution)/shard_map/psum | solution.py:21
  106.8 374.0 %all-gather.6.cloned.1.call-start = ((), (), s32[]{:S(2)}) async-start(), calls=%async_computation.20 | async-start | bytes 15728640 | tf_op jit(solution)/shard_map/all_gather | solution.py:501
  415.8 51.8 %all-to-all-start = ((bf16[8,128,768]{2,1,0:T(8,128)(2,1)}), bf16[8,128,768]{2,1,0:T(8,128)(2,1)}, u32[]{:S(2)}, u32[]{:S(2)}) async-start(bf16[8,128,768]{2,1,0:T(8,128)(2,1)} %bitcast.510), calls=%async_computation | async-start | bytes 3145728 | tf_op jit(solution)/shard_map/all_to_all | solution.py:165
  467.5 43.3 %all-to-all-start.6 = ((bf16[8,128,768]{2,1,0:T(8,128)(2,1)}), bf16[8,128,768]{2,1,0:T(8,128)(2,1)}, u32[]{:S(2)}, u32[]{:S(2)}) async-start(bf16[8,128,768]{2,1,0:T(8,128)(2,1)} %bitcast.540), calls=%async_computation.6 | async-start | bytes 3145728 | tf_op jit(solution)/shard_map/all_to_all | solution.py:280
  532.8 42.4 %all-to-all-start.1 = ((bf16[8,128,768]{2,1,0:T(8,128)(2,1)}), bf16[8,128,768]{2,1,0:T(8,128)(2,1)}, u32[]{:S(2)}, u32[]{:S(2)}) async-start(bf16[8,128,768]{2,1,0:T(8,128)(2,1)} %bitcast.21), calls=%async_computation.1 | async-start | bytes 3145728 | tf_op jit(solution)/shard_map/all_to_all | solution.py:177
  575.2 42.1 %all-to-all-start.7 = ((bf16[8,128,768]{2,1,0:T(8,128)(2,1)}), bf16[8,128,768]{2,1,0:T(8,128)(2,1)}, u32[]{:S(2)}, u32[]{:S(2)}) async-start(bf16[8,128,768]{2,1,0:T(8,128)(2,1)} %bitcast.65), calls=%async_computation.7 | async-start | bytes 3145728 | tf_op jit(solution)/shard_map/all_to_all | solution.py:299
  623.2 42.5 %all-to-all-start.4 = ((bf16[8,128,768]{2,1,0:T(8,128)(2,1)}), bf16[8,128,768]{2,1,0:T(8,128)(2,1)}, u32[]{:S(2)}, u32[]{:S(2)}) async-start(bf16[8,128,768]{2,1,0:T(8,128)(2,1)} %bitcast.55), calls=%async_computation.4 | async-start | bytes 3145728 | tf_op jit(solution)/shard_map/all_to_all | solution.py:165
  665.7 41.3 %all-to-all-start.2 = ((bf16[8,128,768]{2,1,0:T(8,128)(2,1)}), bf16[8,128,768]{2,1,0:T(8,128)(2,1)S(1)}, u32[]{:S(2)}, u32[]{:S(2)}) async-start(bf16[8,128,768]{2,1,0:T(8,128)(2,1)} %bitcast.509), calls=%async_computation.2 | async-start | bytes 3145728 | tf_op jit(solution)/shard_map/all_to_all | solution.py:165
  707.0 42.3 %all-to-all-start.10 = ((bf16[8,128,768]{2,1,0:T(8,128)(2,1)}), bf16[8,128,768]{2,1,0:T(8,128)(2,1)}, u32[]{:S(2)}, u32[]{:S(2)}) async-start(bf16[8,128,768]{2,1,0:T(8,128)(2,1)} %bitcast.542), calls=%async_computation.12 | async-start | bytes 3145728 | tf_op jit(solution)/shard_map/all_to_all | solution.py:280
  749.3 41.3 %all-to-all-start.8 = ((bf16[8,128,768]{2,1,0:T(8,128)(2,1)}), bf16[8,128,768]{2,1,0:T(8,128)(2,1)S(1)}, u32[]{:S(2)}, u32[]{:S(2)}) async-start(bf16[8,128,768]{2,1,0:T(8,128)(2,1)} %bitcast.539), calls=%async_computation.9 | async-start | bytes 3145728 | tf_op jit(solution)/shard_map/all_to_all | solution.py:280
  790.6 42.3 %all-to-all-start.5 = ((bf16[8,128,768]{2,1,0:T(8,128)(2,1)}), bf16[8,128,768]{2,1,0:T(8,128)(2,1)}, u32[]{:S(2)}, u32[]{:S(2)}) async-start(bf16[8,128,768]{2,1,0:T(8,128)(2,1)} %bitcast.544), calls=%async_computation.5 | async-start | bytes 3145728 | tf_op jit(solution)/shard_map/all_to_all | solution.py:177
  832.9 41.3 %all-to-all-start.3 = ((bf16[8,128,768]{2,1,0:T(8,128)(2,1)}), bf16[8,128,768]{2,1,0:T(8,128)(2,1)S(1)}, u32[]{:S(2)}, u32[]{:S(2)}) async-start(bf16[8,128,768]{2,1,0:T(8,128)(2,1)} %bitcast.543), calls=%async_computation.3 | async-start | bytes 3145728 | tf_op jit(solution)/shard_map/all_to_all | solution.py:177
  874.2 41.7 %all-to-all-start.11 = ((bf16[8,128,768]{2,1,0:T(8,128)(2,1)}), bf16[8,128,768]{2,1,0:T(8,128)(2,1)S(1)}, u32[]{:S(2)}, u32[]{:S(2)}) async-start(bf16[8,128,768]{2,1,0:T(8,128)(2,1)} %bitcast.541), calls=%async_computation.13 | async-start | bytes 3145728 | tf_op jit(solution)/shard_map/all_to_all | solution.py:299
  915.9 42.1 %all-to-all-start.9 = ((bf16[8,128,768]{2,1,0:T(8,128)(2,1)}), bf16[8,128,768]{2,1,0:T(8,128)(2,1)}, u32[]{:S(2)}, u32[]{:S(2)}) async-start(bf16[8,128,768]{2,1,0:T(8,128)(2,1)} %bitcast.538), calls=%async_computation.10 | async-start | bytes 3145728 | tf_op jit(solution)/shard_map/all_to_all | solution.py:299
  920.2 214.1 %reduce-scatter.12.cloned.1.call-start = ((), (), s32[]{:S(2)}) async-start(), calls=%async_computation.24 | async-start | bytes 7077888 | tf_op jit(solution)/shard_map/reduce_scatter | solution.py:359
  1006.4 139.2 %reduce-scatter.8.cloned.1.call-start = ((), (), s32[]{:S(2)}) async-start(), calls=%async_computation.22 | async-start | bytes 7077888 | tf_op jit(solution)/shard_map/reduce_scatter | solution.py:359
  1046.5 169.6 %reduce-scatter.10.cloned.1.call-start = ((), (), s32[]{:S(2)}) async-start(), calls=%async_computation.23 | async-start | bytes 7077888 | tf_op jit(solution)/shard_map/reduce_scatter | solution.py:359
  1087.8 255.4 %reduce-scatter.16.cloned.1.call-start = ((), (), s32[]{:S(2)}) async-start(), calls=%async_computation.26 | async-start | bytes 3932160 | tf_op jit(solution)/shard_map/reduce_scatter | solution.py:424
  1109.8 270.2 %reduce-scatter.14.cloned.1.call-start = ((), (), s32[]{:S(2)}) async-start(), calls=%async_computation.25 | async-start | bytes 14008320 | tf_op jit(solution)/shard_map/reduce_scatter | solution.py:424
  1271.7 155.0 %reduce-scatter.20.cloned.1.call-start = ((), (), s32[]{:S(2)}) async-start(), calls=%async_computation.28 | async-start | bytes 3932160 | tf_op jit(solution)/shard_map/reduce_scatter | solution.py:424
  1288.3 211.5 %reduce-scatter.18.cloned.1.call-start = ((), (), s32[]{:S(2)}) async-start(), calls=%async_computation.27 | async-start | bytes 7864320 | tf_op jit(solution)/shard_map/reduce_scatter | solution.py:424
  1331.0 256.4 %all-reduce.10.cloned.1.call-start = ((), (), s32[]{:S(2)}) async-start(), calls=%async_computation.29 | async-start | bytes 7176192 | tf_op jit(solution)/shard_map/psum | solution.py:439
  (309 other events, 3787.1 us)
Sparse Core Ops, SparseCore 0:
  14.6 61.2 all-gather.3
  78.4 70.0 all-gather.7
  153.0 195.5 all-reduce.11
  350.3 122.7 all-gather.5
  1006.5 68.6 reduce-scatter.11
  1077.4 68.1 reduce-scatter.7
  1147.9 68.1 reduce-scatter.9
  1219.1 42.3 reduce-scatter.15
  1271.9 108.0 reduce-scatter.13
  1382.8 43.8 reduce-scatter.19
  1429.7 70.0 reduce-scatter.17
  1502.1 85.2 all-reduce.9

commit v2 on v1

v2 whole, which is shorter than its diff:
```python
import functools
import math

import jax
import jax.numpy as jnp
import numpy as np
from jax import lax
from jax.experimental import pallas as pl
from jax.experimental.pallas import tpu as pltpu
from jax.sharding import PartitionSpec as P

HEADS = 12
HD = 64
PROMPT = 1024
CLEN = 128
LANES = 128
ROUTER_AT = 2

epsilon = 1e-05
neg_large = -1e30
low = jnp.bfloat16
f32 = jnp.float32
VMEM_LIMIT = 66_000_000


def mm(a, b):
    return jnp.dot(a, b, preferred_element_type=f32)


def mm_nt(a, b):
    return lax.dot_general(a, b, (((1,), (1,)), ((), ())), preferred_element_type=f32)


def mm_tn(a, b):
    return lax.dot_general(a, b, (((0,), (0,)), ((), ())), preferred_element_type=f32)


def whole(shape):
    zeros = (0,) * len(shape)
    return pl.BlockSpec(shape, lambda *_: zeros, pipeline_mode=pl.Buffered(1))


def per_step(shape, axis):
    rank = len(shape)
    return pl.BlockSpec(shape, lambda m: tuple(m if d == axis else 0 for d in range(rank)))


def params():
    return pltpu.CompilerParams(
        dimension_semantics=("arbitrary",), vmem_limit_bytes=VMEM_LIMIT
    )


def inverse_rms(values):
    return lax.rsqrt(jnp.mean(values * values, axis=-1, keepdims=True) + epsilon)


def turn(values, cos_table, sine_table):
    lane = lax.broadcasted_iota(jnp.int32, values.shape, 1)
    partner = jnp.where(
        lane % HD < HD // 2,
        pltpu.roll(values, LANES - HD // 2, 1),
        pltpu.roll(values, HD // 2, 1),
    )
    return values * cos_table + partner * sine_table


def slot_ranks(route_rows, experts):
    rows = max(experts, 16)
    tok = route_rows.shape[1]
    expert_id = lax.broadcasted_iota(jnp.int32, (rows, tok), 0)
    member = (route_rows[0:1, :] == expert_id) | (route_rows[1:2, :] == expert_id)
    earlier = lax.broadcasted_iota(jnp.int32, (tok, tok), 0) < lax.broadcasted_iota(
        jnp.int32, (tok, tok), 1
    )
    rank = mm(
        jnp.where(member, 1.0, 0.0).astype(low), jnp.where(earlier, 1.0, 0.0).astype(low)
    )
    return jnp.where(member, rank, -1.0)


def placement(ranks, expert, capacity):
    tok = ranks.shape[1]
    slot = lax.broadcasted_iota(jnp.int32, (capacity, tok), 0).astype(f32)
    return jnp.where(slot == ranks[expert : expert + 1, :], 1.0, 0.0).astype(low)


def send_kernel(experts, capacity, rows_ref, route_ref, out_ref):
    ranks = slot_ranks(route_ref[0], experts)
    rows = rows_ref[0]
    for e in range(experts):
        out_ref[e, 0] = mm(placement(ranks, e, capacity), rows).astype(low)


def gather_slots(ranks, slots_ref, experts, capacity):
    total = None
    for e in range(experts):
        part = mm_tn(placement(ranks, e, capacity), slots_ref[e, 0])
        total = part if total is None else total + part
    return total


def attend_kernel(
    experts,
    capacity,
    own_ref,
    prompt_ref,
    route_ref,
    weight_ref,
    gain_ref,
    cos_p,
    sin_p,
    cos_o,
    sin_o,
    bias_p,
    bias_o,
    sent_ref,
    mixed_ref,
    resid_ref,
    att_ref,
    query_ref,
    key_ref,
    value_ref,
    lse_ref,
    normed_s,
    value_t,
    out_t,
):
    tok, width = own_ref.shape[1:]
    gain_one = gain_ref[0:1, :]
    gain_two = gain_ref[1:2, :]
    step = 256
    for r in range(0, PROMPT, step):
        rows = prompt_ref[0, r : r + step, :].astype(f32)
        normed_s[r : r + step, :] = (rows * inverse_rms(rows) * gain_one).astype(low)
    own = own_ref[0].astype(f32)
    normed_s[PROMPT:, :] = (own * inverse_rms(own) * gain_one).astype(low)
    total = PROMPT + tok
    for j in range(0, width, step):
        keys = mm(normed_s[...], weight_ref[:, width + j : width + j + step])
        for h in range(0, step, LANES):
            key_ref[0, :PROMPT, j + h : j + h + LANES] = turn(
                keys[:PROMPT, h : h + LANES], cos_p[...], sin_p[...]
            ).astype(low)
            key_ref[0, PROMPT:, j + h : j + h + LANES] = turn(
                keys[PROMPT:, h : h + LANES], cos_o[...], sin_o[...]
            ).astype(low)
        values = mm(normed_s[...], weight_ref[:, 2 * width + j : 2 * width + j + step])
        value_ref[0, :, j : j + step] = values.astype(low)
        value_t[j : j + step, :] = values.T.astype(low)
        queries = mm(normed_s[PROMPT:, :], weight_ref[:, j : j + step])
        for h in range(0, step, LANES):
            query_ref[0, :, j + h : j + h + LANES] = turn(
                queries[:, h : h + LANES], cos_o[...], sin_o[...]
            ).astype(low)

    lane = lax.broadcasted_iota(jnp.int32, (tok, LANES), 1)

    def pair(hp, carry):
        col = pl.multiple_of(hp * LANES, LANES)
        query = query_ref[0, :, pl.ds(col, LANES)] * low(1.0 / math.sqrt(HD))
        keys = key_ref[0, :PROMPT, pl.ds(col, LANES)]
        keys_own = key_ref[0, PROMPT:, pl.ds(col, LANES)]
        for i in range(2):
            masked = jnp.where(lane // HD == i, query, jnp.zeros_like(query))
            score = mm_nt(keys, masked) + bias_p[...]
            score_own = jnp.concatenate(
                [
                    mm_nt(keys_own[b : b + CLEN], masked[b : b + CLEN]) + bias_o[...]
                    for b in range(0, tok, CLEN)
                ],
                axis=1,
            )
            top = jnp.maximum(
                jnp.max(score, axis=0, keepdims=True), jnp.max(score_own, axis=0, keepdims=True)
            )
            weight = jnp.exp(score - top)
            weight_own = jnp.exp(score_own - top)
            norm = jnp.sum(weight, axis=0, keepdims=True) + jnp.sum(
                weight_own, axis=0, keepdims=True
            )
            at = pl.multiple_of(col + i * HD, HD)
            turned = value_t[pl.ds(at, HD), :]
            weight_low = weight_own.astype(low)
            result = mm(turned[:, :PROMPT], weight.astype(low)) + jnp.concatenate(
                [
                    mm(turned[:, PROMPT + b : PROMPT + b + CLEN], weight_low[:, b : b + CLEN])
                    for b in range(0, tok, CLEN)
                ],
                axis=1,
            )
            out_t[pl.ds(at, HD), :] = result / norm
            lse_ref[0, pl.ds(2 * hp + i, 1), :] = top + jnp.log(norm)
        return carry

    lax.fori_loop(0, width // LANES, pair, 0)
    attended = out_t[...].T.astype(low)
    att_ref[0] = attended
    resid = own + mm(attended, weight_ref[:, 3 * width : 4 * width])
    resid_ref[0] = resid
    mixed = (resid * inverse_rms(resid) * gain_two).astype(low)
    mixed_ref[0] = mixed
    ranks = slot_ranks(route_ref[0], experts)
    for e in range(experts):
        sent_ref[e, 0] = mm(placement(ranks, e, capacity), mixed).astype(low)


def mlp_kernel(
    gated,
    rows_ref,
    cot_ref,
    wide_ref,
    deep_ref,
    router_ref,
    onehot_ref,
    y_ref,
    dx_ref,
    hidden_ref,
    dwide_ref,
    *rest,
):
    if gated:
        dout_ref, dlogit_ref, gate_s, up_s, acc = rest
    else:
        gate_s, up_s, acc = rest
    ff = deep_ref.shape[0]
    tile = 512
    rows = rows_ref[...]

    def forward(j, carry):
        at = pl.multiple_of(j * tile, tile)
        gate = mm(rows, wide_ref[:, pl.ds(at, tile)])
        up = mm(rows, wide_ref[:, pl.ds(pl.multiple_of(ff + at, tile), tile)])
        gate_s[:, pl.ds(at, tile)] = gate
        up_s[:, pl.ds(at, tile)] = up
        hidden_ref[:, pl.ds(at, tile)] = (gate * jax.nn.sigmoid(gate) * up).astype(low)
        return carry

    lax.fori_loop(0, ff // tile, forward, 0)
    result = mm(hidden_ref[...], deep_ref[...])
    cot = cot_ref[...]
    if gated:
        result = result.astype(low).astype(f32)
        valid = onehot_ref[1:2, :]
        chosen = onehot_ref[0:1, :]
        logits = jnp.where(valid > 0.5, mm(rows, router_ref[...]), neg_large)
        logits = jnp.exp(logits - jnp.max(logits, axis=-1, keepdims=True))
        probs = logits / jnp.sum(logits, axis=-1, keepdims=True)
        gate_value = jnp.sum(probs * chosen, axis=-1, keepdims=True)
        cot32 = cot.astype(f32)
        gate_grad = jnp.sum(cot32 * result, axis=-1, keepdims=True)
        dlogit = (probs * (chosen - gate_value) * gate_grad).astype(low)
        dlogit_ref[...] = dlogit
        y_ref[...] = (gate_value * result).astype(y_ref.dtype)
        cot = (gate_value * cot32).astype(low)
        dout_ref[...] = cot
        acc[...] = mm_nt(dlogit, router_ref[...])
    else:
        y_ref[...] = result.astype(y_ref.dtype)
        acc[...] = jnp.zeros_like(acc)

    def backward(j, carry):
        at = pl.multiple_of(j * tile, tile)
        also = pl.multiple_of(ff + at, tile)
        dhidden = mm_nt(cot, deep_ref[pl.ds(at, tile), :])
        gate = gate_s[:, pl.ds(at, tile)]
        sigma = jax.nn.sigmoid(gate)
        act = gate * sigma
        dgate = (dhidden * up_s[:, pl.ds(at, tile)] * (sigma + act * (1.0 - sigma))).astype(low)
        dup = (dhidden * act).astype(low)
        dwide_ref[0, :, pl.ds(at, tile)] = dgate
        dwide_ref[1, :, pl.ds(at, tile)] = dup
        acc[...] += mm_nt(dgate, wide_ref[:, pl.ds(at, tile)]) + mm_nt(
            dup, wide_ref[:, pl.ds(also, tile)]
        )
        return carry

    lax.fori_loop(0, ff // tile, backward, 0)
    dx_ref[...] = acc[...].astype(dx_ref.dtype)


def mlp(rows, cot, wide, deep, router, onehot, gated):
    count, width = rows.shape
    ff = deep.shape[0]
    tile = math.gcd(count, 512)
    by_row = lambda last: pl.BlockSpec((tile, last), lambda m: (m, 0))
    kept = f32 if not gated else low
    out_shape = [
        jax.ShapeDtypeStruct((count, width), kept),
        jax.ShapeDtypeStruct((count, width), low),
        jax.ShapeDtypeStruct((count, ff), low),
        jax.ShapeDtypeStruct((2, count, ff), low),
    ]
    out_specs = [
        by_row(width),
        by_row(width),
        by_row(ff),
        pl.BlockSpec((2, tile, ff), lambda m: (0, m, 0)),
    ]
    if gated:
        out_shape += [
            jax.ShapeDtypeStruct((count, width), low),
            jax.ShapeDtypeStruct((count, LANES), low),
        ]
        out_specs += [by_row(width), by_row(LANES)]
    return pl.pallas_call(
        functools.partial(mlp_kernel, gated),
        grid=(count // tile,),
        in_specs=[
            by_row(width),
            by_row(width),
            whole((width, 2 * ff)),
            whole((ff, width)),
            whole((width, LANES)),
            whole((2, LANES)),
        ],
        out_specs=out_specs,
        out_shape=out_shape,
        scratch_shapes=[
            pltpu.VMEM((tile, ff), f32),
            pltpu.VMEM((tile, ff), f32),
            pltpu.VMEM((tile, width), f32),
        ],
        compiler_params=params(),
        cost_estimate=pl.CostEstimate(
            flops=12 * count * width * ff,
            bytes_accessed=2 * (3 * width * ff + 4 * count * width + 3 * count * ff),
            transcendentals=2 * count * ff,
        ),
    )(rows, cot, wide, deep, router, onehot)


def mlp_weights_kernel(
    routed, rows_ref, cot_ref, hidden_ref, dwide_ref, dlogit_ref, gwide_ref, gdeep_ref, *rest
):
    if routed:
        grouter_ref, rows_t, cot_t = rest
    else:
        rows_t, cot_t = rest

    @pl.when(pl.program_id(0) == 0)
    def _():
        step = 256
        for r in range(0, rows_ref.shape[0], step):
            rows_t[:, r : r + step] = rows_ref[r : r + step, :].T
            cot_t[:, r : r + step] = cot_ref[r : r + step, :].T
        if routed:
            grouter_ref[...] = mm(rows_t[...], dlogit_ref[...])

    gwide_ref[0] = mm(rows_t[...], dwide_ref[0]).astype(low)
    gwide_ref[1] = mm(rows_t[...], dwide_ref[1]).astype(low)
    gdeep_ref[...] = mm(cot_t[...], hidden_ref[...]).T.astype(low)


def mlp_weights(rows, cot, hidden, dwide, dlogit):
    count, width = rows.shape
    ff = hidden.shape[1]
    tile = 256
    routed = dlogit is not None
    if not routed:
        dlogit = jnp.zeros((8, LANES), low)
    out_shape = [
        jax.ShapeDtypeStruct((2, width, ff), low),
        jax.ShapeDtypeStruct((ff, width), low),
    ]
    out_specs = [
        pl.BlockSpec((2, width, tile), lambda j: (0, 0, j)),
        pl.BlockSpec((tile, width), lambda j: (j, 0)),
    ]
    if routed:
        out_shape.append(jax.ShapeDtypeStruct((width, LANES), f32))
        out_specs.append(whole((width, LANES)))
    return pl.pallas_call(
        functools.partial(mlp_weights_kernel, routed),
        grid=(ff // tile,),
        in_specs=[
            whole((count, width)),
            whole((count, width)),
            pl.BlockSpec((count, tile), lambda j: (0, j)),
            pl.BlockSpec((2, count, tile), lambda j: (0, 0, j)),
            whole(dlogit.shape),
        ],
        out_specs=out_specs,
        out_shape=out_shape,
        scratch_shapes=[pltpu.VMEM((width, count), low), pltpu.VMEM((width, count), low)],
        compiler_params=params(),
        cost_estimate=pl.CostEstimate(
            flops=6 * count * width * ff,
            bytes_accessed=2 * (3 * width * ff + 2 * count * width + 3 * count * ff),
            transcendentals=0,
        ),
    )(rows, cot, hidden, dwide, dlogit)


def attend_back_kernel(
    experts,
    capacity,
    own_ref,
    prompt_ref,
    route_ref,
    weight_ref,
    gain_ref,
    cos_p,
    sin_p,
    cos_o,
    sin_o,
    bias_p,
    bias_o,
    resid_ref,
    att_ref,
    query_ref,
    key_ref,
    value_ref,
    lse_ref,
    cot_ref,
    dmix_ref,
    slots_ref,
    grouter_ref,
    dres_ref,
    down_ref,
    dprompt_ref,
    grads_ref,
    normed_t,
    key_t,
    datt_s,
    delta_s,
    dquery_t,
    dkey_s,
    dvalue_s,
    acc,
    small,
):
    tok, width = own_ref.shape[1:]
    total = PROMPT + tok
    gain_one = gain_ref[0:1, :]
    gain_two = gain_ref[1:2, :]
    step = 256
    first = pl.program_id(0) == 0
    last = pl.program_id(0) == pl.num_programs(0) - 1

    @pl.when(first)
    def _():
        acc[...] = jnp.zeros_like(acc)
        small[...] = jnp.zeros_like(small)

    ranks = slot_ranks(route_ref[0], experts)
    dmix = dmix_ref[0].astype(f32) + gather_slots(ranks, slots_ref, experts, capacity)
    resid = resid_ref[0]
    inverse = inverse_rms(resid)
    hat = resid * inverse
    small[1:2, :] += jnp.sum(dmix * hat, axis=0, keepdims=True)
    scaled = dmix * gain_two
    dres = cot_ref[0].astype(f32) + inverse * (
        scaled - hat * jnp.mean(scaled * hat, axis=-1, keepdims=True)
    )
    dres_ref[0] = dres
    dres_low = dres.astype(low)
    attended = att_ref[0]
    acc[:, 3 * width :] += mm_tn(attended, dres_low)
    datt = mm_nt(dres_low, weight_ref[:, 3 * width : 4 * width]).astype(low)
    datt_s[...] = datt
    product = (datt.astype(f32) * attended.astype(f32)).T
    for h in range(HEADS):
        delta_s[h : h + 1, :] = jnp.sum(product[h * HD : (h + 1) * HD, :], axis=0, keepdims=True)

    for r in range(0, PROMPT, step):
        rows = prompt_ref[0, r : r + step, :].astype(f32)
        normed_t[:, r : r + step] = (rows * inverse_rms(rows) * gain_one).T.astype(low)
        key_t[:, r : r + step] = key_ref[0, r : r + step, :].T
    own = own_ref[0].astype(f32)
    inverse_own = inverse_rms(own)
    normed_t[:, PROMPT:] = (own * inverse_own * gain_one).T.astype(low)
    key_t[:, PROMPT:] = key_ref[0, PROMPT:, :].T

    lane = lax.broadcasted_iota(jnp.int32, (tok, LANES), 1)
    scale = 1.0 / math.sqrt(HD)

    def pair(hp, carry):
        col = pl.multiple_of(hp * LANES, LANES)
        query = query_ref[0, :, pl.ds(col, LANES)] * low(scale)
        keys = key_ref[0, :PROMPT, pl.ds(col, LANES)]
        keys_own = key_ref[0, PROMPT:, pl.ds(col, LANES)]
        values = value_ref[0, :PROMPT, pl.ds(col, LANES)]
        values_own = value_ref[0, PROMPT:, pl.ds(col, LANES)]
        datt = datt_s[:, pl.ds(col, LANES)]
        dkey = dvalue = None
        dkey_own = [None] * (tok // CLEN)
        dvalue_own = [None] * (tok // CLEN)
        for i in range(2):
            masked = jnp.where(lane // HD == i, query, jnp.zeros_like(query))
            dmasked = jnp.where(lane // HD == i, datt, jnp.zeros_like(datt))
            lse = lse_ref[0, pl.ds(2 * hp + i, 1), :]
            delta = delta_s[pl.ds(2 * hp + i, 1), :]
            at = pl.multiple_of(col + i * HD, HD)
            turned = key_t[pl.ds(at, HD), :]
            prob = jnp.exp(mm_nt(keys, masked) + bias_p[...] - lse)
            dscore = (prob * (mm_nt(values, dmasked) - delta)).astype(low)
            part_k = mm(dscore, masked)
            part_v = mm(prob.astype(low), dmasked)
            dkey = part_k if dkey is None else dkey + part_k
            dvalue = part_v if dvalue is None else dvalue + part_v
            dquery = mm(turned[:, :PROMPT], dscore)
            pieces = []
            for n, b in enumerate(range(0, tok, CLEN)):
                q_block = masked[b : b + CLEN]
                d_block = dmasked[b : b + CLEN]
                p_own = jnp.exp(
                    mm_nt(keys_own[b : b + CLEN], q_block) + bias_o[...] - lse[:, b : b + CLEN]
                )
                ds_own = (
                    p_own * (mm_nt(values_own[b : b + CLEN], d_block) - delta[:, b : b + CLEN])
                ).astype(low)
                part_k = mm(ds_own, q_block)
                part_v = mm(p_own.astype(low), d_block)
                dkey_own[n] = part_k if dkey_own[n] is None else dkey_own[n] + part_k
                dvalue_own[n] = part_v if dvalue_own[n] is None else dvalue_own[n] + part_v
                pieces.append(mm(turned[:, PROMPT + b : PROMPT + b + CLEN], ds_own))
            dquery_t[pl.ds(at, HD), :] = (dquery + jnp.concatenate(pieces, axis=1)) * scale
        dkey_s[:PROMPT, pl.ds(col, LANES)] = turn(dkey, cos_p[...], -sin_p[...]).astype(low)
        dvalue_s[:PROMPT, pl.ds(col, LANES)] = dvalue.astype(low)
        dkey_s[PROMPT:, pl.ds(col, LANES)] = turn(
            jnp.concatenate(dkey_own, axis=0), cos_o[...], -sin_o[...]
        ).astype(low)
        dvalue_s[PROMPT:, pl.ds(col, LANES)] = jnp.concatenate(dvalue_own, axis=0).astype(low)
        return carry

    lax.fori_loop(0, width // LANES, pair, 0)

    for j in range(0, width, step):
        block = dquery_t[j : j + step, :].T
        dquery = jnp.concatenate(
            [turn(block[:, h : h + LANES], cos_o[...], -sin_o[...]) for h in range(0, step, LANES)],
            axis=1,
        ).astype(low)
        datt_s[:, j : j + step] = dquery
        acc[:, j : j + step] += mm(normed_t[:, PROMPT:], dquery)
        acc[:, width + j : width + j + step] += mm(normed_t[...], dkey_s[:, j : j + step])
        acc[:, 2 * width + j : 2 * width + j + step] += mm(
            normed_t[...], dvalue_s[:, j : j + step]
        )

    dnorm_own = (
        mm_nt(datt_s[...], weight_ref[:, :width])
        + mm_nt(dkey_s[PROMPT:, :], weight_ref[:, width : 2 * width])
        + mm_nt(dvalue_s[PROMPT:, :], weight_ref[:, 2 * width : 3 * width])
    )
    down_ref[0] = dnorm_own
    norm_grad = jnp.sum(dnorm_own * own * inverse_own, axis=0, keepdims=True)
    for r in range(0, PROMPT, step):
        part = mm_nt(dkey_s[r : r + step, :], weight_ref[:, width : 2 * width]) + mm_nt(
            dvalue_s[r : r + step, :], weight_ref[:, 2 * width : 3 * width]
        )
        dprompt_ref[0, r : r + step, :] = part.astype(low)
        rows = prompt_ref[0, r : r + step, :].astype(f32)
        norm_grad += jnp.sum(part * rows * inverse_rms(rows), axis=0, keepdims=True)
    small[0:1, :] += norm_grad

    @pl.when(last)
    def _():
        for j in range(0, 4 * width, step):
            grads_ref[:, j : j + step] = acc[:, j : j + step].astype(low)
        grads_ref[:, 4 * width :] = (small[...].T + grouter_ref[...]).astype(low)


def finish_kernel(experts, capacity, resid_ref, shared_ref, slots_ref, route_ref, out_ref):
    ranks = slot_ranks(route_ref[0], experts)
    out_ref[0] = (
        resid_ref[0] + shared_ref[0] + gather_slots(ranks, slots_ref, experts, capacity)
    ).astype(low)


def rotary(positions):
    middle = HD // 2
    frequency = jnp.exp(jnp.arange(middle).astype(f32) * (-2.0 * math.log(10000.0) / HD))
    angles = positions.astype(f32)[:, None] * frequency[None, :]
    cos_table, sine_table = jnp.cos(angles), jnp.sin(angles)
    return (
        jnp.concatenate([cos_table] * 4, axis=1),
        jnp.concatenate([-sine_table, sine_table] * 2, axis=1),
    )


def per_device(
    tokens,
    cotangent,
    routes,
    attn_norm,
    query_weight,
    key_weight,
    value_weight,
    out_weight,
    ffn_norm,
    router_weight,
    shared_gate,
    shared_up,
    shared_down,
    expert_gate,
    expert_up,
    expert_down,
):
    batches, tok, width = tokens.shape
    experts = router_weight.shape[1]
    ff = shared_gate.shape[1]
    capacity = 4 * tok // experts
    holders = PROMPT // tok
    me = lax.axis_index("expert")

    small = jnp.concatenate([attn_norm[:, None], ffn_norm[:, None], router_weight], axis=1)
    small = jnp.pad(small, ((0, 0), (0, LANES - small.shape[1])))
    attn_all = lax.all_gather(
        jnp.concatenate([query_weight, key_weight, value_weight, out_weight, small], axis=1),
        "dp",
        axis=0,
        tiled=True,
    )
    prompt = lax.all_gather(tokens, "expert", axis=1, tiled=True)[:, :PROMPT]
    shared_wide = lax.all_gather(
        jnp.concatenate([shared_gate, shared_up], axis=1), "dp", axis=0, tiled=True
    )
    shared_deep = lax.all_gather(shared_down, "dp", axis=0, tiled=True)
    expert_wide = lax.all_gather(
        jnp.concatenate([expert_gate[0], expert_up[0]], axis=1), "dp", axis=0, tiled=True
    )
    expert_deep = lax.all_gather(expert_down[0], "dp", axis=0, tiled=True)

    small_all = attn_all[:, 4 * width :]
    gains = small_all[:, :ROUTER_AT].T.astype(f32)
    router = small_all
    lane = jnp.arange(LANES, dtype=jnp.int32)
    onehot = jnp.stack(
        [
            (lane == me + ROUTER_AT).astype(f32),
            ((lane >= ROUTER_AT) & (lane < ROUTER_AT + experts)).astype(f32),
        ]
    )
    route_rows = jnp.swapaxes(routes, 1, 2)

    row_at = jnp.arange(tok, dtype=jnp.int32)
    query_pos = me * tok + row_at
    later = me >= holders
    cos_o, sin_o = rotary(jnp.where(later, PROMPT + row_at % CLEN, query_pos))
    cos_p, sin_p = rotary(jnp.arange(PROMPT, dtype=jnp.int32))
    key_pos = jnp.arange(PROMPT, dtype=jnp.int32)[:, None]
    bias_p = jnp.where(later | (key_pos <= query_pos[None, :]), 0.0, neg_large).astype(f32)
    near = jnp.arange(CLEN, dtype=jnp.int32)
    bias_o = jnp.where(later & (near[:, None] <= near[None, :]), 0.0, neg_large).astype(f32)

    slots_shape = (experts, batches, capacity, width)
    slots_spec = per_step((experts, 1, capacity, width), 1)
    row_spec = per_step((1, tok, width), 0)
    route_spec = per_step((1, 2, tok), 0)

    cot_sent = pl.pallas_call(
        functools.partial(send_kernel, experts, capacity),
        grid=(batches,),
        in_specs=[row_spec, route_spec],
        out_specs=slots_spec,
        out_shape=jax.ShapeDtypeStruct(slots_shape, low),
        compiler_params=params(),
    )(cotangent, route_rows)
    exchange = functools.partial(
        lax.all_to_all, axis_name="expert", split_axis=0, concat_axis=0, tiled=True
    )
    cot_slots = exchange(cot_sent)

    total = PROMPT + tok
    weight_spec = whole((width, 4 * width + LANES))
    table_specs = [
        whole((PROMPT, LANES)),
        whole((PROMPT, LANES)),
        whole((tok, LANES)),
        whole((tok, LANES)),
        whole((PROMPT, tok)),
        whole((CLEN, CLEN)),
    ]
    tables = (cos_p, sin_p, cos_o, sin_o, bias_p, bias_o)
    full_spec = per_step((1, total, width), 0)
    prompt_spec = per_step((1, PROMPT, width), 0)
    lse_spec = per_step((1, 16, tok), 0)
    rows_shape = (batches, tok, width)
    sent, mixed, resid, attended, query, keys, values, lse = pl.pallas_call(
        functools.partial(attend_kernel, experts, capacity),
        grid=(batches,),
        in_specs=[row_spec, prompt_spec, route_spec, weight_spec, whole((2, width))]
        + table_specs,
        out_specs=[
            slots_spec,
            row_spec,
            row_spec,
            row_spec,
            row_spec,
            full_spec,
            full_spec,
            lse_spec,
        ],
        out_shape=[
            jax.ShapeDtypeStruct(slots_shape, low),
            jax.ShapeDtypeStruct(rows_shape, low),
            jax.ShapeDtypeStruct(rows_shape, f32),
            jax.ShapeDtypeStruct(rows_shape, low),
            jax.ShapeDtypeStruct(rows_shape, low),
            jax.ShapeDtypeStruct((batches, total, width), low),
            jax.ShapeDtypeStruct((batches, total, width), low),
            jax.ShapeDtypeStruct((batches, 16, tok), f32),
        ],
        scratch_shapes=[
            pltpu.VMEM((total, width), low),
            pltpu.VMEM((width, total), low),
            pltpu.VMEM((width, tok), f32),
        ],
        compiler_params=params(),
        cost_estimate=pl.CostEstimate(
            flops=batches * 12 * tok * width * total, bytes_accessed=30_000_000, transcendentals=0
        ),
    )(tokens, prompt, route_rows, attn_all, gains, *tables)

    received = exchange(sent)

    flat = (batches * tok, width)
    shared_y, shared_dx, shared_hidden, shared_dwide = mlp(
        mixed.reshape(flat), cotangent.reshape(flat), shared_wide, shared_deep, router, onehot, False
    )
    gshared_wide, gshared_deep = mlp_weights(
        mixed.reshape(flat), cotangent.reshape(flat), shared_hidden, shared_dwide, None
    )

    slots_flat = (experts * batches * capacity, width)
    slot_rows = received.reshape(slots_flat)
    expert_y, expert_dx, hidden, dwide, dout, dlogit = mlp(
        slot_rows, cot_slots.reshape(slots_flat), expert_wide, expert_deep, router, onehot, True
    )
    dx_back = exchange(expert_dx.reshape(slots_shape))
    y_back = exchange(expert_y.reshape(slots_shape))
    gexpert_wide, gexpert_deep, grouter = mlp_weights(slot_rows, dout, hidden, dwide, dlogit)

    dres, dnorm_own, dprompt, gattn = pl.pallas_call(
        functools.partial(attend_back_kernel, experts, capacity),
        grid=(batches,),
        in_specs=[row_spec, prompt_spec, route_spec, weight_spec, whole((2, width))]
        + table_specs
        + [
            row_spec,
            row_spec,
            row_spec,
            full_spec,
            full_spec,
            lse_spec,
            row_spec,
            row_spec,
            slots_spec,
            whole((width, LANES)),
        ],
        out_specs=[
            row_spec,
            row_spec,
            prompt_spec,
            whole((width, 4 * width + LANES)),
        ],
        out_shape=[
            jax.ShapeDtypeStruct(rows_shape, f32),
            jax.ShapeDtypeStruct(rows_shape, f32),
            jax.ShapeDtypeStruct((batches, PROMPT, width), low),
            jax.ShapeDtypeStruct((width, 4 * width + LANES), low),
        ],
        scratch_shapes=[
            pltpu.VMEM((width, total), low),
            pltpu.VMEM((width, total), low),
            pltpu.VMEM((tok, width), low),
            pltpu.VMEM((16, tok), f32),
            pltpu.VMEM((width, tok), f32),
            pltpu.VMEM((total, width), low),
            pltpu.VMEM((total, width), low),
            pltpu.VMEM((width, 4 * width), f32),
            pltpu.VMEM((LANES, width), f32),
        ],
        compiler_params=params(),
        cost_estimate=pl.CostEstimate(
            flops=batches * 24 * tok * width * total, bytes_accessed=40_000_000, transcendentals=0
        ),
    )(
        tokens,
        prompt,
        route_rows,
        attn_all,
        gains,
        *tables,
        resid,
        attended,
        query,
        keys,
        values,
        lse,
        cotangent,
        shared_dx.reshape(rows_shape),
        dx_back,
        grouter,
    )

    output = pl.pallas_call(
        functools.partial(finish_kernel, experts, capacity),
        grid=(batches,),
        in_specs=[row_spec, row_spec, slots_spec, route_spec],
        out_specs=row_spec,
        out_shape=jax.ShapeDtypeStruct(rows_shape, low),
        compiler_params=params(),
    )(resid, shared_y.reshape(rows_shape), y_back, route_rows)

    padded = jnp.pad(dprompt, ((0, 0), (0, (experts - holders) * tok), (0, 0)))
    dnorm_prompt = lax.psum_scatter(padded, "expert", scatter_dimension=1, tiled=True)
    dnorm = dnorm_own + dnorm_prompt.astype(f32)
    own = tokens.astype(f32)
    inverse = inverse_rms(own)
    hat = own * inverse
    scaled = dnorm * gains[0][None, None, :]
    input_grad = (
        dres + inverse * (scaled - hat * jnp.mean(scaled * hat, axis=-1, keepdims=True))
    ).astype(low)

    def scatter(value, dimension):
        return lax.psum_scatter(value, "dp", scatter_dimension=dimension, tiled=True)

    gexpert_wide = scatter(gexpert_wide, 1).astype(f32)
    gexpert_deep = scatter(gexpert_deep, 0).astype(f32)
    gshared_wide = lax.psum(scatter(gshared_wide, 1), "expert").astype(f32)
    gshared_deep = lax.psum(scatter(gshared_deep, 0), "expert").astype(f32)
    gattn = lax.psum(scatter(gattn, 0), "expert").astype(f32)
    at = 4 * width
    return (
        output,
        input_grad,
        gattn[:, at],
        gattn[:, :width],
        gattn[:, width : 2 * width],
        gattn[:, 2 * width : 3 * width],
        gattn[:, 3 * width : at],
        gattn[:, at + 1],
        gattn[:, at + ROUTER_AT : at + ROUTER_AT + experts],
        gshared_wide[0],
        gshared_wide[1],
        gshared_deep,
        gexpert_wide[:1],
        gexpert_wide[1:],
        gexpert_deep[None],
    )


def solution(mesh):
    rows = P(None, ("dp", "expert"), None)
    by_row = P("dp", None)
    by_expert = P("expert", "dp", None)
    return jax.shard_map(
        per_device,
        mesh=mesh,
        in_specs=(
            rows,
            rows,
            rows,
            P("dp"),
            by_row,
            by_row,
            by_row,
            by_row,
            P("dp"),
            by_row,
            by_row,
            by_row,
            by_row,
            by_expert,
            by_expert,
            by_expert,
        ),
        out_specs=(
            rows,
            rows,
            P("dp"),
            by_row,
            by_row,
            by_row,
            by_row,
            P("dp"),
            by_row,
            by_row,
            by_row,
            by_row,
            by_expert,
            by_expert,
            by_expert,
        ),
        check_vma=False,
    )
```

time: 1610 us -> 1120 us (0.70)
  matrix products: 510 us -> 0 us
  Pallas kernels: 0 us -> 331 us
  local copies, waits for them, and re-layouts: 153 us -> 31.7 us
  other arithmetic: 106 us -> 24.9 us
  waiting for transfers between devices: 763 us -> 687 us
  starting transfers between devices: 53.1 us -> 21.5 us
    dot_general x129 -> x0, matrix products: 510 us -> none  [the longest x39 145 us: matmul(): return jnp.dot(left_side, right_side, preferred_element_type=jnp.float32)]
    pallas_call x0 -> x8, Pallas kernels: none -> 331 us  [the longest x2 126 us: mlp(): pl.pallas_call(functools.partial(mlp_kernel, gated), grid=(count // tile,...]
    all_gather x2 -> x5, waiting for transfers between devices: 20.9 us -> 255 us  [the longest x1 133 us: per_device(): prompt = lax.all_gather(tokens, 'expert', axis=1, tiled=True)[:, :PROMPT]]
    psum x2 -> x1, waiting for transfers between devices: 277 us -> 80.3 us  [per_device(): gattn = lax.psum(scatter(gattn, 0), 'expert').astype(f32)]
    unnamed x643 -> x36, local copies, waits for them, and re-layouts: 64.1 us -> 8.12 us
    reduce_scatter x7 -> x6, waiting for transfers between devices: 228 us -> 178 us  [the longest x5 90.1 us: scatter(): lax.psum_scatter(value, 'dp', scatter_dimension=dimension, tiled=True)]
    all_to_all x12 -> x4, waiting for transfers between devices: 180 us -> 133 us  [the longest x1 67.7 us: per_device(): y_back = exchange(expert_y.reshape(slots_shape))]
    all_to_all x12 -> x4, starting transfers between devices: 51.8 us -> 20.7 us  [the longest x1 6.49 us: per_device(): cot_slots = exchange(cot_sent)]
  transfers between devices with their start and end apart: 24 -> 17, of which waited for: 20 -> 10; matrix products, arithmetic and copies ran while one was open for 40% -> 4% of each run, Pallas kernels for 0% -> 30%
where the time goes in v2:
time: 1120 us; the launch traced here: 1110 us
  waiting for transfers between devices  687 us (61%)
  Pallas kernels  331 us (30%)
  local copies, waits for them, and re-layouts  31.7 us (3%)
  other arithmetic  24.9 us (2%)
  starting transfers between devices  21.5 us (2%)
  between operations  14.4 us (1%)
    all_gather x1, waiting for transfers between devices, per_device(): prompt = lax.all_gather(tokens, 'expert', axis=1, tiled=True)[:, :PROMPT]  133 us
    pallas_call x2, Pallas kernels, mlp(): pl.pallas_call(functools.partial(mlp_kernel, gated), grid=(count // tile,...  126 us
    reduce_scatter x5, waiting for transfers between devices, scatter(): lax.psum_scatter(value, 'dp', scatter_dimension=dimension, tiled=True)  90.1 us
    reduce_scatter x1, waiting for transfers between devices, per_device(): lax.psum_scatter(padded, 'expert', scatter_dimension=1, tiled=True)  88.3 us
    psum x1, waiting for transfers between devices, per_device(): gattn = lax.psum(scatter(gattn, 0), 'expert').astype(f32)  80.3 us
    pallas_call x1, Pallas kernels, per_device(): pl.pallas_call(functools.partial(attend_back_kernel, experts, capacity),...  80.2 us
    all_gather x1, waiting for transfers between devices, per_device(): lax.all_gather(jnp.concatenate([expert_gate[0], expert_up[0]], axis=1), '...  71.9 us
    all_to_all x1, waiting for transfers between devices, per_device(): y_back = exchange(expert_y.reshape(slots_shape))  67.7 us
  transfers between devices with their start and end apart: 17, of which 10 were waited for; matrix products, arithmetic and copies ran while one was open for 4% of the time, Pallas kernels for 30%

profile of v2, /device:TPU:0, one launch (start us, length us, event | category | flops | bytes accessed | tf_op | source)
XLA Modules:
  0.0 1110.4 jit_solution(8457591354277870537)
XLA Ops:
  18.0 4.9 shard_map.273
  23.0 6.5 all-to-all-start.1
  38.5 37.5 %all-gather.10.cloned.1.call-done.weight_ref = bf16[768,3200]{1,0:T(8,128)(2,1)} async-done(((bf16[192,3200]{1,0:T(8,128)(2,1)}), bf16[768,3200]{1,0:T(8,128)(2,1)}) %all-gather.10.cloned.1.call-update) | async-done | bytes 4915216 | tf_op jit(solution)/shard_map/all_gather | solution.py:610
  79.3 132.8 %all-gather.8.cloned.1.call-done = bf16[3,2048,768]{2,1,0:T(8,128)(2,1)} async-done(((bf16[3,256,768]{2,1,0:T(8,128)(2,1)}), bf16[3,2048,768]{2,1,0:T(8,128)(2,1)}) %all-gather.8.cloned.1.call-update) | async-done | bytes 9437200 | tf_op jit(solution)/shard_map/all_gather | solution.py:616
  212.1 4.8 slice.61.prompt_ref
  217.0 57.3 %shard_map.271 = (bf16[8,3,128,768]{3,2,1,0:T(8,128)(2,1)}, bf16[3,256,768]{2,1,0:T(8,128)(2,1)}, f32[3,256,768]{2,1,0:T(8,128)}, bf16[3,256,768]{2,1,0:T(8,128)...) custom-call(bf16[3,256,768]{2,1,0:T(8,128)(2,1)} %own_ref.3, ...), custom_call_target="tpu_custom_call" | custom-call | flops 9059696640 | bytes 30000000 | tf_op jit(solution)/shard_map/pallas_call | solution.py:681
  274.2 4.6 all-to-all-start
  279.3 49.9 %all-gather.12.cloned.1.call-done.wide_ref = bf16[768,4096]{1,0:T(8,128)(2,1)} async-done(((bf16[192,4096]{1,0:T(8,128)(2,1)}), bf16[768,4096]{1,0:T(8,128)(2,1)}) %all-gather.12.cloned.1.call-update) | async-done | bytes 6291472 | tf_op jit(solution)/shard_map/all_gather | solution.py:617
  329.2 30.0 %shard_map.272 = (f32[768,768]{1,0:T(8,128)}, bf16[768,768]{1,0:T(8,128)(2,1)}, bf16[768,2048]{1,0:T(8,128)(2,1)}, bf16[2,768,2048]{2,1,0:T(8,128)(2,1)}) custom-call(bf16[768,768]{1,0:T(8,128)(2,1)} %bitcast.36, bf16[768,768]{1,0:T(8,128)(2,1)} %bitcast.23, bf16[768,4096]{1,0:T(8,128)(2,1)} %all-gather.12.cloned.1.call-done.wide_ref, ...), custom_call_target="tpu_custom_call" | custom-call | flops 14495514624 | bytes 23592960 | tf_op jit(solution)/shard_map/pallas_call | solution.py:306
  359.7 14.6 %shard_map.278 = (bf16[2,768,2048]{2,1,0:T(8,128)(2,1)}, bf16[2048,768]{1,0:T(8,128)(2,1)}) custom-call(bf16[768,768]{1,0:T(8,128)(2,1)} %bitcast.37, bf16[768,768]{1,0:T(8,128)(2,1)} %bitcast.24, bf16[768,2048]{1,0:T(8,128)(2,1)} %get-tuple-element.63.hidden_ref, bf16[2,768,2048]{2,1,0:T(8,128)(2,1)} %get-tuple-element.64.dwide_ref, ...), custom_call_target="tpu_custom_call" | custom-call | flops 7247757312 | bytes 21233664 | tf_op jit(solution)/shard_map/pallas_call | solution.py:373
  375.1 71.9 %all-gather.16.cloned.1.call-done.wide_ref = bf16[768,4096]{1,0:T(8,128)(2,1)} async-done(((bf16[192,4096]{1,0:T(8,128)(2,1)}), bf16[768,4096]{1,0:T(8,128)(2,1)}) %all-gather.16.cloned.1.call-update) | async-done | bytes 6291472 | tf_op jit(solution)/shard_map/all_gather | solution.py:621
  447.1 96.0 %shard_map.274 = (bf16[3072,768]{1,0:T(8,128)(2,1)}, bf16[3072,768]{1,0:T(8,128)(2,1)}, bf16[3072,2048]{1,0:T(8,128)(2,1)}, bf16[2,3072,2048]{2,1,0:T(8,128)(2,1...) custom-call(bf16[3072,768]{1,0:T(8,128)(2,1)} %bitcast.5.rows_ref, bf16[3072,768]{1,0:T(8,128)(2,1)} %bitcast.6.cot_ref, ...), custom_call_target="tpu_custom_call" | custom-call | flops 57982058496 | bytes 66060288 | tf_op jit(solution)/shard_map/pallas_call | solution.py:306
  543.1 4.6 all-to-all-start.3
  547.7 40.4 %shard_map.276 = (bf16[2,768,2048]{2,1,0:T(8,128)(2,1)}, bf16[2048,768]{1,0:T(8,128)(2,1)}, f32[768,128]{1,0:T(8,128)}) custom-call(bf16[3072,768]{1,0:T(8,128)(2,1)} %bitcast.5.rows_ref, bf16[3072,768]{1,0:T(8,128)(2,1)} %get-tuple-element.54.cot_ref, bf16[3072,2048]{1,0:T(8,128)(2,1)} %get-tuple-element.55.hidden_ref, ...), custom_call_target="tpu_custom_call" | custom-call | flops 28991029248 | bytes 56623104 | tf_op jit(solution)/shard_map/pallas_call | solution.py:373
  588.1 64.9 %all-to-all-done.3.slots_ref = bf16[8,3,128,768]{3,2,1,0:T(8,128)(2,1)} async-done(((bf16[8,3,128,768]{3,2,1,0:T(8,128)(2,1)}), bf16[8,3,128,768]{3,2,1,0:T(8,128)(2,1)}, u32[]{:S(2)}, u32[]{:S(2)}) %all-to-all-start.3) | async-done | bytes 4718624 | tf_op jit(solution)/shard_map/all_to_all | solution.py:732
  653.0 80.2 %shard_map.277 = (f32[3,256,768]{2,1,0:T(8,128)}, f32[3,256,768]{2,1,0:T(8,128)}, bf16[3,1024,768]{2,1,0:T(8,128)(2,1)}, bf16[768,3200]{1,0:T(8,128)(2,1)}) custom-call(bf16[3,256,768]{2,1,0:T(8,128)(2,1)} %own_ref.3, bf16[3,1024,768]{2,1,0:T(8,128)(2,1)} %slice.61.prompt_ref, s32[3,2,256]{2,1,0:T(2,128)} %bitcast.29, ...), custom_call_target="tpu_custom_call" | custom-call | flops 18119393280 | bytes 40000000 | tf_op jit(solution)/shard_map/pallas_call | solution.py:736
  734.7 55.3 %reduce-scatter.9.cloned.1.call-done = bf16[192,3200]{1,0:T(8,128)(2,1)} async-done(((bf16[768,3200]{1,0:T(8,128)(2,1)}), bf16[192,3200]{1,0:T(8,128)(2,1)}) %reduce-scatter.9.cloned.1.call-update) | async-done | bytes 1228816 | tf_op jit(solution)/shard_map/reduce_scatter | solution.py:820
  790.1 6.6 pad.9
  796.7 4.9 all-to-all-start.2
  802.0 34.8 %reduce-scatter.17.cloned.1.call-done = bf16[512,768]{1,0:T(8,128)(2,1)} async-done(((bf16[2048,768]{1,0:T(8,128)(2,1)}), bf16[512,768]{1,0:T(8,128)(2,1)}) %reduce-scatter.17.cloned.1.call-update) | async-done | bytes 786448 | tf_op jit(solution)/shard_map/reduce_scatter | solution.py:820
  839.1 67.7 %all-to-all-done.2.slots_ref = bf16[8,3,128,768]{3,2,1,0:T(8,128)(2,1)} async-done(((bf16[8,3,128,768]{3,2,1,0:T(8,128)(2,1)}), bf16[8,3,128,768]{3,2,1,0:T(8,128)(2,1)}, u32[]{:S(2)}, u32[]{:S(2)}) %all-to-all-start.2) | async-done | bytes 4718624 | tf_op jit(solution)/shard_map/all_to_all | solution.py:733
  906.9 7.1 shard_map.275
  917.3 80.3 %all-reduce.5.cloned.1.call-done = (bf16[192,3200]{1,0:T(8,128)(2,1)}, bf16[2,192,2048]{2,1,0:T(8,128)(2,1)}, bf16[512,768]{1,0:T(8,128)(2,1)}) async-done(((bf16[192,3200]{1,0:T(8,128)(2,1)}, bf16[2,192,2048]{2,1,0:T(8,128)(2,1)}, bf16[512,768]{1,0:T(8,128)(2,1)}), (bf16[192,3200]{1,0:T(8,128)(2,1)}, bf16[2,192,2048]{2,1,0:T(8,128)(2,1)}, bf16[512,768]{1,0:T(8,128)(2,1)})) %all-reduce.5.cloned.1.call-update) | async-done | bytes 3588112 | tf_op jit(solution)/shard_map/psum | solution.py:826
  1011.2 88.3 %reduce-scatter.7.cloned.1.call-done = bf16[3,256,768]{2,1,0:T(8,128)(2,1)} async-done(((bf16[3,2048,768]{2,1,0:T(8,128)(2,1)}), bf16[3,256,768]{2,1,0:T(8,128)(2,1)}) %reduce-scatter.7.cloned.1.call-update) | async-done | bytes 1179664 | tf_op jit(solution)/shard_map/reduce_scatter | solution.py:809
  (106 shorter events, 50.0 us)
Async XLA Ops:
  7.2 68.8 %all-gather.10.cloned.1.call-start = ((), (), s32[]{:S(2)}) async-start(), calls=%async_computation.11 | async-start | bytes 6144000 | tf_op jit(solution)/shard_map/all_gather | solution.py:610
  11.3 4.7 copy-start.9
  14.5 197.6 %all-gather.8.cloned.1.call-start = ((), (), s32[]{:S(2)}) async-start(), calls=%async_computation.10 | async-start | bytes 10616832 | tf_op jit(solution)/shard_map/all_gather | solution.py:616
  15.3 264.0 %all-gather.14.cloned.1.call-start = ((), (), s32[]{:S(2)}) async-start(), calls=%async_computation.13 | async-start | bytes 3932160 | tf_op jit(solution)/shard_map/all_gather | solution.py:620
  16.0 313.1 %all-gather.12.cloned.1.call-start = ((), (), s32[]{:S(2)}) async-start(), calls=%async_computation.12 | async-start | bytes 7864320 | tf_op jit(solution)/shard_map/all_gather | solution.py:617
  17.4 357.7 %all-gather.18.cloned.1.call-start = ((), (), s32[]{:S(2)}) async-start(), calls=%async_computation.21 | async-start | bytes 3932160 | tf_op jit(solution)/shard_map/all_gather | solution.py:624
  22.9 6.5 copy-start.11
  23.0 6.5 copy-start.12
  23.0 251.3 %all-to-all-start.1 = ((bf16[8,3,128,768]{3,2,1,0:T(8,128)(2,1)}), bf16[8,3,128,768]{3,2,1,0:T(8,128)(2,1)}, u32[]{:S(2)}, u32[]{:S(2)}) async-start(bf16[8,3,128,768]{3,2,1,0:T(8,128)(2,1)} %shard_map.273), calls=%async_computation.1 | async-start | bytes 9437184 | tf_op jit(solution)/shard_map/all_to_all | solution.py:664
  29.4 417.6 %all-gather.16.cloned.1.call-start = ((), (), s32[]{:S(2)}) async-start(), calls=%async_computation.14 | async-start | bytes 7864320 | tf_op jit(solution)/shard_map/all_gather | solution.py:621
  274.2 172.8 %all-to-all-start = ((bf16[8,3,128,768]{3,2,1,0:T(8,128)(2,1)}), bf16[8,3,128,768]{3,2,1,0:T(8,128)(2,1)}, u32[]{:S(2)}, u32[]{:S(2)}) async-start(bf16[8,3,128,768]{3,2,1,0:T(8,128)(2,1)} %get-tuple-element.45), calls=%async_computation | async-start | bytes 9437184 | tf_op jit(solution)/shard_map/all_to_all | solution.py:717
  278.9 455.8 %reduce-scatter.13.cloned.1.call-start = ((), (), s32[]{:S(2)}) async-start(), calls=%async_computation.18 | async-start | bytes 3932160 | tf_op jit(solution)/shard_map/reduce_scatter | solution.py:820
  374.4 360.3 %reduce-scatter.11.cloned.1.call-start = ((), (), s32[]{:S(2)}) async-start(), calls=%async_computation.17 | async-start | bytes 7864320 | tf_op jit(solution)/shard_map/reduce_scatter | solution.py:820
  543.1 109.9 %all-to-all-start.3 = ((bf16[8,3,128,768]{3,2,1,0:T(8,128)(2,1)}), bf16[8,3,128,768]{3,2,1,0:T(8,128)(2,1)}, u32[]{:S(2)}, u32[]{:S(2)}) async-start(bf16[8,3,128,768]{3,2,1,0:T(8,128)(2,1)} %bitcast.21), calls=%async_computation.3 | async-start | bytes 9437184 | tf_op jit(solution)/shard_map/all_to_all | solution.py:732
  547.7 242.3 %reduce-scatter.9.cloned.1.call-start = ((), (), s32[]{:S(2)}) async-start(), calls=%async_computation.16 | async-start | bytes 6144000 | tf_op jit(solution)/shard_map/reduce_scatter | solution.py:820
  733.3 103.5 %reduce-scatter.17.cloned.1.call-start = ((), (), s32[]{:S(2)}) async-start(), calls=%async_computation.20 | async-start | bytes 3932160 | tf_op jit(solution)/shard_map/reduce_scatter | solution.py:820
  733.9 180.1 %reduce-scatter.15.cloned.1.call-start = ((), (), s32[]{:S(2)}) async-start(), calls=%async_computation.19 | async-start | bytes 7864320 | tf_op jit(solution)/shard_map/reduce_scatter | solution.py:820
  734.6 263.1 %all-reduce.5.cloned.1.call-start = ((), (), s32[]{:S(2)}) async-start(), calls=%async_computation.22 | async-start | bytes 7176192 | tf_op jit(solution)/shard_map/psum | solution.py:826
  790.0 309.4 %reduce-scatter.7.cloned.1.call-start = ((), (), s32[]{:S(2)}) async-start(), calls=%async_computation.15 | async-start | bytes 10616832 | tf_op jit(solution)/shard_map/reduce_scatter | solution.py:809
  796.7 5.0 copy-start
  796.7 5.3 copy-start.14
  796.7 110.2 %all-to-all-start.2 = ((bf16[8,3,128,768]{3,2,1,0:T(8,128)(2,1)}), bf16[8,3,128,768]{3,2,1,0:T(8,128)(2,1)}, u32[]{:S(2)}, u32[]{:S(2)}) async-start(bf16[8,3,128,768]{3,2,1,0:T(8,128)(2,1)} %bitcast.20), calls=%async_computation.2 | async-start | bytes 9437184 | tf_op jit(solution)/shard_map/all_to_all | solution.py:733
  1009.3 90.2 %copy-start.1 = (bf16[3,256,768]{2,1,0:T(8,128)(2,1)S(1)}, bf16[3,256,768]{2,1,0:T(8,128)(2,1)}, u32[]{:S(2)}) copy-start(bf16[3,256,768]{2,1,0:T(8,128)(2,1)} %own_ref.3) | copy-start | bytes 3538948
  1009.3 90.2 %copy-start.4 = (f32[3,256,768]{2,1,0:T(8,128)S(1)}, f32[3,256,768]{2,1,0:T(8,128)}, u32[]{:S(2)}) copy-start(f32[3,256,768]{2,1,0:T(8,128)} %get-tuple-element.60) | copy-start | bytes 7077892
  (8 other events, 21.2 us)
Sparse Core Ops, SparseCore 0:
  14.7 61.2 all-gather.9
  77.6 134.4 all-gather.7
  214.0 42.7 all-gather.13
  259.1 70.0 all-gather.11
  330.8 43.8 all-gather.17
  377.0 70.0 all-gather.15
  450.0 43.8 reduce-scatter.12
  497.0 70.0 reduce-scatter.10
  733.4 56.5 reduce-scatter.8
  792.8 43.8 reduce-scatter.16
  839.8 70.0 reduce-scatter.14
  912.3 85.3 all-reduce.4
  999.9 99.4 reduce-scatter.6

commit v3 on v2

--- a/solution.py
+++ b/solution.py
@@ -569,6 +569,441 @@
     ).astype(low)
 
 
+def chip_place():
+    me = lax.axis_index("expert")
+    return me // 2, me % 2
+
+
+def remote(source, target, send, recv, place):
+    return pltpu.make_async_remote_copy(
+        src_ref=source,
+        dst_ref=target,
+        send_sem=send,
+        recv_sem=recv,
+        device_id=place,
+        device_id_type=pl.DeviceIdType.MESH,
+    )
+
+
+class Chain:
+    def __init__(self, source, target, chips, holders, sems):
+        self.source, self.target = source, target
+        self.chips, self.holders = chips, holders
+        self.send, self.recv, self.give, self.take, self.local = sems
+        self.z, self.core = chip_place()
+        self.batches, self.tok = source.shape[:2]
+
+    @staticmethod
+    def scratch(chips, batches):
+        return [pltpu.SemaphoreType.DMA((2, chips, batches)) for _ in range(4)] + [
+            pltpu.SemaphoreType.DMA((batches,))
+        ]
+
+    def view(self, chip, core, m):
+        at = pl.multiple_of((2 * chip + core) * self.tok, self.tok)
+        return self.target.at[m, pl.ds(at, self.tok), :]
+
+    def hop(self, source, chip, m, way, d):
+        to = self.z + 1 if way == 0 else self.z - 1
+        return remote(
+            source,
+            self.view(chip, self.core, m),
+            self.send.at[way, d, m],
+            self.recv.at[way, d + 1, m],
+            {"expert": 2 * to + self.core},
+        )
+
+    def share(self, source, chip, m, way, d):
+        return remote(
+            source,
+            self.view(chip, self.core, m),
+            self.give.at[way, d, m],
+            self.take.at[way, d, m],
+            {"expert": 2 * self.z + 1 - self.core},
+        )
+
+    def onward(self, way):
+        return self.z + 1 < self.chips if way == 0 else self.z > 0
+
+    def keep(self, m):
+        return pltpu.make_async_copy(
+            self.source.at[m], self.view(self.z, self.core, m), self.local.at[m]
+        )
+
+    def begin(self):
+        @pl.when(self.z < self.holders)
+        def _():
+            for m in range(self.batches):
+                for way in range(2):
+
+                    @pl.when(self.onward(way))
+                    def _():
+                        self.hop(self.source.at[m], self.z, m, way, 0).start()
+
+                self.share(self.source.at[m], self.z, m, 0, 0).start()
+                self.keep(m).start()
+
+    def cases(self, d):
+        below, above = self.z - d, self.z + d
+        return (
+            (0, below, (below >= 0) & (below < self.holders)),
+            (1, above, above < self.holders),
+        )
+
+    def step(self, d):
+        for m in range(self.batches):
+            for way, chip, there in self.cases(d):
+
+                @pl.when(there)
+                def _():
+                    block = self.view(chip, self.core, m)
+                    remote(
+                        block,
+                        block,
+                        self.send.at[way, d, m],
+                        self.recv.at[way, d, m],
+                        {"expert": 2 * self.z + 1 - self.core},
+                    ).wait_recv()
+                    if d + 1 < self.chips:
+
+                        @pl.when(self.onward(way))
+                        def _():
+                            self.hop(block, chip, m, way, d).start()
+
+                    self.share(block, chip, m, way, d).start()
+
+    def finish(self):
+        @pl.when(self.z < self.holders)
+        def _():
+            for m in range(self.batches):
+                for way in range(2):
+
+                    @pl.when(self.onward(way))
+                    def _():
+                        self.hop(self.source.at[m], self.z, m, way, 0).wait_send()
+
+                self.share(self.source.at[m], self.z, m, 0, 0).wait_send()
+                other = self.view(self.z, 1 - self.core, m)
+                remote(
+                    other,
+                    other,
+                    self.give.at[0, 0, m],
+                    self.take.at[0, 0, m],
+                    {"expert": 2 * self.z + 1 - self.core},
+                ).wait_recv()
+                self.keep(m).wait()
+
+        for d in range(1, self.chips):
+            for m in range(self.batches):
+                for way, chip, there in self.cases(d):
+
+                    @pl.when(there)
+                    def _():
+                        block = self.view(chip, self.core, m)
+                        if d + 1 < self.chips:
+
+                            @pl.when(self.onward(way))
+                            def _():
+                                self.hop(block, chip, m, way, d).wait_send()
+
+                        self.share(block, chip, m, way, d).wait_send()
+                        other = self.view(chip, 1 - self.core, m)
+                        remote(
+                            other,
+                            other,
+                            self.give.at[way, d, m],
+                            self.take.at[way, d, m],
+                            {"expert": 2 * self.z + 1 - self.core},
+                        ).wait_recv()
+
+
+def meet(group, rows):
+    barrier = pltpu.get_barrier_semaphore()
+    me = lax.axis_index("expert")
+    for k in range(1, group):
+        pl.semaphore_signal(
+            barrier,
+            inc=1,
+            device_id={"expert": lax.rem(me + k, group)},
+            device_id_type=pl.DeviceIdType.MESH,
+        )
+    here = lax.axis_index("dp")
+    for k in range(1, rows):
+        pl.semaphore_signal(
+            barrier,
+            inc=1,
+            device_id={"dp": lax.rem(here + k, rows)},
+            device_id_type=pl.DeviceIdType.MESH,
+        )
+    pl.semaphore_wait(barrier, group - 1 + rows - 1)
+
+
+def open_kernel(
+    group,
+    parts,
+    holders,
+    tokens_ref,
+    route_ref,
+    weight_ref,
+    prompt_ref,
+    routes_ref,
+    whole_ref,
+    *sems,
+):
+    chain_sems, (wsend, wrecv, wgive, wtake, rsend, rrecv, local) = sems[:5], sems[5:]
+    chain = Chain(tokens_ref, prompt_ref, group // 2, holders, chain_sems)
+    me, here = lax.axis_index("expert"), lax.axis_index("dp")
+    rows = weight_ref.shape[0]
+    shared = rows % 32 == 0
+    part = rows // 2 if shared else rows
+    offset = chain.core * part if shared else 0
+    partner = {"expert": 2 * chain.z + 1 - chain.core}
+
+    def piece(owner, core):
+        at = owner * rows + (core * part if shared else 0)
+        return whole_ref.at[pl.ds(pl.multiple_of(at, part), part), :]
+
+    def spread(k):
+        return remote(
+            weight_ref.at[pl.ds(pl.multiple_of(offset, part), part), :],
+            piece(here, chain.core),
+            wsend.at[k],
+            wrecv.at[k],
+            {"dp": lax.rem(here + k, parts)},
+        )
+
+    def routed(k):
+        return remote(
+            route_ref,
+            routes_ref.at[me],
+            rsend.at[k],
+            rrecv.at[k],
+            {"expert": lax.rem(me + k, group)},
+        )
+
+    def from_behind(k):
+        return lax.rem(here + parts - k, parts)
+
+    def handed(k, core):
+        block = piece(from_behind(k), core)
+        return remote(block, block, wgive.at[k], wtake.at[k], partner)
+
+    keep_weights = pltpu.make_async_copy(
+        weight_ref, whole_ref.at[pl.ds(pl.multiple_of(here * rows, rows), rows), :], local.at[0]
+    )
+    keep_routes = pltpu.make_async_copy(route_ref, routes_ref.at[me], local.at[1])
+
+    meet(group, parts)
+    chain.begin()
+    for k in range(1, parts):
+        spread(k).start()
+    for k in range(1, group):
+        routed(k).start()
+    keep_weights.start()
+    keep_routes.start()
+
+    def pass_weights(k):
+        block = piece(from_behind(k), chain.core)
+        remote(block, block, wsend.at[k], wrecv.at[k], partner).wait_recv()
+        if shared:
+            handed(k, chain.core).start()
+
+    chain.step(1)
+    for k in range(1, parts):
+        pass_weights(k)
+    for d in range(2, group // 2):
+        chain.step(d)
+    for k in range(1, parts):
+        spread(k).wait_send()
+        if shared:
+            handed(k, chain.core).wait_send()
+            handed(k, 1 - chain.core).wait_recv()
+    for k in range(1, group):
+        routed(k).wait_send()
+        came = routes_ref.at[lax.rem(me + group - k, group)]
+        remote(came, came, rsend.at[k], rrecv.at[k], partner).wait_recv()
+    keep_weights.wait()
+    keep_routes.wait()
+    chain.finish()
+
+
+def vmem():
+    return pl.BlockSpec(memory_space=pltpu.VMEM)
+
+
+def in_place():
+    return pl.BlockSpec(memory_space=pl.ANY)
+
+
+def open_gather(tokens, route_rows, weight_rows, group, parts, holders):
+    batches, tok, width = tokens.shape
+    rows, columns = weight_rows.shape
+    dma = pltpu.SemaphoreType.DMA
+    return pl.pallas_call(
+        functools.partial(open_kernel, group, parts, holders // 2),
+        in_specs=[vmem(), vmem(), vmem()],
+        out_specs=[in_place(), in_place(), in_place()],
+        out_shape=[
+            jax.ShapeDtypeStruct((batches, holders * tok, width), low),
+            jax.ShapeDtypeStruct((group,) + route_rows.shape, route_rows.dtype),
+            jax.ShapeDtypeStruct((parts * rows, columns), low),
+        ],
+        scratch_shapes=Chain.scratch(group // 2, batches)
+        + [dma((parts,))] * 4
+        + [dma((group,))] * 2
+        + [dma((2,))],
+        compiler_params=pltpu.CompilerParams(
+            collective_id=0, has_side_effects=True, vmem_limit_bytes=24_000_000
+        ),
+    )(tokens, route_rows, weight_rows)
+
+
+def spread_kernel(group, parts, rows_ref, all_ref, *sems):
+    chips = group // 2
+    chain = Chain(rows_ref, all_ref, chips, chips, sems)
+    meet(group, 1)
+    chain.begin()
+    for d in range(1, chips):
+        chain.step(d)
+    chain.finish()
+
+
+def spread_rows(rows, group):
+    batches, tok, width = rows.shape
+    return pl.pallas_call(
+        functools.partial(spread_kernel, group, 1),
+        in_specs=[vmem()],
+        out_specs=in_place(),
+        out_shape=jax.ShapeDtypeStruct((batches, group * tok, width), low),
+        scratch_shapes=Chain.scratch(group // 2, batches),
+        compiler_params=pltpu.CompilerParams(
+            collective_id=1, has_side_effects=True, vmem_limit_bytes=24_000_000
+        ),
+    )(rows)
+
+
+def collect_kernel(group, holders, part_ref, sum_ref, take, above, below, acc, *sems):
+    give_s, take_s, send_s, above_s, below_s = sems
+    chips = group // 2
+    z, core = chip_place()
+    batches = part_ref.shape[0]
+    tok = sum_ref.shape[1]
+    partner = {"expert": 2 * z + 1 - core}
+    chunks = [(m, chip) for chip in range(holders) for m in range(batches)]
+
+    def mine(m, chip, owner):
+        at = pl.multiple_of((2 * chip + owner) * tok, tok)
+        return part_ref.at[m, pl.ds(at, tok), :]
+
+    def give(m, chip):
+        return remote(
+            mine(m, chip, 1 - core),
+            take.at[chip, m],
+            give_s.at[chip, m],
+            take_s.at[chip, m],
+            partner,
+        )
+
+    def down(m, chip):
+        return remote(
+            acc.at[chip, m],
+            above.at[chip, m],
+            send_s.at[chip, m],
+            above_s.at[chip, m],
+            {"expert": 2 * (z - 1) + core},
+        )
+
+    def up(m, chip):
+        return remote(
+            acc.at[chip, m],
+            below.at[chip, m],
+            send_s.at[chip, m],
+            below_s.at[chip, m],
+            {"expert": 2 * (z + 1) + core},
+        )
+
+    def here(m, chip, sem):
+        return remote(
+            acc.at[chip, m], take.at[chip, m], send_s.at[chip, m], sem.at[chip, m], partner
+        )
+
+    meet(group, 1)
+    for m, chip in chunks:
+        give(m, chip).start()
+
+    @pl.when(z >= holders)
+    def _():
+        sum_ref[...] = jnp.zeros_like(sum_ref)
+
+    def add(m, chip, waits):
+        here(m, chip, take_s).wait_recv()
+        acc[chip, m] = (
+            mine(m, chip, core)[...].astype(f32) + take[chip, m].astype(f32)
+        ).astype(low)
+        for there, sem, came in waits:
+
+            @pl.when(there)
+            def _():
+                here(m, chip, sem).wait_recv()
+                acc[chip, m] = (acc[chip, m].astype(f32) + came[chip, m].astype(f32)).astype(low)
+
+    def stream(chip, onward, waits):
+        for m in range(batches):
+            add(m, chip, waits)
+            if m:
+                onward(m - 1, chip).start()
+        last = batches - 1
+        onward(last - 1, chip).wait_send()
+        onward(last, chip).start()
+
+    from_above = (z + 1 < chips, above_s, above)
+    from_below = (z > 0, below_s, below)
+    for chip in reversed(range(holders)):
+
+        @pl.when(z < chip)
+        def _():
+            stream(chip, up, [from_below])
+
+    for chip in range(holders):
+
+        @pl.when(z > chip)
+        def _():
+            stream(chip, down, [from_above])
+
+    for chip in range(holders):
+
+        @pl.when(z == chip)
+        def _():
+            for m in range(batches):
+                add(m, chip, [from_above, from_below])
+                sum_ref[m] = acc[chip, m]
+
+    for m, chip in chunks:
+        give(m, chip).wait_send()
+
+        if m != batches - 2:
+
+            @pl.when(z != chip)
+            def _():
+                here(m, chip, take_s).wait_send()
+
+
+def collect_rows(part, group, holders, tok):
+    batches, _, width = part.shape
+    chips = holders // 2
+    block = pltpu.VMEM((chips, batches, tok, width), low)
+    return pl.pallas_call(
+        functools.partial(collect_kernel, group, chips),
+        in_specs=[vmem()],
+        out_specs=vmem(),
+        out_shape=jax.ShapeDtypeStruct((batches, tok, width), low),
+        scratch_shapes=[block] * 4 + [pltpu.SemaphoreType.DMA((chips, batches))] * 5,
+        compiler_params=pltpu.CompilerParams(
+            collective_id=2, has_side_effects=True, vmem_limit_bytes=40_000_000
+        ),
+    )(part)
+
+
 def rotary(positions):
     middle = HD // 2
     frequency = jnp.exp(jnp.arange(middle).astype(f32) * (-2.0 * math.log(10000.0) / HD))
@@ -607,13 +1042,17 @@
 
     small = jnp.concatenate([attn_norm[:, None], ffn_norm[:, None], router_weight], axis=1)
     small = jnp.pad(small, ((0, 0), (0, LANES - small.shape[1])))
-    attn_all = lax.all_gather(
+    group, parts = lax.axis_size("expert"), lax.axis_size("dp")
+    route_rows = jnp.swapaxes(routes, 1, 2)
+    prompt, routes_all, attn_all = open_gather(
+        tokens,
+        route_rows,
         jnp.concatenate([query_weight, key_weight, value_weight, out_weight, small], axis=1),
-        "dp",
-        axis=0,
-        tiled=True,
-    )
-    prompt = lax.all_gather(tokens, "expert", axis=1, tiled=True)[:, :PROMPT]
+        group,
+        parts,
+        holders,
+    )
+    prompt, cot_rows = lax.optimization_barrier((prompt, cotangent))
     shared_wide = lax.all_gather(
         jnp.concatenate([shared_gate, shared_up], axis=1), "dp", axis=0, tiled=True
     )
@@ -633,7 +1072,6 @@
             ((lane >= ROUTER_AT) & (lane < ROUTER_AT + experts)).astype(f32),
         ]
     )
-    route_rows = jnp.swapaxes(routes, 1, 2)
 
     row_at = jnp.arange(tok, dtype=jnp.int32)
     query_pos = me * tok + row_at
@@ -657,10 +1095,11 @@
         out_specs=slots_spec,
         out_shape=jax.ShapeDtypeStruct(slots_shape, low),
         compiler_params=params(),
-    )(cotangent, route_rows)
+    )(cot_rows, route_rows)
     exchange = functools.partial(
         lax.all_to_all, axis_name="expert", split_axis=0, concat_axis=0, tiled=True
     )
+    prompt, cot_sent = lax.optimization_barrier((prompt, cot_sent))
     cot_slots = exchange(cot_sent)
 
     total = PROMPT + tok
@@ -714,6 +1153,7 @@
         ),
     )(tokens, prompt, route_rows, attn_all, gains, *tables)
 
+    sent, cot_slots = lax.optimization_barrier((sent, cot_slots))
     received = exchange(sent)
 
     flat = (batches * tok, width)
@@ -722,6 +1162,14 @@
     )
     gshared_wide, gshared_deep = mlp_weights(
         mixed.reshape(flat), cotangent.reshape(flat), shared_hidden, shared_dwide, None
+    )
+
+
+    def scatter(value, dimension):
+        return lax.psum_scatter(value, "dp", scatter_dimension=dimension, tiled=True)
+
+    gshared_wide, gshared_deep = lax.psum(
+        (scatter(gshared_wide, 1), scatter(gshared_deep, 0)), "expert"
     )
 
     slots_flat = (experts * batches * capacity, width)
@@ -730,8 +1178,13 @@
         slot_rows, cot_slots.reshape(slots_flat), expert_wide, expert_deep, router, onehot, True
     )
     dx_back = exchange(expert_dx.reshape(slots_shape))
+    dx_back, expert_y, gshared_wide, gshared_deep = lax.optimization_barrier(
+        (dx_back, expert_y, gshared_wide, gshared_deep)
+    )
     y_back = exchange(expert_y.reshape(slots_shape))
     gexpert_wide, gexpert_deep, grouter = mlp_weights(slot_rows, dout, hidden, dwide, dlogit)
+    gexpert_deep = scatter(gexpert_deep, 0)
+    gexpert_wide = scatter(gexpert_wide, 1)
 
     dres, dnorm_own, dprompt, gattn = pl.pallas_call(
         functools.partial(attend_back_kernel, experts, capacity),
@@ -796,6 +1249,12 @@
         grouter,
     )
 
+    gattn, gexpert_deep, gexpert_wide = lax.optimization_barrier(
+        (gattn, gexpert_deep, gexpert_wide)
+    )
+    gattn = lax.psum(scatter(gattn, 0), "expert").astype(f32)
+    dprompt, y_back = lax.optimization_barrier((dprompt, y_back))
+    dnorm_prompt = collect_rows(dprompt, group, holders, tok)
     output = pl.pallas_call(
         functools.partial(finish_kernel, experts, capacity),
         grid=(batches,),
@@ -805,8 +1264,6 @@
         compiler_params=params(),
     )(resid, shared_y.reshape(rows_shape), y_back, route_rows)
 
-    padded = jnp.pad(dprompt, ((0, 0), (0, (experts - holders) * tok), (0, 0)))
-    dnorm_prompt = lax.psum_scatter(padded, "expert", scatter_dimension=1, tiled=True)
     dnorm = dnorm_own + dnorm_prompt.astype(f32)
     own = tokens.astype(f32)
     inverse = inverse_rms(own)
@@ -816,14 +1273,8 @@
         dres + inverse * (scaled - hat * jnp.mean(scaled * hat, axis=-1, keepdims=True))
     ).astype(low)
 
-    def scatter(value, dimension):
-        return lax.psum_scatter(value, "dp", scatter_dimension=dimension, tiled=True)
-
-    gexpert_wide = scatter(gexpert_wide, 1).astype(f32)
-    gexpert_deep = scatter(gexpert_deep, 0).astype(f32)
-    gshared_wide = lax.psum(scatter(gshared_wide, 1), "expert").astype(f32)
-    gshared_deep = lax.psum(scatter(gshared_deep, 0), "expert").astype(f32)
-    gattn = lax.psum(scatter(gattn, 0), "expert").astype(f32)
+    gexpert_wide, gexpert_deep = gexpert_wide.astype(f32), gexpert_deep.astype(f32)
+    gshared_wide, gshared_deep = gshared_wide.astype(f32), gshared_deep.astype(f32)
     at = 4 * width
     return (
         output,

time: 1120 us -> 946 us (0.84)
  waiting for transfers between devices: 687 us -> 387 us
  Pallas kernels: 331 us -> 446 us
  starting transfers between devices: 21.5 us -> 42.6 us
    all_gather x2 -> x0, waiting for transfers between devices: 170 us -> none  [the longest x1 133 us: per_device(): prompt = lax.all_gather(tokens, 'expert', axis=1, tiled=True)[:, :PROMPT]]
    pallas_call x0 -> x2, Pallas kernels: none -> 114 us  [the longest x1 67.4 us: collect_rows(): pl.pallas_call(functools.partial(collect_kernel, group, chips), in_specs=...]
    reduce_scatter x5, waiting for transfers between devices: 90.1 us -> 0.08 us  [scatter(): lax.psum_scatter(value, 'dp', scatter_dimension=dimension, tiled=True)]
    reduce_scatter x1 -> x0, waiting for transfers between devices: 88.3 us -> none  [per_device(): lax.psum_scatter(padded, 'expert', scatter_dimension=1, tiled=True)]
    all_to_all x1, waiting for transfers between devices: 0.01 us -> 64.5 us  [per_device(): received = exchange(sent)]
    all_gather x1, waiting for transfers between devices: 49.9 us -> 0.02 us  [per_device(): lax.all_gather(jnp.concatenate([shared_gate, shared_up], axis=1), 'dp', a...]
    psum x0 -> x1, waiting for transfers between devices: none -> 49.1 us  [per_device(): lax.psum((scatter(gshared_wide, 1), scatter(gshared_deep, 0)), 'expert')]
    all_gather x1, waiting for transfers between devices: 71.9 us -> 40.2 us  [per_device(): lax.all_gather(jnp.concatenate([expert_gate[0], expert_up[0]], axis=1), '...]
  transfers between devices with their start and end apart: 17 -> 15, of which waited for: 10 -> 6; matrix products, arithmetic and copies ran while one was open for 4% -> 4% of each run, Pallas kernels for 30% -> 47%
where the time goes in v3:
time: 946 us; the launch traced here: 942 us
  Pallas kernels  446 us (47%)
  waiting for transfers between devices  387 us (41%)
  starting transfers between devices  42.6 us (5%)
  local copies, waits for them, and re-layouts  27 us (3%)
  other arithmetic  25.1 us (3%)
  between operations  14.6 us (2%)
    pallas_call x2, Pallas kernels, mlp(): pl.pallas_call(functools.partial(mlp_kernel, gated), grid=(count // tile,...  127 us
    all_to_all x1, waiting for transfers between devices, per_device(): y_back = exchange(expert_y.reshape(slots_shape))  96.5 us
    pallas_call x1, Pallas kernels, per_device(): pl.pallas_call(functools.partial(attend_back_kernel, experts, capacity),...  80.7 us
    all_to_all x1, waiting for transfers between devices, per_device(): dx_back = exchange(expert_dx.reshape(slots_shape))  71.1 us
    pallas_call x1, Pallas kernels, collect_rows(): pl.pallas_call(functools.partial(collect_kernel, group, chips), in_specs=...  67.4 us
    all_to_all x1, waiting for transfers between devices, per_device(): received = exchange(sent)  64.5 us
    psum x1, waiting for transfers between devices, per_device(): gattn = lax.psum(scatter(gattn, 0), 'expert').astype(f32)  62.9 us
    pallas_call x1, Pallas kernels, per_device(): pl.pallas_call(functools.partial(attend_kernel, experts, capacity), grid=...  56.7 us
  transfers between devices with their start and end apart: 15, of which 6 were waited for; matrix products, arithmetic and copies ran while one was open for 4% of the time, Pallas kernels for 47%

profile of v3, /device:TPU:0, one launch (start us, length us, event | category | flops | bytes accessed | tf_op | source)
XLA Modules:
  0.0 942.4 jit_solution(8025122689896153015)
XLA Ops:
  8.0 2.8 pad_maximum_fusion
  14.3 46.8 %shard_map.271 = (bf16[3,1024,768]{2,1,0:T(8,128)(2,1)S(1)}, s32[8,3,2,256]{3,2,1,0:T(2,128)}, bf16[768,3200]{1,0:T(8,128)(2,1)S(1)}) custom-call(bf16[3,256,768]{2,1,0:T(8,128)(2,1)S(1)} %copy-done, s32[3,2,256]{2,1,0:T(2,128)S(1)} %bitcast.25, bf16[192,3200]{1,0:T(8,128)(2,1)S(1)} %pad_dynamic-update-slice_fusion.weight_ref), custom_call_target="tpu_custom_call" | custom-call | tf_op jit(solution)/shard_map/pallas_call | solution.py:842
  65.4 4.9 shard_map.272
  70.3 27.4 %all-to-all-start = ((bf16[8,3,128,768]{3,2,1,0:T(8,128)(2,1)}), bf16[8,3,128,768]{3,2,1,0:T(8,128)(2,1)}, u32[]{:S(2)}, u32[]{:S(2)}) async-start(bf16[8,3,128,768]{3,2,1,0:T(8,128)(2,1)} %shard_map.272), calls=%async_computation | async-start | bytes 9437184 | tf_op jit(solution)/shard_map/all_to_all | solution.py:1103
  97.9 7.4 copy.43
  116.0 56.7 %shard_map.273 = (bf16[8,3,128,768]{3,2,1,0:T(8,128)(2,1)}, bf16[3,256,768]{2,1,0:T(8,128)(2,1)}, f32[3,256,768]{2,1,0:T(8,128)}, bf16[3,256,768]{2,1,0:T(8,128)...) custom-call(bf16[3,256,768]{2,1,0:T(8,128)(2,1)} %own_ref.3, ...), custom_call_target="tpu_custom_call" | custom-call | flops 9059696640 | bytes 30000000 | tf_op jit(solution)/shard_map/pallas_call | solution.py:1120
  172.8 30.8 %shard_map.274 = (f32[768,768]{1,0:T(8,128)}, bf16[768,768]{1,0:T(8,128)(2,1)}, bf16[768,2048]{1,0:T(8,128)(2,1)}, bf16[2,768,2048]{2,1,0:T(8,128)(2,1)}) custom-call(bf16[768,768]{1,0:T(8,128)(2,1)} %bitcast.35, bf16[768,768]{1,0:T(8,128)(2,1)} %bitcast.29, bf16[768,4096]{1,0:T(8,128)(2,1)} %all-gather.6.cloned.1.call-done.wide_ref, ...), custom_call_target="tpu_custom_call" | custom-call | flops 14495514624 | bytes 23592960 | tf_op jit(solution)/shard_map/pallas_call | solution.py:306
  204.2 15.1 %shard_map.276 = (bf16[2,768,2048]{2,1,0:T(8,128)(2,1)}, bf16[2048,768]{1,0:T(8,128)(2,1)}) custom-call(bf16[768,768]{1,0:T(8,128)(2,1)} %bitcast.36, bf16[768,768]{1,0:T(8,128)(2,1)} %bitcast.30, bf16[768,2048]{1,0:T(8,128)(2,1)} %get-tuple-element.79.hidden_ref, bf16[2,768,2048]{2,1,0:T(8,128)(2,1)} %get-tuple-element.80.dwide_ref, ...), custom_call_target="tpu_custom_call" | custom-call | flops 7247757312 | bytes 21233664 | tf_op jit(solution)/shard_map/pallas_call | solution.py:373
  219.3 5.1 all-to-all-start.1
  225.0 40.2 %all-gather.10.cloned.1.call-done.wide_ref = bf16[768,4096]{1,0:T(8,128)(2,1)} async-done(((bf16[192,4096]{1,0:T(8,128)(2,1)}), bf16[768,4096]{1,0:T(8,128)(2,1)}) %all-gather.10.cloned.1.call-update) | async-done | bytes 6291472 | tf_op jit(solution)/shard_map/all_gather | solution.py:1060
  265.1 64.5 %all-to-all-done.1 = bf16[8,3,128,768]{3,2,1,0:T(8,128)(2,1)} async-done(((bf16[8,3,128,768]{3,2,1,0:T(8,128)(2,1)}), bf16[8,3,128,768]{3,2,1,0:T(8,128)(2,1)}, u32[]{:S(2)}, u32[]{:S(2)}) %all-to-all-start.1) | async-done | bytes 4718624 | tf_op jit(solution)/shard_map/all_to_all | solution.py:1157
  329.6 96.1 %shard_map.275 = (bf16[3072,768]{1,0:T(8,128)(2,1)}, bf16[3072,768]{1,0:T(8,128)(2,1)}, bf16[3072,2048]{1,0:T(8,128)(2,1)}, bf16[2,3072,2048]{2,1,0:T(8,128)(2,1...) custom-call(bf16[3072,768]{1,0:T(8,128)(2,1)} %bitcast.6.rows_ref, bf16[3072,768]{1,0:T(8,128)(2,1)} %bitcast.7.cot_ref, ...), custom_call_target="tpu_custom_call" | custom-call | flops 57982058496 | bytes 66060288 | tf_op jit(solution)/shard_map/pallas_call | solution.py:306
  425.8 40.6 %shard_map.277 = (bf16[2,768,2048]{2,1,0:T(8,128)(2,1)}, bf16[2048,768]{1,0:T(8,128)(2,1)}, f32[768,128]{1,0:T(8,128)}) custom-call(bf16[3072,768]{1,0:T(8,128)(2,1)} %bitcast.6.rows_ref, bf16[3072,768]{1,0:T(8,128)(2,1)} %get-tuple-element.84.cot_ref, bf16[3072,2048]{1,0:T(8,128)(2,1)} %get-tuple-element.85.hidden_ref, ...), custom_call_target="tpu_custom_call" | custom-call | flops 28991029248 | bytes 56623104 | tf_op jit(solution)/shard_map/pallas_call | solution.py:373
  467.2 4.6 all-to-all-start.2
  471.8 49.1 %all-reduce.7.cloned.1.call-done = (bf16[2,192,2048]{2,1,0:T(8,128)(2,1)}, bf16[512,768]{1,0:T(8,128)(2,1)}) async-done(((bf16[2,192,2048]{2,1,0:T(8,128)(2,1)}, bf16[512,768]{1,0:T(8,128)(2,1)}), (bf16[2,192,2048]{2,1,0:T(8,128)(2,1)}, bf16[512,768]{1,0:T(8,128)(2,1)})) %all-reduce.7.cloned.1.call-update) | async-done | bytes 2359312 | tf_op jit(solution)/shard_map/psum | solution.py:1171
  520.9 71.1 %all-to-all-done.2.slots_ref = bf16[8,3,128,768]{3,2,1,0:T(8,128)(2,1)} async-done(((bf16[8,3,128,768]{3,2,1,0:T(8,128)(2,1)}), bf16[8,3,128,768]{3,2,1,0:T(8,128)(2,1)}, u32[]{:S(2)}, u32[]{:S(2)}) %all-to-all-start.2) | async-done | bytes 4718624 | tf_op jit(solution)/shard_map/all_to_all | solution.py:1180
  592.0 80.7 %shard_map.278 = (f32[3,256,768]{2,1,0:T(8,128)}, f32[3,256,768]{2,1,0:T(8,128)}, bf16[3,1024,768]{2,1,0:T(8,128)(2,1)}, bf16[768,3200]{1,0:T(8,128)(2,1)}) custom-call(bf16[3,256,768]{2,1,0:T(8,128)(2,1)} %own_ref.3, bf16[3,1024,768]{2,1,0:T(8,128)(2,1)} %copy-done.8, s32[3,2,256]{2,1,0:T(2,128)} %bitcast.23, bf16[768,3200]{1,0:T(8,128)(2,1)} %copy-done.5, ...), custom_call_target="tpu_custom_call" | custom-call | flops 18119393280 | bytes 40000000 | tf_op jit(solution)/shard_map/pallas_call | solution.py:1189
  672.8 4.9 all-to-all-start.3
  686.4 96.5 %all-to-all-done.3.slots_ref = bf16[8,3,128,768]{3,2,1,0:T(8,128)(2,1)} async-done(((bf16[8,3,128,768]{3,2,1,0:T(8,128)(2,1)}), bf16[8,3,128,768]{3,2,1,0:T(8,128)(2,1)}, u32[]{:S(2)}, u32[]{:S(2)}) %all-to-all-start.3) | async-done | bytes 4718624 | tf_op jit(solution)/shard_map/all_to_all | solution.py:1184
  785.3 67.4 %shard_map.280 = bf16[3,256,768]{2,1,0:T(8,128)(2,1)S(1)} custom-call(bf16[3,1024,768]{2,1,0:T(8,128)(2,1)S(1)} %copy-done.6), custom_call_target="tpu_custom_call" | custom-call | tf_op jit(solution)/shard_map/pallas_call | solution.py:995
  853.7 7.1 shard_map.279
  860.8 3.2 fusion.2
  864.0 4.1 fusion.6
  868.2 62.9 %all-reduce.5.cloned.1.call-done = bf16[192,3200]{1,0:T(8,128)(2,1)} async-done(((bf16[192,3200]{1,0:T(8,128)(2,1)}), bf16[192,3200]{1,0:T(8,128)(2,1)}) %all-reduce.5.cloned.1.call-update) | async-done | bytes 1228816 | tf_op jit(solution)/shard_map/psum | solution.py:1255
  (118 shorter events, 38.0 us)
Async XLA Ops:
  7.2 165.6 %all-gather.8.cloned.1.call-start = ((), (), s32[]{:S(2)}) async-start(), calls=%async_computation.10 | async-start | bytes 3932160 | tf_op jit(solution)/shard_map/all_gather | solution.py:1059
  7.9 3.6 copy-start.12
  7.9 3.6 copy-start.13
  7.9 164.8 %all-gather.6.cloned.1.call-start = ((), (), s32[]{:S(2)}) async-start(), calls=%async_computation.9 | async-start | bytes 7864320 | tf_op jit(solution)/shard_map/all_gather | solution.py:1056
  10.8 214.2 %all-gather.12.cloned.1.call-start = ((), (), s32[]{:S(2)}) async-start(), calls=%async_computation.18 | async-start | bytes 3932160 | tf_op jit(solution)/shard_map/all_gather | solution.py:1063
  11.5 253.6 %all-gather.10.cloned.1.call-start = ((), (), s32[]{:S(2)}) async-start(), calls=%async_computation.11 | async-start | bytes 7864320 | tf_op jit(solution)/shard_map/all_gather | solution.py:1060
  70.3 148.9 %all-to-all-start = ((bf16[8,3,128,768]{3,2,1,0:T(8,128)(2,1)}), bf16[8,3,128,768]{3,2,1,0:T(8,128)(2,1)}, u32[]{:S(2)}, u32[]{:S(2)}) async-start(bf16[8,3,128,768]{3,2,1,0:T(8,128)(2,1)} %shard_map.272), calls=%async_computation | async-start | bytes 9437184 | tf_op jit(solution)/shard_map/all_to_all | solution.py:1103
  97.7 328.1 %reduce-scatter.8.cloned.1.call-start = ((), (), s32[]{:S(2)}) async-start(), calls=%async_computation.13 | async-start | bytes 3932160 | tf_op jit(solution)/shard_map/reduce_scatter | solution.py:1169
  219.3 110.4 %all-to-all-start.1 = ((bf16[8,3,128,768]{3,2,1,0:T(8,128)(2,1)}), bf16[8,3,128,768]{3,2,1,0:T(8,128)(2,1)}, u32[]{:S(2)}, u32[]{:S(2)}) async-start(bf16[8,3,128,768]{3,2,1,0:T(8,128)(2,1)} %get-tuple-element.75), calls=%async_computation.1 | async-start | bytes 9437184 | tf_op jit(solution)/shard_map/all_to_all | solution.py:1157
  224.3 201.4 %reduce-scatter.6.cloned.1.call-start = ((), (), s32[]{:S(2)}) async-start(), calls=%async_computation.12 | async-start | bytes 7864320 | tf_op jit(solution)/shard_map/reduce_scatter | solution.py:1169
  224.9 296.0 %all-reduce.7.cloned.1.call-start = ((), (), s32[]{:S(2)}) async-start(), calls=%async_computation.19 | async-start | bytes 4718592 | tf_op jit(solution)/shard_map/psum | solution.py:1171
  425.8 246.9 %reduce-scatter.10.cloned.1.call-start = ((), (), s32[]{:S(2)}) async-start(), calls=%async_computation.14 | async-start | bytes 3932160 | tf_op jit(solution)/shard_map/reduce_scatter | solution.py:1169
  466.4 206.3 %reduce-scatter.12.cloned.1.call-start = ((), (), s32[]{:S(2)}) async-start(), calls=%async_computation.15 | async-start | bytes 7864320 | tf_op jit(solution)/shard_map/reduce_scatter | solution.py:1169
  467.2 124.9 %all-to-all-start.2 = ((bf16[8,3,128,768]{3,2,1,0:T(8,128)(2,1)}), bf16[8,3,128,768]{3,2,1,0:T(8,128)(2,1)}, u32[]{:S(2)}, u32[]{:S(2)}) async-start(bf16[8,3,128,768]{3,2,1,0:T(8,128)(2,1)} %bitcast.27), calls=%async_computation.2 | async-start | bytes 9437184 | tf_op jit(solution)/shard_map/all_to_all | solution.py:1180
  471.8 392.2 %reduce-scatter.14.cloned.1.call-start = ((), (), s32[]{:S(2)}) async-start(), calls=%async_computation.16 | async-start | bytes 6144000 | tf_op jit(solution)/shard_map/reduce_scatter | solution.py:1169
  672.8 5.0 copy-start.20
  672.8 5.0 copy-start.1
  672.8 5.3 copy-start.11
  672.8 110.1 %all-to-all-start.3 = ((bf16[8,3,128,768]{3,2,1,0:T(8,128)(2,1)}), bf16[8,3,128,768]{3,2,1,0:T(8,128)(2,1)}, u32[]{:S(2)}, u32[]{:S(2)}) async-start(bf16[8,3,128,768]{3,2,1,0:T(8,128)(2,1)} %bitcast.26), calls=%async_computation.5 | async-start | bytes 9437184 | tf_op jit(solution)/shard_map/all_to_all | solution.py:1184
  677.7 253.4 %all-reduce.5.cloned.1.call-start = ((), (), s32[]{:S(2)}) async-start(), calls=%async_computation.17 | async-start | bytes 2457600 | tf_op jit(solution)/shard_map/psum | solution.py:1255
  782.9 2.3 copy-start.6
  860.8 3.2 copy-start.2
  860.8 3.2 copy-start.4
  931.1 2.3 copy-start.9
  (15 other events, 22.9 us)
Sparse Core Ops, SparseCore 0:
  9.8 64.6 all-gather.7
  77.0 70.0 all-gather.5
  148.9 43.8 all-gather.11
  195.1 70.0 all-gather.9
  268.0 43.8 reduce-scatter.7
  314.8 70.0 reduce-scatter.5
  425.9 94.9 all-reduce.6
  523.9 55.3 reduce-scatter.9
  582.3 70.0 reduce-scatter.11
  672.9 56.7 reduce-scatter.13
  864.1 66.9 all-reduce.4

commit v4 on v3

--- a/solution.py
+++ b/solution.py
@@ -21,6 +21,7 @@
 low = jnp.bfloat16
 f32 = jnp.float32
 VMEM_LIMIT = 66_000_000
+LIGHT = pl.CostEstimate(flops=1, bytes_accessed=1, transcendentals=0)
 
 
 def mm(a, b):
@@ -206,23 +207,18 @@
 
 
 def mlp_kernel(
-    gated,
     rows_ref,
     cot_ref,
     wide_ref,
     deep_ref,
-    router_ref,
-    onehot_ref,
     y_ref,
     dx_ref,
     hidden_ref,
     dwide_ref,
-    *rest,
+    gate_s,
+    up_s,
+    acc,
 ):
-    if gated:
-        dout_ref, dlogit_ref, gate_s, up_s, acc = rest
-    else:
-        gate_s, up_s, acc = rest
     ff = deep_ref.shape[0]
     tile = 512
     rows = rows_ref[...]
@@ -237,27 +233,9 @@
         return carry
 
     lax.fori_loop(0, ff // tile, forward, 0)
-    result = mm(hidden_ref[...], deep_ref[...])
+    y_ref[...] = mm(hidden_ref[...], deep_ref[...])
     cot = cot_ref[...]
-    if gated:
-        result = result.astype(low).astype(f32)
-        valid = onehot_ref[1:2, :]
-        chosen = onehot_ref[0:1, :]
-        logits = jnp.where(valid > 0.5, mm(rows, router_ref[...]), neg_large)
-        logits = jnp.exp(logits - jnp.max(logits, axis=-1, keepdims=True))
-        probs = logits / jnp.sum(logits, axis=-1, keepdims=True)
-        gate_value = jnp.sum(probs * chosen, axis=-1, keepdims=True)
-        cot32 = cot.astype(f32)
-        gate_grad = jnp.sum(cot32 * result, axis=-1, keepdims=True)
-        dlogit = (probs * (chosen - gate_value) * gate_grad).astype(low)
-        dlogit_ref[...] = dlogit
-        y_ref[...] = (gate_value * result).astype(y_ref.dtype)
-        cot = (gate_value * cot32).astype(low)
-        dout_ref[...] = cot
-        acc[...] = mm_nt(dlogit, router_ref[...])
-    else:
-        y_ref[...] = result.astype(y_ref.dtype)
-        acc[...] = jnp.zeros_like(acc)
+    acc[...] = jnp.zeros_like(acc)
 
     def backward(j, carry):
         at = pl.multiple_of(j * tile, tile)
@@ -276,120 +254,80 @@
         return carry
 
     lax.fori_loop(0, ff // tile, backward, 0)
-    dx_ref[...] = acc[...].astype(dx_ref.dtype)
-
-
-def mlp(rows, cot, wide, deep, router, onehot, gated):
+    dx_ref[...] = acc[...].astype(low)
+
+
+def mlp(rows, cot, wide, deep):
     count, width = rows.shape
     ff = deep.shape[0]
     tile = math.gcd(count, 512)
     by_row = lambda last: pl.BlockSpec((tile, last), lambda m: (m, 0))
-    kept = f32 if not gated else low
-    out_shape = [
-        jax.ShapeDtypeStruct((count, width), kept),
-        jax.ShapeDtypeStruct((count, width), low),
-        jax.ShapeDtypeStruct((count, ff), low),
-        jax.ShapeDtypeStruct((2, count, ff), low),
-    ]
-    out_specs = [
-        by_row(width),
-        by_row(width),
-        by_row(ff),
-        pl.BlockSpec((2, tile, ff), lambda m: (0, m, 0)),
-    ]
-    if gated:
-        out_shape += [
-            jax.ShapeDtypeStruct((count, width), low),
-            jax.ShapeDtypeStruct((count, LANES), low),
-        ]
-        out_specs += [by_row(width), by_row(LANES)]
     return pl.pallas_call(
-        functools.partial(mlp_kernel, gated),
+        mlp_kernel,
         grid=(count // tile,),
-        in_specs=[
+        in_specs=[by_row(width), by_row(width), whole((width, 2 * ff)), whole((ff, width))],
+        out_specs=[
             by_row(width),
             by_row(width),
-            whole((width, 2 * ff)),
-            whole((ff, width)),
-            whole((width, LANES)),
-            whole((2, LANES)),
+            by_row(ff),
+            pl.BlockSpec((2, tile, ff), lambda m: (0, m, 0)),
         ],
-        out_specs=out_specs,
-        out_shape=out_shape,
+        out_shape=[
+            jax.ShapeDtypeStruct((count, width), f32),
+            jax.ShapeDtypeStruct((count, width), low),
+            jax.ShapeDtypeStruct((count, ff), low),
+            jax.ShapeDtypeStruct((2, count, ff), low),
+        ],
         scratch_shapes=[
             pltpu.VMEM((tile, ff), f32),
             pltpu.VMEM((tile, ff), f32),
             pltpu.VMEM((tile, width), f32),
         ],
         compiler_params=params(),
-        cost_estimate=pl.CostEstimate(
-            flops=12 * count * width * ff,
-            bytes_accessed=2 * (3 * width * ff + 4 * count * width + 3 * count * ff),
-            transcendentals=2 * count * ff,
-        ),
-    )(rows, cot, wide, deep, router, onehot)
+        cost_estimate=LIGHT,
+    )(rows, cot, wide, deep)
 
 
 def mlp_weights_kernel(
-    routed, rows_ref, cot_ref, hidden_ref, dwide_ref, dlogit_ref, gwide_ref, gdeep_ref, *rest
+    rows_ref, cot_ref, hidden_ref, dwide_ref, gwide_ref, gdeep_ref, rows_t, cot_t
 ):
-    if routed:
-        grouter_ref, rows_t, cot_t = rest
-    else:
-        rows_t, cot_t = rest
-
     @pl.when(pl.program_id(0) == 0)
     def _():
-        step = 256
+        step = math.gcd(rows_ref.shape[0], 256)
         for r in range(0, rows_ref.shape[0], step):
             rows_t[:, r : r + step] = rows_ref[r : r + step, :].T
             cot_t[:, r : r + step] = cot_ref[r : r + step, :].T
-        if routed:
-            grouter_ref[...] = mm(rows_t[...], dlogit_ref[...])
 
     gwide_ref[0] = mm(rows_t[...], dwide_ref[0]).astype(low)
     gwide_ref[1] = mm(rows_t[...], dwide_ref[1]).astype(low)
     gdeep_ref[...] = mm(cot_t[...], hidden_ref[...]).T.astype(low)
 
 
-def mlp_weights(rows, cot, hidden, dwide, dlogit):
+def mlp_weights(rows, cot, hidden, dwide):
     count, width = rows.shape
     ff = hidden.shape[1]
     tile = 256
-    routed = dlogit is not None
-    if not routed:
-        dlogit = jnp.zeros((8, LANES), low)
-    out_shape = [
-        jax.ShapeDtypeStruct((2, width, ff), low),
-        jax.ShapeDtypeStruct((ff, width), low),
-    ]
-    out_specs = [
-        pl.BlockSpec((2, width, tile), lambda j: (0, 0, j)),
-        pl.BlockSpec((tile, width), lambda j: (j, 0)),
-    ]
-    if routed:
-        out_shape.append(jax.ShapeDtypeStruct((width, LANES), f32))
-        out_specs.append(whole((width, LANES)))
     return pl.pallas_call(
-        functools.partial(mlp_weights_kernel, routed),
+        mlp_weights_kernel,
         grid=(ff // tile,),
         in_specs=[
             whole((count, width)),
             whole((count, width)),
             pl.BlockSpec((count, tile), lambda j: (0, j)),
             pl.BlockSpec((2, count, tile), lambda j: (0, 0, j)),
-            whole(dlogit.shape),
         ],
-        out_specs=out_specs,
-        out_shape=out_shape,
+        out_specs=[
+            pl.BlockSpec((2, width, tile), lambda j: (0, 0, j)),
+            pl.BlockSpec((tile, width), lambda j: (j, 0)),
+        ],
+        out_shape=[
+            jax.ShapeDtypeStruct((2, width, ff), low),
+            jax.ShapeDtypeStruct((ff, width), low),
+        ],
         scratch_shapes=[pltpu.VMEM((width, count), low), pltpu.VMEM((width, count), low)],
         compiler_params=params(),
-        cost_estimate=pl.CostEstimate(
-            flops=6 * count * width * ff,
-            bytes_accessed=2 * (3 * width * ff + 2 * count * width + 3 * count * ff),
-            transcendentals=0,
-        ),
-    )(rows, cot, hidden, dwide, dlogit)
+        cost_estimate=LIGHT,
+    )(rows, cot, hidden, dwide)
 
 
 def attend_back_kernel(
@@ -1004,6 +942,286 @@
     )(part)
 
 
+def opposite(me, k, group):
+    other, digit = me, 1
+    while digit < group:
+        other = other + lax.rem(k // digit, 2) * (1 - 2 * lax.rem(me // digit, 2)) * digit
+        digit *= 2
+    return other
+
+
+def expert_kernel(
+    group,
+    sent_ref,
+    cot_hbm,
+    wide_ref,
+    deep_ref,
+    router_ref,
+    onehot_ref,
+    y_hbm,
+    back_hbm,
+    gwide_hbm,
+    gdeep_hbm,
+    grouter_ref,
+    came,
+    cots,
+    ys,
+    dxs,
+    gate_s,
+    up_s,
+    hidden_s,
+    dwide_s,
+    acc,
+    rows_t,
+    dout_t,
+    gwide,
+    gdeep_t,
+    wide_out,
+    deep_out,
+    send_s,
+    recv_s,
+    cot_s,
+    y_s,
+    bsend_s,
+    brecv_s,
+    flush_s,
+    local,
+):
+    me = lax.axis_index("expert")
+    batches, slots, width = came.shape[1:]
+    count = batches * slots
+    ff = deep_ref.shape[0]
+    tile = 512
+
+    def there(k):
+        return {"expert": opposite(me, k, group)}
+
+    def going(k):
+        return remote(
+            sent_ref.at[opposite(me, k, group)], came.at[k], send_s.at[k], recv_s.at[k], there(k)
+        )
+
+    def returning(k):
+        return remote(dxs.at[k], back_hbm.at[me], bsend_s.at[k], brecv_s.at[k], there(k))
+
+    def returned(k):
+        block = back_hbm.at[opposite(me, k, group)]
+        return remote(block, block, bsend_s.at[k], brecv_s.at[k], there(k))
+
+    own_in = pltpu.make_async_copy(sent_ref.at[me], came.at[0], local.at[0])
+    own_out = pltpu.make_async_copy(dxs.at[0], back_hbm.at[me], local.at[1])
+
+    def cot_copy(k):
+        return pltpu.make_async_copy(
+            cot_hbm.at[opposite(me, k, group)], cots.at[lax.rem(k, 2)], cot_s.at[lax.rem(k, 2)]
+        )
+
+    def y_copy(k):
+        return pltpu.make_async_copy(
+            ys.at[lax.rem(k, 2)], y_hbm.at[opposite(me, k, group)], y_s.at[lax.rem(k, 2)]
+        )
+
+    meet(group, 1)
+    for k in range(1, group):
+        going(k).start()
+    own_in.start()
+    cot_copy(0).start()
+    gwide[...] = jnp.zeros_like(gwide)
+    gdeep_t[...] = jnp.zeros_like(gdeep_t)
+    grouter_ref[...] = jnp.zeros_like(grouter_ref)
+
+    def block(k, carry):
+        @pl.when(k == 0)
+        def _():
+            own_in.wait()
+
+        @pl.when(k > 0)
+        def _():
+            going(k).wait_recv()
+
+        cot_copy(k).wait()
+
+        @pl.when(k + 1 < group)
+        def _():
+            cot_copy(k + 1).start()
+
+        @pl.when(k >= 2)
+        def _():
+            y_copy(k - 2).wait()
+
+        rows = came[k].reshape(count, width)
+
+        def forward(j, carry):
+            at = pl.multiple_of(j * tile, tile)
+            gate = mm(rows, wide_ref[:, pl.ds(at, tile)])
+            up = mm(rows, wide_ref[:, pl.ds(pl.multiple_of(ff + at, tile), tile)])
+            gate_s[:, pl.ds(at, tile)] = gate
+            up_s[:, pl.ds(at, tile)] = up
+            hidden_s[:, pl.ds(at, tile)] = (gate * jax.nn.sigmoid(gate) * up).astype(low)
+            return carry
+
+        lax.fori_loop(0, ff // tile, forward, 0)
+        result = mm(hidden_s[...], deep_ref[...]).astype(low).astype(f32)
+        valid = onehot_ref[1:2, :]
+        chosen = onehot_ref[0:1, :]
+        logits = jnp.where(valid > 0.5, mm(rows, router_ref[...]), neg_large)
+        logits = jnp.exp(logits - jnp.max(logits, axis=-1, keepdims=True))
+        probs = logits / jnp.sum(logits, axis=-1, keepdims=True)
+        gate_value = jnp.sum(probs * chosen, axis=-1, keepdims=True)
+        cot32 = cots[lax.rem(k, 2)].reshape(count, width).astype(f32)
+        gate_grad = jnp.sum(cot32 * result, axis=-1, keepdims=True)
+        dlogit = (probs * (chosen - gate_value) * gate_grad).astype(low)
+        ys[lax.rem(k, 2)] = (gate_value * result).astype(low).reshape(batches, slots, width)
+        y_copy(k).start()
+        dout = gate_value * cot32
+        cot = dout.astype(low)
+        dout_t[...] = dout.T.astype(low)
+        rows_t[...] = rows.T
+        acc[...] = mm_nt(dlogit, router_ref[...])
+        grouter_ref[...] += mm(rows_t[...], dlogit)
+
+        def backward(j, carry):
+            at = pl.multiple_of(j * tile, tile)
+            also = pl.multiple_of(ff + at, tile)
+            dhidden = mm_nt(cot, deep_ref[pl.ds(at, tile), :])
+            gate = gate_s[:, pl.ds(at, tile)]
+            sigma = jax.nn.sigmoid(gate)
+            act = gate * sigma
+            dgate = (dhidden * up_s[:, pl.ds(at, tile)] * (sigma + act * (1.0 - sigma))).astype(low)
+            dup = (dhidden * act).astype(low)
+            dwide_s[:, pl.ds(at, tile)] = dgate
+            dwide_s[:, pl.ds(also, tile)] = dup
+            acc[...] += mm_nt(dgate, wide_ref[:, pl.ds(at, tile)]) + mm_nt(
+                dup, wide_ref[:, pl.ds(also, tile)]
+            )
+            return carry
+
+        lax.fori_loop(0, ff // tile, backward, 0)
+        dxs[k] = acc[...].astype(low).reshape(batches, slots, width)
+
+        def weights(j, carry):
+            at = pl.multiple_of(j * tile, tile)
+            also = pl.multiple_of(ff + at, tile)
+            gwide[:, pl.ds(at, tile)] += mm(rows_t[...], dwide_s[:, pl.ds(at, tile)])
+            gwide[:, pl.ds(also, tile)] += mm(rows_t[...], dwide_s[:, pl.ds(also, tile)])
+            gdeep_t[:, pl.ds(at, tile)] += mm(dout_t[...], hidden_s[:, pl.ds(at, tile)])
+            return carry
+
+        lax.fori_loop(0, ff // tile, weights, 0)
+
+        @pl.when(k == 0)
+        def _():
+            own_out.start()
+
+        @pl.when(k > 0)
+        def _():
+            returning(k).start()
+
+        return carry
+
+    lax.fori_loop(0, group, block, 0)
+
+    step = wide_out.shape[2]
+
+    def wide_copy(n):
+        slot = lax.rem(n, 2)
+        at = pl.multiple_of(lax.rem(n, ff // step) * step, step)
+        return pltpu.make_async_copy(
+            wide_out.at[slot], gwide_hbm.at[n // (ff // step), :, pl.ds(at, step)], flush_s.at[0, slot]
+        )
+
+    def deep_copy(n):
+        slot = lax.rem(n, 2)
+        at = pl.multiple_of(n * step, step)
+        return pltpu.make_async_copy(
+            deep_out.at[slot], gdeep_hbm.at[pl.ds(at, step), :], flush_s.at[1, slot]
+        )
+
+    def flush_wide(n, carry):
+        @pl.when(n >= 2)
+        def _():
+            wide_copy(n - 2).wait()
+
+        at = pl.multiple_of(n * step, step)
+        wide_out[lax.rem(n, 2)] = gwide[:, pl.ds(at, step)].astype(low)
+        wide_copy(n).start()
+        return carry
+
+    def flush_deep(n, carry):
+        @pl.when(n >= 2)
+        def _():
+            deep_copy(n - 2).wait()
+
+        at = pl.multiple_of(n * step, step)
+        deep_out[lax.rem(n, 2)] = gdeep_t[:, pl.ds(at, step)].T.astype(low)
+        deep_copy(n).start()
+        return carry
+
+    pieces = ff // step
+    lax.fori_loop(0, 2 * pieces, flush_wide, 0)
+    lax.fori_loop(0, pieces, flush_deep, 0)
+    for n in (2, 1):
+        wide_copy(2 * pieces - n).wait()
+        deep_copy(pieces - n).wait()
+        y_copy(group - n).wait()
+    own_out.wait()
+    for k in range(1, group):
+        going(k).wait_send()
+        returning(k).wait_send()
+        returned(k).wait_recv()
+
+
+def expert_layer(sent, cot_slots, wide, deep, router, onehot):
+    group, batches, slots, width = sent.shape
+    ff = deep.shape[0]
+    count = batches * slots
+    step = 256
+    dma = pltpu.SemaphoreType.DMA
+    slots_out = jax.ShapeDtypeStruct(sent.shape, low)
+    block = (batches, slots, width)
+    return pl.pallas_call(
+        functools.partial(expert_kernel, group),
+        in_specs=[in_place(), in_place(), vmem(), vmem(), vmem(), vmem()],
+        out_specs=[in_place(), in_place(), in_place(), in_place(), vmem()],
+        out_shape=[
+            slots_out,
+            slots_out,
+            jax.ShapeDtypeStruct((2, width, ff), low),
+            jax.ShapeDtypeStruct((ff, width), low),
+            jax.ShapeDtypeStruct((width, LANES), f32),
+        ],
+        scratch_shapes=[
+            pltpu.VMEM((group,) + block, low),
+            pltpu.VMEM((2,) + block, low),
+            pltpu.VMEM((2,) + block, low),
+            pltpu.VMEM((group,) + block, low),
+            pltpu.VMEM((count, ff), f32),
+            pltpu.VMEM((count, ff), f32),
+            pltpu.VMEM((count, ff), low),
+            pltpu.VMEM((count, 2 * ff), low),
+            pltpu.VMEM((count, width), f32),
+            pltpu.VMEM((width, count), low),
+            pltpu.VMEM((width, count), low),
+            pltpu.VMEM((width, 2 * ff), f32),
+            pltpu.VMEM((width, ff), f32),
+            pltpu.VMEM((2, width, step), low),
+            pltpu.VMEM((2, step, width), low),
+            dma((group,)),
+            dma((group,)),
+            dma((2,)),
+            dma((2,)),
+            dma((group,)),
+            dma((group,)),
+            dma((2, 2)),
+            dma((2,)),
+        ],
+        compiler_params=pltpu.CompilerParams(
+            collective_id=3, has_side_effects=True, vmem_limit_bytes=VMEM_LIMIT
+        ),
+        cost_estimate=LIGHT,
+    )(sent, cot_slots, wide, deep, router, onehot)
+
+
 def rotary(positions):
     middle = HD // 2
     frequency = jnp.exp(jnp.arange(middle).astype(f32) * (-2.0 * math.log(10000.0) / HD))
@@ -1062,7 +1280,7 @@
     )
     expert_deep = lax.all_gather(expert_down[0], "dp", axis=0, tiled=True)
 
-    small_all = attn_all[:, 4 * width :]
+    small_all = lax.optimization_barrier(attn_all[:, 4 * width :])
     gains = small_all[:, :ROUTER_AT].T.astype(f32)
     router = small_all
     lane = jnp.arange(LANES, dtype=jnp.int32)
@@ -1148,41 +1366,35 @@
             pltpu.VMEM((width, tok), f32),
         ],
         compiler_params=params(),
-        cost_estimate=pl.CostEstimate(
-            flops=batches * 12 * tok * width * total, bytes_accessed=30_000_000, transcendentals=0
-        ),
+        cost_estimate=LIGHT,
     )(tokens, prompt, route_rows, attn_all, gains, *tables)
 
-    sent, cot_slots = lax.optimization_barrier((sent, cot_slots))
-    received = exchange(sent)
 
     flat = (batches * tok, width)
     shared_y, shared_dx, shared_hidden, shared_dwide = mlp(
-        mixed.reshape(flat), cotangent.reshape(flat), shared_wide, shared_deep, router, onehot, False
-    )
+        mixed.reshape(flat), cotangent.reshape(flat), shared_wide, shared_deep
+    )
+    shared_hidden, cot_slots = lax.optimization_barrier((shared_hidden, cot_slots))
     gshared_wide, gshared_deep = mlp_weights(
-        mixed.reshape(flat), cotangent.reshape(flat), shared_hidden, shared_dwide, None
+        mixed.reshape(flat), cotangent.reshape(flat), shared_hidden, shared_dwide
     )
 
 
     def scatter(value, dimension):
         return lax.psum_scatter(value, "dp", scatter_dimension=dimension, tiled=True)
 
-    gshared_wide, gshared_deep = lax.psum(
-        (scatter(gshared_wide, 1), scatter(gshared_deep, 0)), "expert"
-    )
-
-    slots_flat = (experts * batches * capacity, width)
-    slot_rows = received.reshape(slots_flat)
-    expert_y, expert_dx, hidden, dwide, dout, dlogit = mlp(
-        slot_rows, cot_slots.reshape(slots_flat), expert_wide, expert_deep, router, onehot, True
-    )
-    dx_back = exchange(expert_dx.reshape(slots_shape))
+    gshared_wide, gshared_deep, expert_wide, expert_deep = lax.optimization_barrier(
+        (gshared_wide, gshared_deep, expert_wide, expert_deep)
+    )
+    gshared_wide, gshared_deep = scatter(gshared_wide, 1), scatter(gshared_deep, 0)
+    expert_y, dx_back, gexpert_wide, gexpert_deep, grouter = expert_layer(
+        sent, cot_slots, expert_wide, expert_deep, router, onehot
+    )
     dx_back, expert_y, gshared_wide, gshared_deep = lax.optimization_barrier(
         (dx_back, expert_y, gshared_wide, gshared_deep)
     )
-    y_back = exchange(expert_y.reshape(slots_shape))
-    gexpert_wide, gexpert_deep, grouter = mlp_weights(slot_rows, dout, hidden, dwide, dlogit)
+    gshared_wide, gshared_deep = lax.psum((gshared_wide, gshared_deep), "expert")
+    y_back = exchange(expert_y)
     gexpert_deep = scatter(gexpert_deep, 0)
     gexpert_wide = scatter(gexpert_wide, 1)
 
@@ -1227,9 +1439,7 @@
             pltpu.VMEM((LANES, width), f32),
         ],
         compiler_params=params(),
-        cost_estimate=pl.CostEstimate(
-            flops=batches * 24 * tok * width * total, bytes_accessed=40_000_000, transcendentals=0
-        ),
+        cost_estimate=LIGHT,
     )(
         tokens,
         prompt,
@@ -1249,12 +1459,17 @@
         grouter,
     )
 
-    gattn, gexpert_deep, gexpert_wide = lax.optimization_barrier(
-        (gattn, gexpert_deep, gexpert_wide)
+    gattn, gexpert_deep, gexpert_wide, gshared_wide, gshared_deep = lax.optimization_barrier(
+        (gattn, gexpert_deep, gexpert_wide, gshared_wide, gshared_deep)
     )
     gattn = lax.psum(scatter(gattn, 0), "expert").astype(f32)
     dprompt, y_back = lax.optimization_barrier((dprompt, y_back))
     dnorm_prompt = collect_rows(dprompt, group, holders, tok)
+    dnorm_prompt, gexpert_deep, gexpert_wide, gshared_wide, gshared_deep = (
+        lax.optimization_barrier(
+            (dnorm_prompt, gexpert_deep, gexpert_wide, gshared_wide, gshared_deep)
+        )
+    )
     output = pl.pallas_call(
         functools.partial(finish_kernel, experts, capacity),
         grid=(batches,),

time: 946 us -> 932 us (0.985)
  waiting for transfers between devices: 387 us -> 336 us
  Pallas kernels: 446 us -> 495 us
  starting transfers between devices: 42.6 us -> 32.7 us
    all_to_all x3 -> x1, waiting for transfers between devices: 232 us -> 105 us  [per_device(): y_back = exchange(expert_y)]
    reduce_scatter x5, waiting for transfers between devices: 0.08 us -> 58.5 us  [scatter(): lax.psum_scatter(value, 'dp', scatter_dimension=dimension, tiled=True)]
    pallas_call x4 -> x3, Pallas kernels: 183 us -> 232 us  [the longest x1 187 us: expert_layer(): pl.pallas_call(functools.partial(expert_kernel, group), in_specs=[in_plac...]
    psum x1, waiting for transfers between devices: 49.1 us -> 69.4 us  [per_device(): lax.psum((gshared_wide, gshared_deep), 'expert')]
    psum x1, waiting for transfers between devices: 62.9 us -> 51 us  [per_device(): gattn = lax.psum(scatter(gattn, 0), 'expert').astype(f32)]
    all_to_all x3 -> x1, starting transfers between devices: 14.5 us -> 4.74 us  [per_device(): y_back = exchange(expert_y)]
  transfers between devices with their start and end apart: 15 -> 13, of which waited for: 6 -> 6; matrix products, arithmetic and copies ran while one was open for 4% -> 4% of each run, Pallas kernels for 47% -> 53%
where the time goes in v4:
time: 932 us; the launch traced here: 928 us
  Pallas kernels  495 us (53%)
  waiting for transfers between devices  336 us (36%)
  starting transfers between devices  32.7 us (4%)
  local copies, waits for them, and re-layouts  28.7 us (3%)
  other arithmetic  21.2 us (2%)
  between operations  14.5 us (2%)
    pallas_call x1, Pallas kernels, expert_layer(): pl.pallas_call(functools.partial(expert_kernel, group), in_specs=[in_plac...  187 us
    all_to_all x1, waiting for transfers between devices, per_device(): y_back = exchange(expert_y)  105 us
    pallas_call x1, Pallas kernels, per_device(): pl.pallas_call(functools.partial(attend_back_kernel, experts, capacity),...  80.4 us
    psum x1, waiting for transfers between devices, per_device(): lax.psum((gshared_wide, gshared_deep), 'expert')  69.4 us
    pallas_call x1, Pallas kernels, collect_rows(): pl.pallas_call(functools.partial(collect_kernel, group, chips), in_specs=...  67.4 us
    reduce_scatter x5, waiting for transfers between devices, scatter(): lax.psum_scatter(value, 'dp', scatter_dimension=dimension, tiled=True)  58.5 us
    pallas_call x1, Pallas kernels, per_device(): pl.pallas_call(functools.partial(attend_kernel, experts, capacity), grid=...  56.8 us
    psum x1, waiting for transfers between devices, per_device(): gattn = lax.psum(scatter(gattn, 0), 'expert').astype(f32)  51 us
  transfers between devices with their start and end apart: 13, of which 6 were waited for; matrix products, arithmetic and copies ran while one was open for 4% of the time, Pallas kernels for 53%

profile of v4, /device:TPU:0, one launch (start us, length us, event | category | flops | bytes accessed | tf_op | source)
XLA Modules:
  0.0 928.3 jit_solution(5980639158851079163)
XLA Ops:
  8.0 2.8 pad_maximum_fusion
  14.3 46.8 %shard_map.271 = (bf16[3,1024,768]{2,1,0:T(8,128)(2,1)S(1)}, s32[8,3,2,256]{3,2,1,0:T(2,128)}, bf16[768,3200]{1,0:T(8,128)(2,1)S(1)}) custom-call(bf16[3,256,768]{2,1,0:T(8,128)(2,1)S(1)} %copy-done.1, s32[3,2,256]{2,1,0:T(2,128)S(1)} %bitcast.21, bf16[192,3200]{1,0:T(8,128)(2,1)S(1)} %pad_dynamic-update-slice_fusion.weight_ref), custom_call_target="tpu_custom_call" | custom-call | tf_op jit(solution)/shard_map/pallas_call | solution.py:780
  61.1 2.2 copy-done
  63.3 2.2 copy-done.3
  65.5 4.9 shard_map.272
  70.4 27.3 %all-to-all-start = ((bf16[8,3,128,768]{3,2,1,0:T(8,128)(2,1)}), bf16[8,3,128,768]{3,2,1,0:T(8,128)(2,1)}, u32[]{:S(2)}, u32[]{:S(2)}) async-start(bf16[8,3,128,768]{3,2,1,0:T(8,128)(2,1)} %shard_map.272), calls=%async_computation | async-start | bytes 9437184 | tf_op jit(solution)/shard_map/all_to_all | solution.py:1321
  97.9 7.5 copy.46
  114.1 56.8 %shard_map.273 = (bf16[8,3,128,768]{3,2,1,0:T(8,128)(2,1)}, bf16[3,256,768]{2,1,0:T(8,128)(2,1)}, f32[3,256,768]{2,1,0:T(8,128)}, bf16[3,256,768]{2,1,0:T(8,128)...) custom-call(bf16[3,256,768]{2,1,0:T(8,128)(2,1)} %own_ref.3, ...), custom_call_target="tpu_custom_call" | custom-call | flops 1 | bytes 1 | tf_op jit(solution)/shard_map/pallas_call | solution.py:1338
  170.9 30.7 %shard_map.274 = (f32[768,768]{1,0:T(8,128)}, bf16[768,768]{1,0:T(8,128)(2,1)}, bf16[768,2048]{1,0:T(8,128)(2,1)}, bf16[2,768,2048]{2,1,0:T(8,128)(2,1)}) custom-call(bf16[768,768]{1,0:T(8,128)(2,1)} %bitcast.24, bf16[768,768]{1,0:T(8,128)(2,1)} %bitcast.22, bf16[768,4096]{1,0:T(8,128)(2,1)} %all-gather.6.cloned.1.call-done.wide_ref, ...), custom_call_target="tpu_custom_call" | custom-call | flops 1 | bytes 1 | tf_op jit(solution)/shard_map/pallas_call | solution.py:265
  203.0 14.9 %shard_map.275 = (bf16[2,768,2048]{2,1,0:T(8,128)(2,1)}, bf16[2048,768]{1,0:T(8,128)(2,1)}) custom-call(bf16[768,768]{1,0:T(8,128)(2,1)} %bitcast.25, bf16[768,768]{1,0:T(8,128)(2,1)} %bitcast.23, bf16[768,2048]{1,0:T(8,128)(2,1)} %get-tuple-element.84.hidden_ref, bf16[2,768,2048]{2,1,0:T(8,128)(2,1)} %get-tuple-element.85.dwide_ref), custom_call_target="tpu_custom_call" | custom-call | flops 1 | bytes 1 | tf_op jit(solution)/shard_map/pallas_call | solution.py:310
  217.9 47.2 %all-gather.10.cloned.1.call-done.wide_ref = bf16[768,4096]{1,0:T(8,128)(2,1)} async-done(((bf16[192,4096]{1,0:T(8,128)(2,1)}), bf16[768,4096]{1,0:T(8,128)(2,1)}) %all-gather.10.cloned.1.call-update) | async-done | bytes 6291472 | tf_op jit(solution)/shard_map/all_gather | solution.py:1278
  267.2 186.5 %shard_map.276 = (bf16[8,3,128,768]{3,2,1,0:T(8,128)(2,1)}, bf16[8,3,128,768]{3,2,1,0:T(8,128)(2,1)}, bf16[2,768,2048]{2,1,0:T(8,128)(2,1)}, bf16[2048,768]{1,0:T(8,128)(2,1)}, f32[768,128]{1,0:T(8,128)}) custom-call(bf16[8,3,128,768]{3,2,1,0:T(8,128)(2,1)} %get-tuple-element.80.sent_ref, bf16[8,3,128,768]{3,2,1,0:T(8,128)(2,1)} %all-to-all-done.cot_hbm, ...), custom_call_target="tpu_custom_call" | custom-call | flops 1 | bytes 1 | tf_op jit(solution)/shard_map/pallas_call | solution.py:1182
  455.3 80.4 %shard_map.277 = (f32[3,256,768]{2,1,0:T(8,128)}, f32[3,256,768]{2,1,0:T(8,128)}, bf16[3,1024,768]{2,1,0:T(8,128)(2,1)}, bf16[768,3200]{1,0:T(8,128)(2,1)}) custom-call(bf16[3,256,768]{2,1,0:T(8,128)(2,1)} %own_ref.3, bf16[3,1024,768]{2,1,0:T(8,128)(2,1)} %copy-done.3, s32[3,2,256]{2,1,0:T(2,128)} %bitcast.19, bf16[768,3200]{1,0:T(8,128)(2,1)} %copy-done, ...), custom_call_target="tpu_custom_call" | custom-call | flops 1 | bytes 1 | tf_op jit(solution)/shard_map/pallas_call | solution.py:1401
  535.8 58.5 %reduce-scatter.12.cloned.1.call-done = bf16[2,192,2048]{2,1,0:T(8,128)(2,1)} async-done(((bf16[2,768,2048]{2,1,0:T(8,128)(2,1)}), bf16[2,192,2048]{2,1,0:T(8,128)(2,1)}) %reduce-scatter.12.cloned.1.call-update) | async-done | bytes 1572880 | tf_op jit(solution)/shard_map/reduce_scatter | solution.py:1384
  594.3 69.4 %all-reduce.7.cloned.1.call-done = (bf16[2,192,2048]{2,1,0:T(8,128)(2,1)}, bf16[512,768]{1,0:T(8,128)(2,1)}) async-done(((bf16[2,192,2048]{2,1,0:T(8,128)(2,1)}, bf16[512,768]{1,0:T(8,128)(2,1)}), (bf16[2,192,2048]{2,1,0:T(8,128)(2,1)}, bf16[512,768]{1,0:T(8,128)(2,1)})) %all-reduce.7.cloned.1.call-update) | async-done | bytes 2359312 | tf_op jit(solution)/shard_map/psum | solution.py:1396
  663.7 4.7 all-to-all-start.1
  668.9 104.8 %all-to-all-done.1.slots_ref = bf16[8,3,128,768]{3,2,1,0:T(8,128)(2,1)} async-done(((bf16[8,3,128,768]{3,2,1,0:T(8,128)(2,1)}), bf16[8,3,128,768]{3,2,1,0:T(8,128)(2,1)}, u32[]{:S(2)}, u32[]{:S(2)}) %all-to-all-start.1) | async-done | bytes 4718624 | tf_op jit(solution)/shard_map/all_to_all | solution.py:1397
  773.7 2.3 copy-done.4
  776.0 67.4 %shard_map.279 = bf16[3,256,768]{2,1,0:T(8,128)(2,1)S(1)} custom-call(bf16[3,1024,768]{2,1,0:T(8,128)(2,1)S(1)} %copy-done.4), custom_call_target="tpu_custom_call" | custom-call | tf_op jit(solution)/shard_map/pallas_call | solution.py:933
  846.9 2.0 fusion.17
  850.9 2.0 convert_element_type.106
  854.2 7.1 shard_map.278
  861.3 3.9 slice_bitcast_fusion
  865.2 51.0 %all-reduce.5.cloned.1.call-done = bf16[192,3200]{1,0:T(8,128)(2,1)} async-done(((bf16[192,3200]{1,0:T(8,128)(2,1)}), bf16[192,3200]{1,0:T(8,128)(2,1)}) %all-reduce.5.cloned.1.call-update) | async-done | bytes 1228816 | tf_op jit(solution)/shard_map/psum | solution.py:1465
  (111 shorter events, 30.4 us)
Async XLA Ops:
  7.2 163.7 %all-gather.8.cloned.1.call-start = ((), (), s32[]{:S(2)}) async-start(), calls=%async_computation.8 | async-start | bytes 3932160 | tf_op jit(solution)/shard_map/all_gather | solution.py:1277
  7.9 3.6 copy-start.11
  7.9 3.6 copy-start.12
  7.9 163.0 %all-gather.6.cloned.1.call-start = ((), (), s32[]{:S(2)}) async-start(), calls=%async_computation.7 | async-start | bytes 7864320 | tf_op jit(solution)/shard_map/all_gather | solution.py:1274
  10.8 207.2 %all-gather.12.cloned.1.call-start = ((), (), s32[]{:S(2)}) async-start(), calls=%async_computation.16 | async-start | bytes 3932160 | tf_op jit(solution)/shard_map/all_gather | solution.py:1281
  11.5 253.6 %all-gather.10.cloned.1.call-start = ((), (), s32[]{:S(2)}) async-start(), calls=%async_computation.9 | async-start | bytes 7864320 | tf_op jit(solution)/shard_map/all_gather | solution.py:1278
  61.1 2.2 copy-start
  63.3 2.2 copy-start.3
  70.4 132.7 %all-to-all-start = ((bf16[8,3,128,768]{3,2,1,0:T(8,128)(2,1)}), bf16[8,3,128,768]{3,2,1,0:T(8,128)(2,1)}, u32[]{:S(2)}, u32[]{:S(2)}) async-start(bf16[8,3,128,768]{3,2,1,0:T(8,128)(2,1)} %shard_map.272), calls=%async_computation | async-start | bytes 9437184 | tf_op jit(solution)/shard_map/all_to_all | solution.py:1321
  97.7 356.9 %reduce-scatter.8.cloned.1.call-start = ((), (), s32[]{:S(2)}) async-start(), calls=%async_computation.11 | async-start | bytes 3932160 | tf_op jit(solution)/shard_map/reduce_scatter | solution.py:1384
  265.2 189.4 %reduce-scatter.6.cloned.1.call-start = ((), (), s32[]{:S(2)}) async-start(), calls=%async_computation.10 | async-start | bytes 7864320 | tf_op jit(solution)/shard_map/reduce_scatter | solution.py:1384
  265.7 270.0 %reduce-scatter.10.cloned.1.call-start = ((), (), s32[]{:S(2)}) async-start(), calls=%async_computation.12 | async-start | bytes 3932160 | tf_op jit(solution)/shard_map/reduce_scatter | solution.py:1384
  453.8 140.5 %reduce-scatter.12.cloned.1.call-start = ((), (), s32[]{:S(2)}) async-start(), calls=%async_computation.13 | async-start | bytes 7864320 | tf_op jit(solution)/shard_map/reduce_scatter | solution.py:1384
  454.5 209.1 %all-reduce.7.cloned.1.call-start = ((), (), s32[]{:S(2)}) async-start(), calls=%async_computation.17 | async-start | bytes 4718592 | tf_op jit(solution)/shard_map/psum | solution.py:1396
  455.2 393.7 %reduce-scatter.14.cloned.1.call-start = ((), (), s32[]{:S(2)}) async-start(), calls=%async_computation.14 | async-start | bytes 6144000 | tf_op jit(solution)/shard_map/reduce_scatter | solution.py:1384
  663.7 4.8 copy-start.19
  663.7 4.8 copy-start.2
  663.7 110.0 %all-to-all-start.1 = ((bf16[8,3,128,768]{3,2,1,0:T(8,128)(2,1)}), bf16[8,3,128,768]{3,2,1,0:T(8,128)(2,1)}, u32[]{:S(2)}, u32[]{:S(2)}) async-start(bf16[8,3,128,768]{3,2,1,0:T(8,128)(2,1)} %get-tuple-element.97), calls=%async_computation.3 | async-start | bytes 9437184 | tf_op jit(solution)/shard_map/all_to_all | solution.py:1397
  668.4 247.8 %all-reduce.5.cloned.1.call-start = ((), (), s32[]{:S(2)}) async-start(), calls=%async_computation.15 | async-start | bytes 2457600 | tf_op jit(solution)/shard_map/psum | solution.py:1465
  773.7 2.3 copy-start.4
  776.0 67.4 %copy-start.7 = (f32[3,256,768]{2,1,0:T(8,128)S(1)}, f32[3,256,768]{2,1,0:T(8,128)}, u32[]{:S(2)}) copy-start(f32[3,256,768]{2,1,0:T(8,128)} %get-tuple-element.100) | copy-start | bytes 7077892
  846.9 2.1 copy-start.13
  850.9 2.0 copy-start.14
  916.2 3.9 copy-start.6
  (12 other events, 17.9 us)
Sparse Core Ops, SparseCore 0:
  9.8 64.6 all-gather.7
  77.0 70.0 all-gather.5
  148.9 43.8 all-gather.11
  195.0 70.0 all-gather.9
  268.0 43.8 reduce-scatter.7
  314.8 70.0 reduce-scatter.5
  453.9 67.3 reduce-scatter.9
  524.2 70.0 reduce-scatter.11
  596.7 66.8 all-reduce.6
  666.5 57.6 reduce-scatter.13
  849.1 67.0 all-reduce.4

commit v5 on v4

--- a/solution.py
+++ b/solution.py
@@ -108,13 +108,14 @@
     prompt_ref,
     route_ref,
     weight_ref,
-    gain_ref,
     cos_p,
     sin_p,
     cos_o,
     sin_o,
     bias_p,
     bias_o,
+    wide_rows,
+    deep_rows,
     sent_ref,
     mixed_ref,
     resid_ref,
@@ -123,11 +124,30 @@
     key_ref,
     value_ref,
     lse_ref,
+    gain_ref,
+    router_ref,
+    wide_all,
+    deep_all,
     normed_s,
     value_t,
     out_t,
+    *sems,
 ):
     tok, width = own_ref.shape[1:]
+    parts = wide_all.shape[0] // wide_rows.shape[0]
+    spreads = (
+        Spread(deep_rows, deep_all, parts, sems[:4]),
+        Spread(wide_rows, wide_all, parts, sems[4:]),
+    )
+
+    @pl.when(pl.program_id(0) == 0)
+    def _():
+        meet(experts, parts)
+        for spread in spreads:
+            spread.begin()
+        gain_ref[...] = weight_ref[:, 4 * width :].astype(f32).T[:8]
+        router_ref[...] = weight_ref[:, 4 * width :]
+
     gain_one = gain_ref[0:1, :]
     gain_two = gain_ref[1:2, :]
     step = 256
@@ -205,6 +225,13 @@
     for e in range(experts):
         sent_ref[e, 0] = mm(placement(ranks, e, capacity), mixed).astype(low)
 
+    @pl.when(pl.program_id(0) == pl.num_programs(0) - 1)
+    def _():
+        for spread in spreads:
+            spread.forward()
+        for spread in spreads:
+            spread.finish()
+
 
 def mlp_kernel(
     rows_ref,
@@ -354,10 +381,12 @@
     dmix_ref,
     slots_ref,
     grouter_ref,
+    y_hbm,
     dres_ref,
     down_ref,
     dprompt_ref,
     grads_ref,
+    home_hbm,
     normed_t,
     key_t,
     datt_s,
@@ -367,9 +396,27 @@
     dvalue_s,
     acc,
     small,
+    ysend_s,
+    yrecv_s,
+    local,
 ):
     tok, width = own_ref.shape[1:]
     total = PROMPT + tok
+    me = lax.axis_index("expert")
+
+    def homeward(k):
+        to = opposite(me, k, experts)
+        return remote(
+            y_hbm.at[to], home_hbm.at[me], ysend_s.at[k], yrecv_s.at[k], {"expert": to}
+        )
+
+    def arrived(k):
+        to = opposite(me, k, experts)
+        return remote(
+            home_hbm.at[to], home_hbm.at[to], ysend_s.at[k], yrecv_s.at[k], {"expert": to}
+        )
+
+    stays = pltpu.make_async_copy(y_hbm.at[me], home_hbm.at[me], local.at[0])
     gain_one = gain_ref[0:1, :]
     gain_two = gain_ref[1:2, :]
     step = 256
@@ -378,6 +425,10 @@
 
     @pl.when(first)
     def _():
+        meet(experts, 1)
+        stays.start()
+        for k in range(1, experts):
+            homeward(k).start()
         acc[...] = jnp.zeros_like(acc)
         small[...] = jnp.zeros_like(small)
 
@@ -498,6 +549,10 @@
         for j in range(0, 4 * width, step):
             grads_ref[:, j : j + step] = acc[:, j : j + step].astype(low)
         grads_ref[:, 4 * width :] = (small[...].T + grouter_ref[...]).astype(low)
+        stays.wait()
+        for k in range(1, experts):
+            homeward(k).wait_send()
+            arrived(k).wait_recv()
 
 
 def finish_kernel(experts, capacity, resid_ref, shared_ref, slots_ref, route_ref, out_ref):
@@ -674,6 +729,72 @@
             device_id_type=pl.DeviceIdType.MESH,
         )
     pl.semaphore_wait(barrier, group - 1 + rows - 1)
+
+
+class Spread:
+    def __init__(self, source, target, parts, sems):
+        self.source, self.target, self.parts = source, target, parts
+        self.send, self.recv, self.give, self.take = sems
+        self.here = lax.axis_index("dp")
+        z, self.core = chip_place()
+        self.partner = {"expert": 2 * z + 1 - self.core}
+        self.rows = source.shape[0]
+        self.shared = self.rows % 32 == 0
+        self.part = self.rows // 2 if self.shared else self.rows
+
+    @staticmethod
+    def scratch(parts):
+        return [pltpu.SemaphoreType.DMA((parts,)) for _ in range(4)]
+
+    def piece(self, k, core):
+        owner = lax.rem(self.here + self.parts - k, self.parts)
+        at = owner * self.rows + (core * self.part if self.shared else 0)
+        return self.target.at[pl.ds(pl.multiple_of(at, self.part), self.part), :]
+
+    def spread(self, k):
+        at = self.core * self.part if self.shared else 0
+        return remote(
+            self.source.at[pl.ds(pl.multiple_of(at, self.part), self.part), :],
+            self.piece(0, self.core),
+            self.send.at[k],
+            self.recv.at[k],
+            {"dp": lax.rem(self.here + k, self.parts)},
+        )
+
+    def own(self):
+        at = pl.multiple_of(self.here * self.rows, self.rows)
+        return remote(
+            self.source,
+            self.target.at[pl.ds(at, self.rows), :],
+            self.give.at[0],
+            self.take.at[0],
+            self.partner,
+        )
+
+    def handed(self, k, core):
+        block = self.piece(k, core)
+        return remote(block, block, self.give.at[k], self.take.at[k], self.partner)
+
+    def begin(self):
+        for k in range(1, self.parts):
+            self.spread(k).start()
+        self.own().start()
+
+    def forward(self):
+        for k in range(1, self.parts):
+            block = self.piece(k, self.core)
+            remote(block, block, self.send.at[k], self.recv.at[k], self.partner).wait_recv()
+            if self.shared:
+                self.handed(k, self.core).start()
+
+    def finish(self):
+        self.own().wait_send()
+        self.own().wait_recv()
+        for k in range(1, self.parts):
+            self.spread(k).wait_send()
+            if self.shared:
+                self.handed(k, self.core).wait_send()
+                self.handed(k, 1 - self.core).wait_recv()
 
 
 def open_kernel(
@@ -820,14 +941,74 @@
     )(rows)
 
 
-def collect_kernel(group, holders, part_ref, sum_ref, take, above, below, acc, *sems):
-    give_s, take_s, send_s, above_s, below_s = sems
+def tail_kernel(
+    group,
+    holders,
+    parts,
+    part_ref,
+    grads_ref,
+    sum_ref,
+    gsum_ref,
+    take,
+    above,
+    below,
+    acc,
+    pair,
+    across,
+    mine_z,
+    along,
+    *sems,
+):
+    give_s, take_s, send_s, above_s, below_s = sems[:5]
+    pgive_s, ptake_s, xsend_s, xrecv_s, zsend_s, zrecv_s, asend_s, arecv_s, hgive_s, htake_s = sems[5:]
     chips = group // 2
     z, core = chip_place()
+    here_dp = lax.axis_index("dp")
     batches = part_ref.shape[0]
     tok = sum_ref.shape[1]
+    half = pair.shape[1]
+    quarter = half // chips
     partner = {"expert": 2 * z + 1 - core}
     chunks = [(m, chip) for chip in range(holders) for m in range(batches)]
+
+    def grads(q, owner):
+        return grads_ref.at[pl.ds(pl.multiple_of((2 * q + owner) * half, half), half), :]
+
+    def pair_give(q):
+        return remote(grads(q, 1 - core), pair.at[q], pgive_s.at[q], ptake_s.at[q], partner)
+
+    def cross(k):
+        to = lax.rem(here_dp + k, parts)
+        return remote(pair.at[to], across.at[k], xsend_s.at[k], xrecv_s.at[k], {"dp": to})
+
+    def chip_on(j):
+        return lax.rem(z + j, chips)
+
+    def along_z(j):
+        return remote(
+            mine_z.at[chip_on(j)],
+            along.at[j],
+            zsend_s.at[j],
+            zrecv_s.at[j],
+            {"expert": 2 * chip_on(j) + core},
+        )
+
+    def whole_z(j):
+        return remote(
+            gsum_ref.at[core, z],
+            gsum_ref.at[core, z],
+            asend_s.at[j],
+            arecv_s.at[j],
+            {"expert": 2 * chip_on(j) + core},
+        )
+
+    def came_z(j):
+        block = gsum_ref.at[core, lax.rem(z + chips - j, chips)]
+        return remote(block, block, asend_s.at[j], arecv_s.at[j], partner)
+
+    def hand(j, owner):
+        block = gsum_ref.at[owner, lax.rem(z + chips - j, chips)]
+        return remote(block, block, hgive_s.at[j], htake_s.at[j], partner)
 
     def mine(m, chip, owner):
         at = pl.multiple_of((2 * chip + owner) * tok, tok)
@@ -865,9 +1046,14 @@
             acc.at[chip, m], take.at[chip, m], send_s.at[chip, m], sem.at[chip, m], partner
         )
 
-    meet(group, 1)
+    meet(group, parts)
+    for m in range(batches):
+        give(m, 0).start()
+    for q in range(parts):
+        pair_give(q).start()
     for m, chip in chunks:
-        give(m, chip).start()
+        if chip:
+            give(m, chip).start()
 
     @pl.when(z >= holders)
     def _():
@@ -896,18 +1082,69 @@
 
     from_above = (z + 1 < chips, above_s, above)
     from_below = (z > 0, below_s, below)
+
+    def streams(chip):
+        @pl.when(z > chip)
+        def _():
+            stream(chip, down, [from_above])
+
+    def first_sums():
+        for q in range(parts):
+            pair_give(q).wait_recv()
+            pair[q] = (pair[q].astype(f32) + grads(q, core)[...].astype(f32)).astype(low)
+        for q in range(parts):
+            pair_give(q).wait_send()
+        for k in range(1, parts):
+            cross(k).start()
+
+    def second_sums():
+        for k in range(1, parts):
+            cross(k).wait_recv()
+        total = pair[here_dp].astype(f32)
+        for k in range(1, parts):
+            total = total + across[k].astype(f32)
+        total = total.astype(low)
+        for j in range(chips):
+            mine_z[j] = total[j * quarter : (j + 1) * quarter, :]
+        for k in range(1, parts):
+            cross(k).wait_send()
+        for j in range(1, chips):
+            along_z(j).start()
+
+    def third_sums():
+        for j in range(1, chips):
+            along_z(j).wait_recv()
+        total = mine_z[z].astype(f32)
+        for j in range(1, chips):
+            total = total + along[j].astype(f32)
+        gsum_ref[core, z] = total.astype(low)
+        for j in range(1, chips):
+            along_z(j).wait_send()
+        for j in range(1, chips):
+            whole_z(j).start()
+        hand(0, core).start()
+
     for chip in reversed(range(holders)):
 
         @pl.when(z < chip)
         def _():
             stream(chip, up, [from_below])
 
+    @pl.when(z == chips - 1)
+    def _():
+        for chip in range(holders):
+            streams(chip)
+
+    first_sums()
     for chip in range(holders):
-
-        @pl.when(z > chip)
+        if chip == holders - 1:
+            second_sums()
+
+        @pl.when(z < chips - 1)
         def _():
-            stream(chip, down, [from_above])
-
+            streams(chip)
+
+    third_sums()
     for chip in range(holders):
 
         @pl.when(z == chip)
@@ -916,6 +1153,9 @@
                 add(m, chip, [from_above, from_below])
                 sum_ref[m] = acc[chip, m]
 
+    for j in range(1, chips):
+        came_z(j).wait_recv()
+        hand(j, core).start()
     for m, chip in chunks:
         give(m, chip).wait_send()
 
@@ -925,21 +1165,42 @@
             def _():
                 here(m, chip, take_s).wait_send()
 
-
-def collect_rows(part, group, holders, tok):
+    for j in range(chips):
+        hand(j, core).wait_send()
+        hand(j, 1 - core).wait_recv()
+        if j:
+            whole_z(j).wait_send()
+
+
+def tail_sums(part, grads, group, holders, tok, parts):
     batches, _, width = part.shape
-    chips = holders // 2
-    block = pltpu.VMEM((chips, batches, tok, width), low)
-    return pl.pallas_call(
-        functools.partial(collect_kernel, group, chips),
-        in_specs=[vmem()],
-        out_specs=vmem(),
-        out_shape=jax.ShapeDtypeStruct((batches, tok, width), low),
-        scratch_shapes=[block] * 4 + [pltpu.SemaphoreType.DMA((chips, batches))] * 5,
+    rows, columns = grads.shape
+    chips = group // 2
+    held = holders // 2
+    half = rows // parts // 2
+    block = pltpu.VMEM((held, batches, tok, width), low)
+    halves = pltpu.VMEM((parts, half, columns), low)
+    quarters = pltpu.VMEM((chips, half // chips, columns), low)
+    dma = pltpu.SemaphoreType.DMA
+    summed, gsum = pl.pallas_call(
+        functools.partial(tail_kernel, group, held, parts),
+        in_specs=[vmem(), vmem()],
+        out_specs=[vmem(), vmem()],
+        out_shape=[
+            jax.ShapeDtypeStruct((batches, tok, width), low),
+            jax.ShapeDtypeStruct((2, chips, half // chips, columns), low),
+        ],
+        scratch_shapes=[block] * 4
+        + [halves] * 2
+        + [quarters] * 2
+        + [dma((held, batches))] * 5
+        + [dma((parts,))] * 4
+        + [dma((chips,))] * 6,
         compiler_params=pltpu.CompilerParams(
-            collective_id=2, has_side_effects=True, vmem_limit_bytes=40_000_000
+            collective_id=2, has_side_effects=True, vmem_limit_bytes=56_000_000
         ),
-    )(part)
+    )(part, grads)
+    return summed, gsum.reshape(rows // parts, columns)
 
 
 def opposite(me, k, group):
@@ -1222,14 +1483,14 @@
     )(sent, cot_slots, wide, deep, router, onehot)
 
 
-def rotary(positions):
-    middle = HD // 2
-    frequency = jnp.exp(jnp.arange(middle).astype(f32) * (-2.0 * math.log(10000.0) / HD))
-    angles = positions.astype(f32)[:, None] * frequency[None, :]
-    cos_table, sine_table = jnp.cos(angles), jnp.sin(angles)
+def rotary(tok):
+    positions = np.concatenate([np.arange(PROMPT), PROMPT + np.arange(tok) % CLEN])
+    frequency = 10000.0 ** (np.arange(HD // 2) * (-2.0 / HD))
+    angles = positions[:, None] * frequency[None, :]
+    cos_table, sine_table = np.cos(angles), np.sin(angles)
     return (
-        jnp.concatenate([cos_table] * 4, axis=1),
-        jnp.concatenate([-sine_table, sine_table] * 2, axis=1),
+        np.concatenate([cos_table] * 4, axis=1).astype(np.float32),
+        np.concatenate([-sine_table, sine_table] * 2, axis=1).astype(np.float32),
     )
 
 
@@ -1271,18 +1532,12 @@
         holders,
     )
     prompt, cot_rows = lax.optimization_barrier((prompt, cotangent))
-    shared_wide = lax.all_gather(
-        jnp.concatenate([shared_gate, shared_up], axis=1), "dp", axis=0, tiled=True
-    )
-    shared_deep = lax.all_gather(shared_down, "dp", axis=0, tiled=True)
+    shared_wide_rows = jnp.concatenate([shared_gate, shared_up], axis=1)
     expert_wide = lax.all_gather(
         jnp.concatenate([expert_gate[0], expert_up[0]], axis=1), "dp", axis=0, tiled=True
     )
     expert_deep = lax.all_gather(expert_down[0], "dp", axis=0, tiled=True)
 
-    small_all = lax.optimization_barrier(attn_all[:, 4 * width :])
-    gains = small_all[:, :ROUTER_AT].T.astype(f32)
-    router = small_all
     lane = jnp.arange(LANES, dtype=jnp.int32)
     onehot = jnp.stack(
         [
@@ -1294,8 +1549,10 @@
     row_at = jnp.arange(tok, dtype=jnp.int32)
     query_pos = me * tok + row_at
     later = me >= holders
-    cos_o, sin_o = rotary(jnp.where(later, PROMPT + row_at % CLEN, query_pos))
-    cos_p, sin_p = rotary(jnp.arange(PROMPT, dtype=jnp.int32))
+    cos_p, sin_p = (jnp.asarray(table) for table in rotary(tok))
+    start = jnp.minimum(me, holders) * tok
+    cos_o = lax.dynamic_slice_in_dim(cos_p, start, tok, 0)
+    sin_o = lax.dynamic_slice_in_dim(sin_p, start, tok, 0)
     key_pos = jnp.arange(PROMPT, dtype=jnp.int32)[:, None]
     bias_p = jnp.where(later | (key_pos <= query_pos[None, :]), 0.0, neg_large).astype(f32)
     near = jnp.arange(CLEN, dtype=jnp.int32)
@@ -1335,11 +1592,25 @@
     prompt_spec = per_step((1, PROMPT, width), 0)
     lse_spec = per_step((1, 16, tok), 0)
     rows_shape = (batches, tok, width)
-    sent, mixed, resid, attended, query, keys, values, lse = pl.pallas_call(
+    (
+        sent,
+        mixed,
+        resid,
+        attended,
+        query,
+        keys,
+        values,
+        lse,
+        gains,
+        router,
+        shared_wide,
+        shared_deep,
+    ) = pl.pallas_call(
         functools.partial(attend_kernel, experts, capacity),
         grid=(batches,),
-        in_specs=[row_spec, prompt_spec, route_spec, weight_spec, whole((2, width))]
-        + table_specs,
+        in_specs=[row_spec, prompt_spec, route_spec, weight_spec]
+        + table_specs
+        + [in_place(), in_place()],
         out_specs=[
             slots_spec,
             row_spec,
@@ -1349,6 +1620,10 @@
             full_spec,
             full_spec,
             lse_spec,
+            whole((8, width)),
+            whole((width, LANES)),
+            in_place(),
+            in_place(),
         ],
         out_shape=[
             jax.ShapeDtypeStruct(slots_shape, low),
@@ -1359,15 +1634,26 @@
             jax.ShapeDtypeStruct((batches, total, width), low),
             jax.ShapeDtypeStruct((batches, total, width), low),
             jax.ShapeDtypeStruct((batches, 16, tok), f32),
+            jax.ShapeDtypeStruct((8, width), f32),
+            jax.ShapeDtypeStruct((width, LANES), low),
+            jax.ShapeDtypeStruct((width, 2 * ff), low),
+            jax.ShapeDtypeStruct((ff, width), low),
         ],
         scratch_shapes=[
             pltpu.VMEM((total, width), low),
             pltpu.VMEM((width, total), low),
             pltpu.VMEM((width, tok), f32),
-        ],
-        compiler_params=params(),
+        ]
+        + Spread.scratch(parts)
+        + Spread.scratch(parts),
+        compiler_params=pltpu.CompilerParams(
+            dimension_semantics=("arbitrary",),
+            vmem_limit_bytes=VMEM_LIMIT,
+            collective_id=5,
+            has_side_effects=True,
+        ),
         cost_estimate=LIGHT,
-    )(tokens, prompt, route_rows, attn_all, gains, *tables)
+    )(tokens, prompt, route_rows, attn_all, *tables, shared_wide_rows, shared_down)
 
 
     flat = (batches * tok, width)
@@ -1390,18 +1676,15 @@
     expert_y, dx_back, gexpert_wide, gexpert_deep, grouter = expert_layer(
         sent, cot_slots, expert_wide, expert_deep, router, onehot
     )
-    dx_back, expert_y, gshared_wide, gshared_deep = lax.optimization_barrier(
-        (dx_back, expert_y, gshared_wide, gshared_deep)
+    dx_back, gshared_wide, gshared_deep = lax.optimization_barrier(
+        (dx_back, gshared_wide, gshared_deep)
     )
     gshared_wide, gshared_deep = lax.psum((gshared_wide, gshared_deep), "expert")
-    y_back = exchange(expert_y)
-    gexpert_deep = scatter(gexpert_deep, 0)
-    gexpert_wide = scatter(gexpert_wide, 1)
-
-    dres, dnorm_own, dprompt, gattn = pl.pallas_call(
+
+    dres, dnorm_own, dprompt, gattn, y_back = pl.pallas_call(
         functools.partial(attend_back_kernel, experts, capacity),
         grid=(batches,),
-        in_specs=[row_spec, prompt_spec, route_spec, weight_spec, whole((2, width))]
+        in_specs=[row_spec, prompt_spec, route_spec, weight_spec, whole((8, width))]
         + table_specs
         + [
             row_spec,
@@ -1414,18 +1697,21 @@
             row_spec,
             slots_spec,
             whole((width, LANES)),
+            in_place(),
         ],
         out_specs=[
             row_spec,
             row_spec,
             prompt_spec,
             whole((width, 4 * width + LANES)),
+            in_place(),
         ],
         out_shape=[
             jax.ShapeDtypeStruct(rows_shape, f32),
             jax.ShapeDtypeStruct(rows_shape, f32),
             jax.ShapeDtypeStruct((batches, PROMPT, width), low),
             jax.ShapeDtypeStruct((width, 4 * width + LANES), low),
+            jax.ShapeDtypeStruct(slots_shape, low),
         ],
         scratch_shapes=[
             pltpu.VMEM((width, total), low),
@@ -1437,8 +1723,16 @@
             pltpu.VMEM((total, width), low),
             pltpu.VMEM((width, 4 * width), f32),
             pltpu.VMEM((LANES, width), f32),
+            pltpu.SemaphoreType.DMA((group,)),
+            pltpu.SemaphoreType.DMA((group,)),
+            pltpu.SemaphoreType.DMA((1,)),
         ],
-        compiler_params=params(),
+        compiler_params=pltpu.CompilerParams(
+            dimension_semantics=("arbitrary",),
+            vmem_limit_bytes=VMEM_LIMIT,
+            collective_id=4,
+            has_side_effects=True,
+        ),
         cost_estimate=LIGHT,
     )(
         tokens,
@@ -1457,14 +1751,16 @@
         shared_dx.reshape(rows_shape),
         dx_back,
         grouter,
-    )
-
-    gattn, gexpert_deep, gexpert_wide, gshared_wide, gshared_deep = lax.optimization_barrier(
-        (gattn, gexpert_deep, gexpert_wide, gshared_wide, gshared_deep)
-    )
-    gattn = lax.psum(scatter(gattn, 0), "expert").astype(f32)
-    dprompt, y_back = lax.optimization_barrier((dprompt, y_back))
-    dnorm_prompt = collect_rows(dprompt, group, holders, tok)
+        expert_y,
+    )
+
+    gexpert_deep, gexpert_wide, gshared_wide, gshared_deep, gattn = lax.optimization_barrier(
+        (gexpert_deep, gexpert_wide, gshared_wide, gshared_deep, gattn)
+    )
+    gexpert_deep = scatter(gexpert_deep, 0)
+    gexpert_wide = scatter(gexpert_wide, 1)
+    dnorm_prompt, gattn = tail_sums(dprompt, gattn, group, holders, tok, parts)
+    gattn = gattn.astype(f32)
     dnorm_prompt, gexpert_deep, gexpert_wide, gshared_wide, gshared_deep = (
         lax.optimization_barrier(
             (dnorm_prompt, gexpert_deep, gexpert_wide, gshared_wide, gshared_deep)

time: 932 us -> 783 us (0.84)
  waiting for transfers between devices: 336 us -> 72.4 us
  Pallas kernels: 495 us -> 631 us
  local copies, waits for them, and re-layouts: 28.7 us -> 18.8 us
    all_to_all x1 -> x0, waiting for transfers between devices: 105 us -> none  [per_device(): y_back = exchange(expert_y)]
    pallas_call x1, Pallas kernels: 80.4 us -> 133 us  [per_device(): pl.pallas_call(functools.partial(attend_back_kernel, experts, capacity),...]
    psum x1 -> x0, waiting for transfers between devices: 51 us -> none  [per_device(): gattn = lax.psum(scatter(gattn, 0), 'expert').astype(f32)]
    all_gather x1, waiting for transfers between devices: 47.2 us -> 0.01 us  [per_device(): lax.all_gather(jnp.concatenate([expert_gate[0], expert_up[0]], axis=1), '...]
    pallas_call x1, Pallas kernels: 56.8 us -> 101 us  [per_device(): pl.pallas_call(functools.partial(attend_kernel, experts, capacity), grid=...]
    pallas_call x1, Pallas kernels: 67.4 us -> 109 us  [tail_sums(): pl.pallas_call(functools.partial(tail_kernel, group, held, parts), in_spe...]
    reduce_scatter x5 -> x4, waiting for transfers between devices: 58.5 us -> 25.2 us  [scatter(): lax.psum_scatter(value, 'dp', scatter_dimension=dimension, tiled=True)]
    psum x1, waiting for transfers between devices: 69.4 us -> 45.2 us  [per_device(): lax.psum((gshared_wide, gshared_deep), 'expert')]
  transfers between devices with their start and end apart: 13 -> 8, of which waited for: 6 -> 2; matrix products, arithmetic and copies ran while one was open for 4% -> 2% of each run, Pallas kernels for 53% -> 81%
where the time goes in v5:
time: 783 us; the launch traced here: 780 us
  Pallas kernels  631 us (81%)
  waiting for transfers between devices  72.4 us (9%)
  starting transfers between devices  28 us (4%)
  local copies, waits for them, and re-layouts  18.8 us (2%)
  other arithmetic  15 us (2%)
  between operations  14.7 us (2%)
    pallas_call x1, Pallas kernels, expert_layer(): pl.pallas_call(functools.partial(expert_kernel, group), in_specs=[in_plac...  186 us
    pallas_call x1, Pallas kernels, per_device(): pl.pallas_call(functools.partial(attend_back_kernel, experts, capacity),...  133 us
    pallas_call x1, Pallas kernels, tail_sums(): pl.pallas_call(functools.partial(tail_kernel, group, held, parts), in_spe...  109 us
    pallas_call x1, Pallas kernels, per_device(): pl.pallas_call(functools.partial(attend_kernel, experts, capacity), grid=...  101 us
    pallas_call x1, Pallas kernels, open_gather(): pl.pallas_call(functools.partial(open_kernel, group, parts, holders // 2)...  46.8 us
    psum x1, waiting for transfers between devices, per_device(): lax.psum((gshared_wide, gshared_deep), 'expert')  45.2 us
    pallas_call x1, Pallas kernels, mlp(): pl.pallas_call(mlp_kernel, grid=(count // tile,), in_specs=[by_row(width)...  29.9 us
    all_to_all x1, starting transfers between devices, per_device(): cot_slots = exchange(cot_sent)  27.5 us
  transfers between devices with their start and end apart: 8, of which 2 were waited for; matrix products, arithmetic and copies ran while one was open for 2% of the time, Pallas kernels for 81%

profile of v5, /device:TPU:0, one launch (start us, length us, event | category | flops | bytes accessed | tf_op | source)
XLA Modules:
  0.0 779.8 jit_solution(2057020537211522620)
XLA Ops:
  8.0 2.7 pad_maximum_fusion.1
  12.1 46.8 %shard_map.289 = (bf16[3,1024,768]{2,1,0:T(8,128)(2,1)S(1)}, s32[8,3,2,256]{3,2,1,0:T(2,128)}, bf16[768,3200]{1,0:T(8,128)(2,1)S(1)}) custom-call(bf16[3,256,768]{2,1,0:T(8,128)(2,1)S(1)} %copy-done, s32[3,2,256]{2,1,0:T(2,128)S(1)} %bitcast.22, bf16[192,3200]{1,0:T(8,128)(2,1)S(1)} %pad_dynamic-update-slice_fusion.weight_ref), custom_call_target="tpu_custom_call" | custom-call | tf_op jit(solution)/shard_map/pallas_call | solution.py:901
  58.9 2.2 copy-done.3
  61.1 2.2 copy-done.4
  63.3 4.9 shard_map.290
  68.2 27.5 %all-to-all-start = ((bf16[8,3,128,768]{3,2,1,0:T(8,128)(2,1)}), bf16[8,3,128,768]{3,2,1,0:T(8,128)(2,1)}, u32[]{:S(2)}, u32[]{:S(2)}) async-start(bf16[8,3,128,768]{3,2,1,0:T(8,128)(2,1)} %shard_map.290), calls=%async_computation | async-start | bytes 9437184 | tf_op jit(solution)/shard_map/all_to_all | solution.py:1578
  96.4 1.7 constant_dynamic-slice_fusion
  100.5 100.5 %shard_map.291 = (bf16[8,3,128,768]{3,2,1,0:T(8,128)(2,1)}, bf16[3,256,768]{2,1,0:T(8,128)(2,1)}, f32[3,256,768]{2,1,0:T(8,128)}, bf16[3,256,768]{2,1,0:T(8,128)...) custom-call(bf16[3,256,768]{2,1,0:T(8,128)(2,1)} %own_ref.3, ...), custom_call_target="tpu_custom_call" | custom-call | flops 1 | bytes 1 | tf_op jit(solution)/shard_map/pallas_call | solution.py:1608
  201.0 29.9 %shard_map.292 = (f32[768,768]{1,0:T(8,128)}, bf16[768,768]{1,0:T(8,128)(2,1)}, bf16[768,2048]{1,0:T(8,128)(2,1)}, bf16[2,768,2048]{2,1,0:T(8,128)(2,1)}) custom-call(bf16[768,768]{1,0:T(8,128)(2,1)} %bitcast.25, bf16[768,768]{1,0:T(8,128)(2,1)} %bitcast.23, bf16[768,4096]{1,0:T(8,128)(2,1)} %get-tuple-element.77.wide_ref, ...), custom_call_target="tpu_custom_call" | custom-call | flops 1 | bytes 1 | tf_op jit(solution)/shard_map/pallas_call | solution.py:292
  230.9 14.6 %shard_map.293 = (bf16[2,768,2048]{2,1,0:T(8,128)(2,1)}, bf16[2048,768]{1,0:T(8,128)(2,1)}) custom-call(bf16[768,768]{1,0:T(8,128)(2,1)} %bitcast.26, bf16[768,768]{1,0:T(8,128)(2,1)} %bitcast.24, bf16[768,2048]{1,0:T(8,128)(2,1)} %get-tuple-element.91.hidden_ref, bf16[2,768,2048]{2,1,0:T(8,128)(2,1)} %get-tuple-element.92.dwide_ref), custom_call_target="tpu_custom_call" | custom-call | flops 1 | bytes 1 | tf_op jit(solution)/shard_map/pallas_call | solution.py:337
  247.0 185.6 %shard_map.294 = (bf16[8,3,128,768]{3,2,1,0:T(8,128)(2,1)}, bf16[8,3,128,768]{3,2,1,0:T(8,128)(2,1)}, bf16[2,768,2048]{2,1,0:T(8,128)(2,1)}, bf16[2048,768]{1,0:T(8,128)(2,1)}, f32[768,128]{1,0:T(8,128)}) custom-call(bf16[8,3,128,768]{3,2,1,0:T(8,128)(2,1)} %get-tuple-element.87.sent_ref, bf16[8,3,128,768]{3,2,1,0:T(8,128)(2,1)} %all-to-all-done.cot_hbm, ...), custom_call_target="tpu_custom_call" | custom-call | flops 1 | bytes 1 | tf_op jit(solution)/shard_map/pallas_call | solution.py:1443
  432.7 133.2 %shard_map.295 = (f32[3,256,768]{2,1,0:T(8,128)}, f32[3,256,768]{2,1,0:T(8,128)}, bf16[3,1024,768]{2,1,0:T(8,128)(2,1)}, bf16[768,3200]{1,0:T(8,128)(2,1)}, bf16[8,3,128,768]{3,2,1,0:T(8,128)(2,1)}) custom-call(bf16[3,256,768]{2,1,0:T(8,128)(2,1)} %own_ref.3, bf16[3,1024,768]{2,1,0:T(8,128)(2,1)} %copy-done.4, s32[3,2,256]{2,1,0:T(2,128)} %bitcast.20, ...), custom_call_target="tpu_custom_call" | custom-call | flops 1 | bytes 1 | tf_op jit(solution)/shard_map/pallas_call | solution.py:1684
  565.9 45.2 %all-reduce.4.cloned.1.call-done = (bf16[2,192,2048]{2,1,0:T(8,128)(2,1)}, bf16[512,768]{1,0:T(8,128)(2,1)}) async-done(((bf16[2,192,2048]{2,1,0:T(8,128)(2,1)}, bf16[512,768]{1,0:T(8,128)(2,1)}), (bf16[2,192,2048]{2,1,0:T(8,128)(2,1)}, bf16[512,768]{1,0:T(8,128)(2,1)})) %all-reduce.4.cloned.1.call-update) | async-done | bytes 2359312 | tf_op jit(solution)/shard_map/psum | solution.py:1682
  613.0 7.1 shard_map.296
  620.1 108.6 %shard_map.297 = (bf16[3,256,768]{2,1,0:T(8,128)(2,1)}, bf16[2,4,24,3200]{3,2,1,0:T(8,128)(2,1)}) custom-call(bf16[3,1024,768]{2,1,0:T(8,128)(2,1)} %get-tuple-element.107.part_ref, bf16[768,3200]{1,0:T(8,128)(2,1)} %get-tuple-element.113.grads_ref), custom_call_target="tpu_custom_call" | custom-call | tf_op jit(solution)/shard_map/pallas_call | solution.py:1185
  728.7 1.4 bitcast_convert_fusion
  732.4 3.2 fusion.12
  735.7 25.1 %reduce-scatter.11.cloned.1.call-done = bf16[2,192,2048]{2,1,0:T(8,128)(2,1)} async-done(((bf16[2,768,2048]{2,1,0:T(8,128)(2,1)}), bf16[2,192,2048]{2,1,0:T(8,128)(2,1)}) %reduce-scatter.11.cloned.1.call-update) | async-done | bytes 1572880 | tf_op jit(solution)/shard_map/reduce_scatter | solution.py:1670
  760.8 2.1 fusion.2
  763.3 1.9 slice_bitcast_fusion
  765.2 1.3 convert_element_type.49
  766.5 1.3 bitcast_convert_fusion.1
  767.8 2.0 fusion.13
  771.0 1.8 fusion.6
  (87 shorter events, 12.4 us)
Async XLA Ops:
  7.2 238.3 %all-gather.6.cloned.1.call-start = ((), (), s32[]{:S(2)}) async-start(), calls=%async_computation.10 | async-start | bytes 3932160 | tf_op jit(solution)/shard_map/all_gather | solution.py:1539
  7.9 237.6 %all-gather.4.cloned.1.call-start = ((), (), s32[]{:S(2)}) async-start(), calls=%async_computation.5 | async-start | bytes 7864320 | tf_op jit(solution)/shard_map/all_gather | solution.py:1536
  8.0 2.8 copy-start.21
  8.0 2.8 copy-start.22
  8.0 2.9 copy-start.20
  8.0 3.0 copy-start.16
  8.0 3.0 copy-start.17
  8.0 3.1 copy-start.18
  58.9 2.2 copy-start.3
  61.1 2.2 copy-start.4
  68.2 31.1 %copy-start.12 = (bf16[192,2048]{1,0:T(8,128)(2,1)S(1)}, bf16[192,2048]{1,0:T(8,128)(2,1)}, u32[]{:S(2)}) copy-start(bf16[192,2048]{1,0:T(8,128)(2,1)} %param.29) | copy-start | bytes 2359300
  68.2 31.1 %copy-start.13 = (bf16[192,2048]{1,0:T(8,128)(2,1)S(1)}, bf16[192,2048]{1,0:T(8,128)(2,1)}, u32[]{:S(2)}) copy-start(bf16[192,2048]{1,0:T(8,128)(2,1)} %param.28) | copy-start | bytes 2359300
  68.2 162.8 %all-to-all-start = ((bf16[8,3,128,768]{3,2,1,0:T(8,128)(2,1)}), bf16[8,3,128,768]{3,2,1,0:T(8,128)(2,1)}, u32[]{:S(2)}, u32[]{:S(2)}) async-start(bf16[8,3,128,768]{3,2,1,0:T(8,128)(2,1)} %shard_map.290), calls=%async_computation | async-start | bytes 9437184 | tf_op jit(solution)/shard_map/all_to_all | solution.py:1578
  95.6 336.9 %reduce-scatter.7.cloned.1.call-start = ((), (), s32[]{:S(2)}) async-start(), calls=%async_computation.7 | async-start | bytes 3932160 | tf_op jit(solution)/shard_map/reduce_scatter | solution.py:1670
  245.6 187.0 %reduce-scatter.5.cloned.1.call-start = ((), (), s32[]{:S(2)}) async-start(), calls=%async_computation.6 | async-start | bytes 7864320 | tf_op jit(solution)/shard_map/reduce_scatter | solution.py:1670
  246.1 365.0 %all-reduce.4.cloned.1.call-start = ((), (), s32[]{:S(2)}) async-start(), calls=%async_computation.11 | async-start | bytes 4718592 | tf_op jit(solution)/shard_map/psum | solution.py:1682
  432.6 303.0 %reduce-scatter.9.cloned.1.call-start = ((), (), s32[]{:S(2)}) async-start(), calls=%async_computation.8 | async-start | bytes 3932160 | tf_op jit(solution)/shard_map/reduce_scatter | solution.py:1670
  611.2 149.6 %reduce-scatter.11.cloned.1.call-start = ((), (), s32[]{:S(2)}) async-start(), calls=%async_computation.9 | async-start | bytes 7864320 | tf_op jit(solution)/shard_map/reduce_scatter | solution.py:1670
  732.4 28.4 %copy-start.2 = (bf16[3,256,768]{2,1,0:T(8,128)(2,1)S(1)}, bf16[3,256,768]{2,1,0:T(8,128)(2,1)}, u32[]{:S(2)}) copy-start(bf16[3,256,768]{2,1,0:T(8,128)(2,1)} %own_ref.3) | copy-start | bytes 3538948
  732.4 28.4 %copy-start.7 = (f32[3,256,768]{2,1,0:T(8,128)S(1)}, f32[3,256,768]{2,1,0:T(8,128)}, u32[]{:S(2)}) copy-start(f32[3,256,768]{2,1,0:T(8,128)} %get-tuple-element.106) | copy-start | bytes 7077892
  760.8 2.1 copy-start.11
  765.1 2.6 copy-start.8
  767.8 2.0 copy-start.9
  767.8 3.2 copy-start.10
  (7 other events, 10.0 us)
Sparse Core Ops, SparseCore 0:
  9.8 62.5 all-gather.5
  74.8 120.5 all-gather.3
  245.7 42.9 reduce-scatter.6
  291.6 70.0 reduce-scatter.4
  432.8 178.3 all-reduce.3
  614.0 72.0 reduce-scatter.8
  689.0 71.7 reduce-scatter.10

commit v6 on v5

--- a/solution.py
+++ b/solution.py
@@ -84,13 +84,6 @@
     tok = ranks.shape[1]
     slot = lax.broadcasted_iota(jnp.int32, (capacity, tok), 0).astype(f32)
     return jnp.where(slot == ranks[expert : expert + 1, :], 1.0, 0.0).astype(low)
-
-
-def send_kernel(experts, capacity, rows_ref, route_ref, out_ref):
-    ranks = slot_ranks(route_ref[0], experts)
-    rows = rows_ref[0]
-    for e in range(experts):
-        out_ref[e, 0] = mm(placement(ranks, e, capacity), rows).astype(low)
 
 
 def gather_slots(ranks, slots_ref, experts, capacity):
@@ -114,8 +107,6 @@
     sin_o,
     bias_p,
     bias_o,
-    wide_rows,
-    deep_rows,
     sent_ref,
     mixed_ref,
     resid_ref,
@@ -126,25 +117,14 @@
     lse_ref,
     gain_ref,
     router_ref,
-    wide_all,
-    deep_all,
     normed_s,
     value_t,
     out_t,
-    *sems,
 ):
     tok, width = own_ref.shape[1:]
-    parts = wide_all.shape[0] // wide_rows.shape[0]
-    spreads = (
-        Spread(deep_rows, deep_all, parts, sems[:4]),
-        Spread(wide_rows, wide_all, parts, sems[4:]),
-    )
 
     @pl.when(pl.program_id(0) == 0)
     def _():
-        meet(experts, parts)
-        for spread in spreads:
-            spread.begin()
         gain_ref[...] = weight_ref[:, 4 * width :].astype(f32).T[:8]
         router_ref[...] = weight_ref[:, 4 * width :]
 
@@ -224,14 +204,6 @@
     ranks = slot_ranks(route_ref[0], experts)
     for e in range(experts):
         sent_ref[e, 0] = mm(placement(ranks, e, capacity), mixed).astype(low)
-
-    @pl.when(pl.program_id(0) == pl.num_programs(0) - 1)
-    def _():
-        for spread in spreads:
-            spread.forward()
-        for spread in spreads:
-            spread.finish()
-
 
 def mlp_kernel(
     rows_ref,
@@ -741,24 +713,42 @@
         self.rows = source.shape[0]
         self.shared = self.rows % 32 == 0
         self.part = self.rows // 2 if self.shared else self.rows
+        self.square = parts == 4 and self.rows % 64 == 0
 
     @staticmethod
     def scratch(parts):
-        return [pltpu.SemaphoreType.DMA((parts,)) for _ in range(4)]
-
-    def piece(self, k, core):
-        owner = lax.rem(self.here + self.parts - k, self.parts)
+        return [pltpu.SemaphoreType.DMA((max(parts, 5),)) for _ in range(4)]
+
+    def peer(self, k):
+        if not self.square:
+            return lax.rem(self.here + k, self.parts)
+        first, second = self.here // 2, lax.rem(self.here, 2)
+        if k == 1:
+            return 2 * first + 1 - second
+        if k == 2:
+            return 2 * (1 - first) + second
+        return 3 - self.here
+
+    def sender(self, k):
+        return self.peer(k) if self.square else lax.rem(self.here + self.parts - k, self.parts)
+
+    def piece(self, owner, core):
         at = owner * self.rows + (core * self.part if self.shared else 0)
         return self.target.at[pl.ds(pl.multiple_of(at, self.part), self.part), :]
+
+    def corner(self, owner, core, side):
+        size = self.part // 2
+        at = owner * self.rows + core * self.part + side * size
+        return self.target.at[pl.ds(pl.multiple_of(at, size), size), :]
 
     def spread(self, k):
         at = self.core * self.part if self.shared else 0
         return remote(
             self.source.at[pl.ds(pl.multiple_of(at, self.part), self.part), :],
-            self.piece(0, self.core),
+            self.piece(self.here, self.core),
             self.send.at[k],
             self.recv.at[k],
-            {"dp": lax.rem(self.here + k, self.parts)},
+            {"dp": self.peer(k)},
         )
 
     def own(self):
@@ -771,28 +761,56 @@
             self.partner,
         )
 
+    def relay(self, k):
+        block = self.corner(self.sender(k), self.core, k - 1)
+        return remote(
+            block, block, self.send.at[k + 2], self.recv.at[k + 2], {"dp": self.peer(3 - k)}
+        )
+
+    def block(self, k, core):
+        if self.square and k > 2:
+            return self.corner(self.peer(3), core, k - 3)
+        return self.piece(self.sender(k), core)
+
     def handed(self, k, core):
-        block = self.piece(k, core)
+        block = self.block(k, core)
         return remote(block, block, self.give.at[k], self.take.at[k], self.partner)
 
+    def direct(self):
+        return range(1, 3 if self.square else self.parts)
+
+    def arrivals(self):
+        return range(1, 5 if self.square else self.parts)
+
     def begin(self):
-        for k in range(1, self.parts):
+        for k in self.direct():
             self.spread(k).start()
         self.own().start()
 
+    def arrive(self, k):
+        block = self.block(k, self.core)
+        remote(block, block, self.send.at[k], self.recv.at[k], self.partner).wait_recv()
+        if self.square and k < 3:
+            self.relay(k).start()
+        if self.shared:
+            self.handed(k, self.core).start()
+
     def forward(self):
-        for k in range(1, self.parts):
-            block = self.piece(k, self.core)
-            remote(block, block, self.send.at[k], self.recv.at[k], self.partner).wait_recv()
-            if self.shared:
-                self.handed(k, self.core).start()
+        for k in self.direct():
+            self.arrive(k)
 
     def finish(self):
+        if self.square:
+            for k in (3, 4):
+                self.arrive(k)
         self.own().wait_send()
         self.own().wait_recv()
-        for k in range(1, self.parts):
+        for k in self.direct():
             self.spread(k).wait_send()
-            if self.shared:
+            if self.square:
+                self.relay(k).wait_send()
+        if self.shared:
+            for k in self.arrivals():
                 self.handed(k, self.core).wait_send()
                 self.handed(k, 1 - self.core).wait_recv()
 
@@ -801,35 +819,44 @@
     group,
     parts,
     holders,
+    capacity,
     tokens_ref,
     route_ref,
-    weight_ref,
+    query_ref,
+    key_ref,
+    value_ref,
+    out_ref,
+    small_ref,
+    deep_ref,
+    gate_ref,
+    up_ref,
+    cot_ref,
     prompt_ref,
     routes_ref,
     whole_ref,
+    deep_all,
+    wide_all,
+    cot_slots,
+    weight_ref,
+    wide_ref,
     *sems,
 ):
-    chain_sems, (wsend, wrecv, wgive, wtake, rsend, rrecv, local) = sems[:5], sems[5:]
-    chain = Chain(tokens_ref, prompt_ref, group // 2, holders, chain_sems)
-    me, here = lax.axis_index("expert"), lax.axis_index("dp")
-    rows = weight_ref.shape[0]
-    shared = rows % 32 == 0
-    part = rows // 2 if shared else rows
-    offset = chain.core * part if shared else 0
+    width = tokens_ref.shape[2]
+    for n, part in enumerate((query_ref, key_ref, value_ref, out_ref)):
+        weight_ref[:, n * width : (n + 1) * width] = part[...]
+    weight_ref[:, 4 * width :] = small_ref[...]
+    ff = gate_ref.shape[1]
+    wide_ref[:, :ff] = gate_ref[...]
+    wide_ref[:, ff:] = up_ref[...]
+    chain = Chain(tokens_ref, prompt_ref, group // 2, holders, sems[:5])
+    spreads = (
+        Spread(weight_ref, whole_ref, parts, sems[5:9]),
+        Spread(deep_ref, deep_all, parts, sems[9:13]),
+        Spread(wide_ref, wide_all, parts, sems[13:17]),
+    )
+    rsend, rrecv, local = sems[17:]
+    me = lax.axis_index("expert")
     partner = {"expert": 2 * chain.z + 1 - chain.core}
-
-    def piece(owner, core):
-        at = owner * rows + (core * part if shared else 0)
-        return whole_ref.at[pl.ds(pl.multiple_of(at, part), part), :]
-
-    def spread(k):
-        return remote(
-            weight_ref.at[pl.ds(pl.multiple_of(offset, part), part), :],
-            piece(here, chain.core),
-            wsend.at[k],
-            wrecv.at[k],
-            {"dp": lax.rem(here + k, parts)},
-        )
 
     def routed(k):
         return remote(
@@ -840,48 +867,31 @@
             {"expert": lax.rem(me + k, group)},
         )
 
-    def from_behind(k):
-        return lax.rem(here + parts - k, parts)
-
-    def handed(k, core):
-        block = piece(from_behind(k), core)
-        return remote(block, block, wgive.at[k], wtake.at[k], partner)
-
-    keep_weights = pltpu.make_async_copy(
-        weight_ref, whole_ref.at[pl.ds(pl.multiple_of(here * rows, rows), rows), :], local.at[0]
-    )
-    keep_routes = pltpu.make_async_copy(route_ref, routes_ref.at[me], local.at[1])
+    keep_routes = pltpu.make_async_copy(route_ref, routes_ref.at[me], local.at[0])
 
     meet(group, parts)
     chain.begin()
-    for k in range(1, parts):
-        spread(k).start()
+    for spread in spreads:
+        spread.begin()
     for k in range(1, group):
         routed(k).start()
-    keep_weights.start()
     keep_routes.start()
-
-    def pass_weights(k):
-        block = piece(from_behind(k), chain.core)
-        remote(block, block, wsend.at[k], wrecv.at[k], partner).wait_recv()
-        if shared:
-            handed(k, chain.core).start()
-
+    spreads[0].forward()
     chain.step(1)
-    for k in range(1, parts):
-        pass_weights(k)
+    for m in range(cot_ref.shape[0]):
+        ranks = slot_ranks(route_ref[m], group)
+        for e in range(group):
+            cot_slots[e, m] = mm(placement(ranks, e, capacity), cot_ref[m]).astype(low)
+    spreads[1].forward()
+    spreads[2].forward()
     for d in range(2, group // 2):
         chain.step(d)
-    for k in range(1, parts):
-        spread(k).wait_send()
-        if shared:
-            handed(k, chain.core).wait_send()
-            handed(k, 1 - chain.core).wait_recv()
+    for spread in spreads:
+        spread.finish()
     for k in range(1, group):
         routed(k).wait_send()
         came = routes_ref.at[lax.rem(me + group - k, group)]
         remote(came, came, rsend.at[k], rrecv.at[k], partner).wait_recv()
-    keep_weights.wait()
     keep_routes.wait()
     chain.finish()
 
@@ -894,51 +904,39 @@
     return pl.BlockSpec(memory_space=pl.ANY)
 
 
-def open_gather(tokens, route_rows, weight_rows, group, parts, holders):
+def open_gather(tokens, route_rows, attn, deep_rows, wide, cot, group, parts, holders, capacity):
     batches, tok, width = tokens.shape
-    rows, columns = weight_rows.shape
     dma = pltpu.SemaphoreType.DMA
+    columns = sum(part.shape[1] for part in attn)
+    rows = attn[0].shape[0]
+    ff = wide[0].shape[1]
+    gathered = [
+        jax.ShapeDtypeStruct((parts * rows, columns), low),
+        jax.ShapeDtypeStruct((parts * deep_rows.shape[0], width), low),
+        jax.ShapeDtypeStruct((parts * rows, 2 * ff), low),
+    ]
     return pl.pallas_call(
-        functools.partial(open_kernel, group, parts, holders // 2),
-        in_specs=[vmem(), vmem(), vmem()],
-        out_specs=[in_place(), in_place(), in_place()],
+        functools.partial(open_kernel, group, parts, holders // 2, capacity),
+        in_specs=[vmem()] * 11,
+        out_specs=[in_place()] * 5 + [vmem()],
         out_shape=[
             jax.ShapeDtypeStruct((batches, holders * tok, width), low),
             jax.ShapeDtypeStruct((group,) + route_rows.shape, route_rows.dtype),
-            jax.ShapeDtypeStruct((parts * rows, columns), low),
-        ],
-        scratch_shapes=Chain.scratch(group // 2, batches)
-        + [dma((parts,))] * 4
+        ]
+        + gathered
+        + [jax.ShapeDtypeStruct((group, batches, capacity, width), low)],
+        scratch_shapes=[
+            pltpu.VMEM((rows, columns), low),
+            pltpu.VMEM((rows, 2 * ff), low),
+        ]
+        + Chain.scratch(group // 2, batches)
+        + Spread.scratch(parts) * 3
         + [dma((group,))] * 2
-        + [dma((2,))],
+        + [dma((1,))],
         compiler_params=pltpu.CompilerParams(
-            collective_id=0, has_side_effects=True, vmem_limit_bytes=24_000_000
+            collective_id=0, has_side_effects=True, vmem_limit_bytes=VMEM_LIMIT
         ),
-    )(tokens, route_rows, weight_rows)
-
-
-def spread_kernel(group, parts, rows_ref, all_ref, *sems):
-    chips = group // 2
-    chain = Chain(rows_ref, all_ref, chips, chips, sems)
-    meet(group, 1)
-    chain.begin()
-    for d in range(1, chips):
-        chain.step(d)
-    chain.finish()
-
-
-def spread_rows(rows, group):
-    batches, tok, width = rows.shape
-    return pl.pallas_call(
-        functools.partial(spread_kernel, group, 1),
-        in_specs=[vmem()],
-        out_specs=in_place(),
-        out_shape=jax.ShapeDtypeStruct((batches, group * tok, width), low),
-        scratch_shapes=Chain.scratch(group // 2, batches),
-        compiler_params=pltpu.CompilerParams(
-            collective_id=1, has_side_effects=True, vmem_limit_bytes=24_000_000
-        ),
-    )(rows)
+    )(tokens, route_rows, *attn, deep_rows, *wide, cot)
 
 
 def tail_kernel(
@@ -1523,20 +1521,23 @@
     small = jnp.pad(small, ((0, 0), (0, LANES - small.shape[1])))
     group, parts = lax.axis_size("expert"), lax.axis_size("dp")
     route_rows = jnp.swapaxes(routes, 1, 2)
-    prompt, routes_all, attn_all = open_gather(
+    prompt, routes_all, attn_all, shared_deep, shared_wide, cot_sent = open_gather(
         tokens,
         route_rows,
-        jnp.concatenate([query_weight, key_weight, value_weight, out_weight, small], axis=1),
+        (query_weight, key_weight, value_weight, out_weight, small),
+        shared_down,
+        (shared_gate, shared_up),
+        cotangent,
         group,
         parts,
         holders,
-    )
-    prompt, cot_rows = lax.optimization_barrier((prompt, cotangent))
-    shared_wide_rows = jnp.concatenate([shared_gate, shared_up], axis=1)
-    expert_wide = lax.all_gather(
-        jnp.concatenate([expert_gate[0], expert_up[0]], axis=1), "dp", axis=0, tiled=True
-    )
-    expert_deep = lax.all_gather(expert_down[0], "dp", axis=0, tiled=True)
+        capacity,
+    )
+    prompt, expert_wide, expert_deep = lax.optimization_barrier(
+        (prompt, jnp.concatenate([expert_gate[0], expert_up[0]], axis=1), expert_down[0])
+    )
+    expert_deep = lax.all_gather(expert_deep, "dp", axis=0, tiled=True)
+    expert_wide = lax.all_gather(expert_wide, "dp", axis=0, tiled=True)
 
     lane = jnp.arange(LANES, dtype=jnp.int32)
     onehot = jnp.stack(
@@ -1563,14 +1564,6 @@
     row_spec = per_step((1, tok, width), 0)
     route_spec = per_step((1, 2, tok), 0)
 
-    cot_sent = pl.pallas_call(
-        functools.partial(send_kernel, experts, capacity),
-        grid=(batches,),
-        in_specs=[row_spec, route_spec],
-        out_specs=slots_spec,
-        out_shape=jax.ShapeDtypeStruct(slots_shape, low),
-        compiler_params=params(),
-    )(cot_rows, route_rows)
     exchange = functools.partial(
         lax.all_to_all, axis_name="expert", split_axis=0, concat_axis=0, tiled=True
     )
@@ -1603,14 +1596,11 @@
         lse,
         gains,
         router,
-        shared_wide,
-        shared_deep,
     ) = pl.pallas_call(
         functools.partial(attend_kernel, experts, capacity),
         grid=(batches,),
         in_specs=[row_spec, prompt_spec, route_spec, weight_spec]
-        + table_specs
-        + [in_place(), in_place()],
+        + table_specs,
         out_specs=[
             slots_spec,
             row_spec,
@@ -1622,8 +1612,6 @@
             lse_spec,
             whole((8, width)),
             whole((width, LANES)),
-            in_place(),
-            in_place(),
         ],
         out_shape=[
             jax.ShapeDtypeStruct(slots_shape, low),
@@ -1636,31 +1624,21 @@
             jax.ShapeDtypeStruct((batches, 16, tok), f32),
             jax.ShapeDtypeStruct((8, width), f32),
             jax.ShapeDtypeStruct((width, LANES), low),
-            jax.ShapeDtypeStruct((width, 2 * ff), low),
-            jax.ShapeDtypeStruct((ff, width), low),
         ],
         scratch_shapes=[
             pltpu.VMEM((total, width), low),
             pltpu.VMEM((width, total), low),
             pltpu.VMEM((width, tok), f32),
-        ]
-        + Spread.scratch(parts)
-        + Spread.scratch(parts),
-        compiler_params=pltpu.CompilerParams(
-            dimension_semantics=("arbitrary",),
-            vmem_limit_bytes=VMEM_LIMIT,
-            collective_id=5,
-            has_side_effects=True,
-        ),
+        ],
+        compiler_params=params(),
         cost_estimate=LIGHT,
-    )(tokens, prompt, route_rows, attn_all, *tables, shared_wide_rows, shared_down)
+    )(tokens, prompt, route_rows, attn_all, *tables)
 
 
     flat = (batches * tok, width)
     shared_y, shared_dx, shared_hidden, shared_dwide = mlp(
         mixed.reshape(flat), cotangent.reshape(flat), shared_wide, shared_deep
     )
-    shared_hidden, cot_slots = lax.optimization_barrier((shared_hidden, cot_slots))
     gshared_wide, gshared_deep = mlp_weights(
         mixed.reshape(flat), cotangent.reshape(flat), shared_hidden, shared_dwide
     )
@@ -1669,17 +1647,15 @@
     def scatter(value, dimension):
         return lax.psum_scatter(value, "dp", scatter_dimension=dimension, tiled=True)
 
-    gshared_wide, gshared_deep, expert_wide, expert_deep = lax.optimization_barrier(
-        (gshared_wide, gshared_deep, expert_wide, expert_deep)
+    gshared_wide, gshared_deep, expert_wide, expert_deep, cot_slots = lax.optimization_barrier(
+        (gshared_wide, gshared_deep, expert_wide, expert_deep, cot_slots)
     )
     gshared_wide, gshared_deep = scatter(gshared_wide, 1), scatter(gshared_deep, 0)
     expert_y, dx_back, gexpert_wide, gexpert_deep, grouter = expert_layer(
         sent, cot_slots, expert_wide, expert_deep, router, onehot
     )
-    dx_back, gshared_wide, gshared_deep = lax.optimization_barrier(
-        (dx_back, gshared_wide, gshared_deep)
-    )
-    gshared_wide, gshared_deep = lax.psum((gshared_wide, gshared_deep), "expert")
+    gexpert_deep = scatter(gexpert_deep, 0)
+    gexpert_wide = scatter(gexpert_wide, 1)
 
     dres, dnorm_own, dprompt, gattn, y_back = pl.pallas_call(
         functools.partial(attend_back_kernel, experts, capacity),
@@ -1754,18 +1730,10 @@
         expert_y,
     )
 
-    gexpert_deep, gexpert_wide, gshared_wide, gshared_deep, gattn = lax.optimization_barrier(
-        (gexpert_deep, gexpert_wide, gshared_wide, gshared_deep, gattn)
-    )
-    gexpert_deep = scatter(gexpert_deep, 0)
-    gexpert_wide = scatter(gexpert_wide, 1)
-    dnorm_prompt, gattn = tail_sums(dprompt, gattn, group, holders, tok, parts)
-    gattn = gattn.astype(f32)
-    dnorm_prompt, gexpert_deep, gexpert_wide, gshared_wide, gshared_deep = (
-        lax.optimization_barrier(
-            (dnorm_prompt, gexpert_deep, gexpert_wide, gshared_wide, gshared_deep)
-        )
-    )
+    gshared_deep, gshared_wide, gattn = lax.optimization_barrier(
+        (gshared_deep, gshared_wide, gattn)
+    )
+    gshared_wide, gshared_deep = lax.psum((gshared_wide, gshared_deep), "expert")
     output = pl.pallas_call(
         functools.partial(finish_kernel, experts, capacity),
         grid=(batches,),
@@ -1775,6 +1743,16 @@
         compiler_params=params(),
     )(resid, shared_y.reshape(rows_shape), y_back, route_rows)
 
+    output, dprompt, gattn = lax.optimization_barrier((output, dprompt, gattn))
+    dnorm_prompt, gattn = tail_sums(dprompt, gattn, group, holders, tok, parts)
+    at = 4 * width
+    pieces = [gattn[:, j : j + width] for j in range(0, at, width)] + [gattn[:, at:]]
+    dnorm_prompt, pieces, gexpert_deep, gexpert_wide, gshared_wide, gshared_deep = (
+        lax.optimization_barrier(
+            (dnorm_prompt, pieces, gexpert_deep, gexpert_wide, gshared_wide, gshared_deep)
+        )
+    )
+    gquery, gkey, gvalue, gout, gsmall = (piece.astype(f32) for piece in pieces)
     dnorm = dnorm_own + dnorm_prompt.astype(f32)
     own = tokens.astype(f32)
     inverse = inverse_rms(own)
@@ -1786,17 +1764,16 @@
 
     gexpert_wide, gexpert_deep = gexpert_wide.astype(f32), gexpert_deep.astype(f32)
     gshared_wide, gshared_deep = gshared_wide.astype(f32), gshared_deep.astype(f32)
-    at = 4 * width
     return (
         output,
         input_grad,
-        gattn[:, at],
-        gattn[:, :width],
-        gattn[:, width : 2 * width],
-        gattn[:, 2 * width : 3 * width],
-        gattn[:, 3 * width : at],
-        gattn[:, at + 1],
-        gattn[:, at + ROUTER_AT : at + ROUTER_AT + experts],
+        gsmall[:, 0],
+        gquery,
+        gkey,
+        gvalue,
+        gout,
+        gsmall[:, 1],
+        gsmall[:, ROUTER_AT : ROUTER_AT + experts],
         gshared_wide[0],
         gshared_wide[1],
         gshared_deep,

time: 783 us -> 730 us (0.932)
  waiting for transfers between devices: 72.4 us -> 7.87 us
  Pallas kernels: 631 us -> 653 us
  starting transfers between devices: 28 us -> 15.8 us
    pallas_call x1, Pallas kernels: 109 us -> 168 us  [tail_sums(): pl.pallas_call(functools.partial(tail_kernel, group, held, parts), in_spe...]
    psum x1, waiting for transfers between devices: 45.2 us -> 0.01 us  [per_device(): lax.psum((gshared_wide, gshared_deep), 'expert')]
    pallas_call x1, Pallas kernels: 101 us -> 56.8 us  [per_device(): pl.pallas_call(functools.partial(attend_kernel, experts, capacity), grid=...]
    reduce_scatter x4, waiting for transfers between devices: 25.2 us -> 0.04 us  [scatter(): lax.psum_scatter(value, 'dp', scatter_dimension=dimension, tiled=True)]
    pallas_call x2 -> x1, Pallas kernels: 51.6 us -> 74.4 us  [open_gather(): pl.pallas_call(functools.partial(open_kernel, group, parts, holders // 2,...]
    pallas_call x1, Pallas kernels: 133 us -> 115 us  [per_device(): pl.pallas_call(functools.partial(attend_back_kernel, experts, capacity),...]
    all_to_all x1, starting transfers between devices: 27.5 us -> 15.1 us  [per_device(): cot_slots = exchange(cot_sent)]
  transfers between devices with their start and end apart: 8 -> 8, of which waited for: 2 -> 2; matrix products, arithmetic and copies ran while one was open for 2% -> 1% of each run, Pallas kernels for 81% -> 80%
where the time goes in v6:
time: 730 us; the launch traced here: 725 us
  Pallas kernels  653 us (89%)
  local copies, waits for them, and re-layouts  18.2 us (2%)
  other arithmetic  16.2 us (2%)
  starting transfers between devices  15.8 us (2%)
  between operations  14.5 us (2%)
  waiting for transfers between devices  7.87 us (1%)
    pallas_call x1, Pallas kernels, expert_layer(): pl.pallas_call(functools.partial(expert_kernel, group), in_specs=[in_plac...  187 us
    pallas_call x1, Pallas kernels, tail_sums(): pl.pallas_call(functools.partial(tail_kernel, group, held, parts), in_spe...  168 us
    pallas_call x1, Pallas kernels, per_device(): pl.pallas_call(functools.partial(attend_back_kernel, experts, capacity),...  115 us
    pallas_call x1, Pallas kernels, open_gather(): pl.pallas_call(functools.partial(open_kernel, group, parts, holders // 2,...  74.4 us
    pallas_call x1, Pallas kernels, per_device(): pl.pallas_call(functools.partial(attend_kernel, experts, capacity), grid=...  56.8 us
    pallas_call x1, Pallas kernels, mlp(): pl.pallas_call(mlp_kernel, grid=(count // tile,), in_specs=[by_row(width)...  29.9 us
    all_to_all x1, starting transfers between devices, per_device(): cot_slots = exchange(cot_sent)  15.1 us
    pallas_call x1, Pallas kernels, mlp_weights(): pl.pallas_call(mlp_weights_kernel, grid=(ff // tile,), in_specs=[whole((c...  14.6 us
  transfers between devices with their start and end apart: 8, of which 2 were waited for; matrix products, arithmetic and copies ran while one was open for 1% of the time, Pallas kernels for 80%

profile of v6, /device:TPU:0, one launch (start us, length us, event | category | flops | bytes accessed | tf_op | source)
XLA Modules:
  0.0 725.4 jit_solution(17808359686512108249)
XLA Ops:
  10.0 2.7 pad_maximum_fusion
  12.7 74.4 %shard_map.289 = (bf16[3,1024,768]{2,1,0:T(8,128)(2,1)}, s32[8,3,2,256]{3,2,1,0:T(2,128)}, bf16[768,3200]{1,0:T(8,128)(2,1)}, bf16[2048,768]{1,0:T(8,128)(2,1)},...) custom-call(bf16[3,256,768]{2,1,0:T(8,128)(2,1)} %own_ref.3, s32[3,2,256]{2,1,0:T(2,128)} %bitcast.29, ...), custom_call_target="tpu_custom_call" | custom-call | tf_op jit(solution)/shard_map/pallas_call | solution.py:918
  87.8 15.1 %all-to-all-start = ((bf16[8,3,128,768]{3,2,1,0:T(8,128)(2,1)}), bf16[8,3,128,768]{3,2,1,0:T(8,128)(2,1)}, u32[]{:S(2)}, u32[]{:S(2)}) async-start(bf16[8,3,128,768]{3,2,1,0:T(8,128)(2,1)} %get-tuple-element.98), calls=%async_computation | async-start | bytes 9437184 | tf_op jit(solution)/shard_map/all_to_all | solution.py:1571
  103.8 1.7 constant_dynamic-slice_fusion
  105.6 1.2 fusion.9.bias_p
  106.7 56.8 %shard_map.290 = (bf16[8,3,128,768]{3,2,1,0:T(8,128)(2,1)}, bf16[3,256,768]{2,1,0:T(8,128)(2,1)}, f32[3,256,768]{2,1,0:T(8,128)}, bf16[3,256,768]{2,1,0:T(8,128)...) custom-call(bf16[3,256,768]{2,1,0:T(8,128)(2,1)} %own_ref.3, ...), custom_call_target="tpu_custom_call" | custom-call | flops 1 | bytes 1 | tf_op jit(solution)/shard_map/pallas_call | solution.py:1599
  163.6 29.9 %shard_map.291 = (f32[768,768]{1,0:T(8,128)}, bf16[768,768]{1,0:T(8,128)(2,1)}, bf16[768,2048]{1,0:T(8,128)(2,1)}, bf16[2,768,2048]{2,1,0:T(8,128)(2,1)}) custom-call(bf16[768,768]{1,0:T(8,128)(2,1)} %bitcast.20, bf16[768,768]{1,0:T(8,128)(2,1)} %bitcast.18, bf16[768,4096]{1,0:T(8,128)(2,1)} %get-tuple-element.81.wide_ref, ...), custom_call_target="tpu_custom_call" | custom-call | flops 1 | bytes 1 | tf_op jit(solution)/shard_map/pallas_call | solution.py:264
  193.5 14.6 %shard_map.292 = (bf16[2,768,2048]{2,1,0:T(8,128)(2,1)}, bf16[2048,768]{1,0:T(8,128)(2,1)}) custom-call(bf16[768,768]{1,0:T(8,128)(2,1)} %bitcast.21, bf16[768,768]{1,0:T(8,128)(2,1)} %bitcast.19, bf16[768,2048]{1,0:T(8,128)(2,1)} %get-tuple-element.92.hidden_ref, bf16[2,768,2048]{2,1,0:T(8,128)(2,1)} %get-tuple-element.93.dwide_ref), custom_call_target="tpu_custom_call" | custom-call | flops 1 | bytes 1 | tf_op jit(solution)/shard_map/pallas_call | solution.py:309
  208.3 5.8 all-gather.3.cloned.1.call-done.wide_ref
  215.5 186.6 %shard_map.293 = (bf16[8,3,128,768]{3,2,1,0:T(8,128)(2,1)}, bf16[8,3,128,768]{3,2,1,0:T(8,128)(2,1)}, bf16[2,768,2048]{2,1,0:T(8,128)(2,1)}, bf16[2048,768]{1,0:T(8,128)(2,1)}, f32[768,128]{1,0:T(8,128)}) custom-call(bf16[8,3,128,768]{3,2,1,0:T(8,128)(2,1)} %get-tuple-element.91.sent_ref, bf16[8,3,128,768]{3,2,1,0:T(8,128)(2,1)} %all-to-all-done.cot_hbm, ...), custom_call_target="tpu_custom_call" | custom-call | flops 1 | bytes 1 | tf_op jit(solution)/shard_map/pallas_call | solution.py:1441
  402.8 115.4 %shard_map.294 = (f32[3,256,768]{2,1,0:T(8,128)}, f32[3,256,768]{2,1,0:T(8,128)}, bf16[3,1024,768]{2,1,0:T(8,128)(2,1)}, bf16[768,3200]{1,0:T(8,128)(2,1)}, bf16[8,3,128,768]{3,2,1,0:T(8,128)(2,1)}) custom-call(bf16[3,256,768]{2,1,0:T(8,128)(2,1)} %own_ref.3, bf16[3,1024,768]{2,1,0:T(8,128)(2,1)} %get-tuple-element.77.prompt_ref, s32[3,2,256]{2,1,0:T(2,128)} %bitcast.31, ...), custom_call_target="tpu_custom_call" | custom-call | flops 1 | bytes 1 | tf_op jit(solution)/shard_map/pallas_call | solution.py:1660
  519.8 7.2 shard_map.295
  527.0 167.9 %shard_map.296 = (bf16[3,256,768]{2,1,0:T(8,128)(2,1)}, bf16[2,4,24,3200]{3,2,1,0:T(8,128)(2,1)}) custom-call(bf16[3,1024,768]{2,1,0:T(8,128)(2,1)} %get-tuple-element.115.part_ref, bf16[768,3200]{1,0:T(8,128)(2,1)} %get-tuple-element.116.grads_ref), custom_call_target="tpu_custom_call" | custom-call | tf_op jit(solution)/shard_map/pallas_call | solution.py:1183
  695.0 1.5 slice.56
  696.5 1.5 copy.41
  698.0 2.3 fusion.13
  700.3 1.3 fusion.14
  701.6 1.3 slice.59
  703.0 2.0 fusion.2
  708.5 1.3 convert_element_type.61
  709.7 1.3 bitcast_convert_fusion
  711.4 1.9 slice_bitcast_fusion
  713.4 2.0 fusion.12
  716.6 1.8 fusion.6
  (65 shorter events, 13.3 us)
Async XLA Ops:
  7.2 200.9 %all-gather.5.cloned.1.call-start = ((), (), s32[]{:S(2)}) async-start(), calls=%async_computation.6 | async-start | bytes 3932160 | tf_op jit(solution)/shard_map/all_gather | solution.py:1539
  87.1 127.0 %all-gather.3.cloned.1.call-start = ((), (), s32[]{:S(2)}) async-start(), calls=%async_computation.5 | async-start | bytes 7864320 | tf_op jit(solution)/shard_map/all_gather | solution.py:1540
  87.8 120.5 %all-to-all-start = ((bf16[8,3,128,768]{3,2,1,0:T(8,128)(2,1)}), bf16[8,3,128,768]{3,2,1,0:T(8,128)(2,1)}, u32[]{:S(2)}, u32[]{:S(2)}) async-start(bf16[8,3,128,768]{3,2,1,0:T(8,128)(2,1)} %get-tuple-element.98), calls=%async_computation | async-start | bytes 9437184 | tf_op jit(solution)/shard_map/all_to_all | solution.py:1571
  103.0 415.3 %reduce-scatter.5.cloned.1.call-start = ((), (), s32[]{:S(2)}) async-start(), calls=%async_computation.7 | async-start | bytes 3932160 | tf_op jit(solution)/shard_map/reduce_scatter | solution.py:1648
  214.1 304.2 %reduce-scatter.7.cloned.1.call-start = ((), (), s32[]{:S(2)}) async-start(), calls=%async_computation.8 | async-start | bytes 7864320 | tf_op jit(solution)/shard_map/reduce_scatter | solution.py:1648
  214.7 485.6 %reduce-scatter.9.cloned.1.call-start = ((), (), s32[]{:S(2)}) async-start(), calls=%async_computation.9 | async-start | bytes 3932160 | tf_op jit(solution)/shard_map/reduce_scatter | solution.py:1648
  402.2 298.1 %reduce-scatter.11.cloned.1.call-start = ((), (), s32[]{:S(2)}) async-start(), calls=%async_computation.10 | async-start | bytes 7864320 | tf_op jit(solution)/shard_map/reduce_scatter | solution.py:1648
  402.7 297.6 %all-reduce.4.cloned.1.call-start = ((), (), s32[]{:S(2)}) async-start(), calls=%async_computation.11 | async-start | bytes 4718592 | tf_op jit(solution)/shard_map/psum | solution.py:1736
  518.2 1.3 copy-start
  527.0 175.9 %copy-start.2 = (f32[3,256,768]{2,1,0:T(8,128)S(1)}, f32[3,256,768]{2,1,0:T(8,128)}, u32[]{:S(2)}) copy-start(f32[3,256,768]{2,1,0:T(8,128)} %get-tuple-element.114) | copy-start | bytes 7077892
  695.0 8.0 %copy-start.1 = (bf16[3,256,768]{2,1,0:T(8,128)(2,1)S(1)}, bf16[3,256,768]{2,1,0:T(8,128)(2,1)}, u32[]{:S(2)}) copy-start(bf16[3,256,768]{2,1,0:T(8,128)(2,1)} %own_ref.3) | copy-start | bytes 3538948
  702.9 2.1 copy-start.10
  702.9 3.0 copy-start.9
  702.9 3.8 copy-start.8
  705.0 2.6 copy-start.7
  705.0 3.5 copy-start.12
  705.9 3.8 copy-start.11
  708.5 2.5 copy-start.6
  711.4 2.0 copy-start.3
  713.4 2.0 copy-start.4
  713.4 3.2 copy-start.5
Sparse Core Ops, SparseCore 0:
  87.2 54.3 all-gather.4
  144.0 70.0 all-gather.2
  217.1 43.9 reduce-scatter.4
  263.9 70.0 reduce-scatter.6
  402.3 67.2 reduce-scatter.8
  472.4 70.0 reduce-scatter.10
  545.0 100.4 all-reduce.3

commit v7 on v6

--- a/solution.py
+++ b/solution.py
@@ -527,13 +527,6 @@
             arrived(k).wait_recv()
 
 
-def finish_kernel(experts, capacity, resid_ref, shared_ref, slots_ref, route_ref, out_ref):
-    ranks = slot_ranks(route_ref[0], experts)
-    out_ref[0] = (
-        resid_ref[0] + shared_ref[0] + gather_slots(ranks, slots_ref, experts, capacity)
-    ).astype(low)
-
-
 def chip_place():
     me = lax.axis_index("expert")
     return me // 2, me % 2
@@ -615,8 +608,8 @@
             (1, above, above < self.holders),
         )
 
-    def step(self, d):
-        for m in range(self.batches):
+    def step(self, d, some=None):
+        for m in range(self.batches) if some is None else some:
             for way, chip, there in self.cases(d):
 
                 @pl.when(there)
@@ -753,12 +746,8 @@
 
     def own(self):
         at = pl.multiple_of(self.here * self.rows, self.rows)
-        return remote(
-            self.source,
-            self.target.at[pl.ds(at, self.rows), :],
-            self.give.at[0],
-            self.take.at[0],
-            self.partner,
+        return pltpu.make_async_copy(
+            self.source, self.target.at[pl.ds(at, self.rows), :], self.give.at[0]
         )
 
     def relay(self, k):
@@ -803,8 +792,7 @@
         if self.square:
             for k in (3, 4):
                 self.arrive(k)
-        self.own().wait_send()
-        self.own().wait_recv()
+        self.own().wait()
         for k in self.direct():
             self.spread(k).wait_send()
             if self.square:
@@ -878,14 +866,18 @@
     keep_routes.start()
     spreads[0].forward()
     chain.step(1)
+    spreads[1].forward()
+    if group > 4:
+        chain.step(2, range(1))
+    spreads[2].forward()
+    if group > 4:
+        chain.step(2, range(1, cot_ref.shape[0]))
+    for d in range(3, group // 2):
+        chain.step(d)
     for m in range(cot_ref.shape[0]):
         ranks = slot_ranks(route_ref[m], group)
         for e in range(group):
             cot_slots[e, m] = mm(placement(ranks, e, capacity), cot_ref[m]).astype(low)
-    spreads[1].forward()
-    spreads[2].forward()
-    for d in range(2, group // 2):
-        chain.step(d)
     for spread in spreads:
         spread.finish()
     for k in range(1, group):
@@ -945,8 +937,14 @@
     parts,
     part_ref,
     grads_ref,
+    resid_hbm,
+    shared_hbm,
+    slots_hbm,
+    route_ref,
     sum_ref,
     gsum_ref,
+    output_ref,
+    narrow_ref,
     take,
     above,
     below,
@@ -955,10 +953,19 @@
     across,
     mine_z,
     along,
+    resid_v,
+    shared_v,
+    slots_v,
     *sems,
 ):
+    load_s = sems[-1]
+    loads = [
+        pltpu.make_async_copy(resid_hbm, resid_v, load_s.at[0]),
+        pltpu.make_async_copy(shared_hbm, shared_v, load_s.at[1]),
+        pltpu.make_async_copy(slots_hbm, slots_v, load_s.at[2]),
+    ]
     give_s, take_s, send_s, above_s, below_s = sems[:5]
-    pgive_s, ptake_s, xsend_s, xrecv_s, zsend_s, zrecv_s, asend_s, arecv_s, hgive_s, htake_s = sems[5:]
+    pgive_s, ptake_s, xsend_s, xrecv_s, zsend_s, zrecv_s, asend_s, arecv_s, hgive_s, htake_s = sems[5:15]
     chips = group // 2
     z, core = chip_place()
     here_dp = lax.axis_index("dp")
@@ -1052,6 +1059,16 @@
     for m, chip in chunks:
         if chip:
             give(m, chip).start()
+    for load in loads:
+        load.start()
+    for load in loads:
+        load.wait()
+    for m in range(batches):
+        ranks = slot_ranks(route_ref[m], group)
+        slots = slots_v.at[:, m : m + 1]
+        output_ref[m] = (
+            resid_v[m] + shared_v[m] + gather_slots(ranks, slots, group, slots.shape[2])
+        ).astype(low)
 
     @pl.when(z >= holders)
     def _():
@@ -1168,9 +1185,12 @@
         hand(j, 1 - core).wait_recv()
         if j:
             whole_z(j).wait_send()
-
-
-def tail_sums(part, grads, group, holders, tok, parts):
+    width = part_ref.shape[2]
+    narrow = [gsum_ref[c, q, :, 4 * width :].astype(f32) for c in range(2) for q in range(chips)]
+    narrow_ref[...] = jnp.concatenate(narrow, axis=0).T[: narrow_ref.shape[0]]
+
+
+def tail_sums(part, grads, resid, shared, slots, routes, group, holders, tok, parts):
     batches, _, width = part.shape
     rows, columns = grads.shape
     chips = group // 2
@@ -1180,25 +1200,33 @@
     halves = pltpu.VMEM((parts, half, columns), low)
     quarters = pltpu.VMEM((chips, half // chips, columns), low)
     dma = pltpu.SemaphoreType.DMA
-    summed, gsum = pl.pallas_call(
+    summed, gsum, output, narrow = pl.pallas_call(
         functools.partial(tail_kernel, group, held, parts),
-        in_specs=[vmem(), vmem()],
-        out_specs=[vmem(), vmem()],
+        in_specs=[vmem(), vmem(), in_place(), in_place(), in_place(), vmem()],
+        out_specs=[vmem()] * 4,
         out_shape=[
             jax.ShapeDtypeStruct((batches, tok, width), low),
             jax.ShapeDtypeStruct((2, chips, half // chips, columns), low),
+            jax.ShapeDtypeStruct((batches, tok, width), low),
+            jax.ShapeDtypeStruct((32, rows // parts), f32),
         ],
         scratch_shapes=[block] * 4
         + [halves] * 2
         + [quarters] * 2
+        + [
+            pltpu.VMEM((batches, tok, width), f32),
+            pltpu.VMEM((batches, tok, width), f32),
+            pltpu.VMEM(slots.shape, low),
+        ]
         + [dma((held, batches))] * 5
         + [dma((parts,))] * 4
-        + [dma((chips,))] * 6,
+        + [dma((chips,))] * 6
+        + [dma((3,))],
         compiler_params=pltpu.CompilerParams(
             collective_id=2, has_side_effects=True, vmem_limit_bytes=56_000_000
         ),
-    )(part, grads)
-    return summed, gsum.reshape(rows // parts, columns)
+    )(part, grads, resid, shared, slots, routes)
+    return summed, gsum.reshape(rows // parts, columns), output, narrow
 
 
 def opposite(me, k, group):
@@ -1734,25 +1762,26 @@
         (gshared_deep, gshared_wide, gattn)
     )
     gshared_wide, gshared_deep = lax.psum((gshared_wide, gshared_deep), "expert")
-    output = pl.pallas_call(
-        functools.partial(finish_kernel, experts, capacity),
-        grid=(batches,),
-        in_specs=[row_spec, row_spec, slots_spec, route_spec],
-        out_specs=row_spec,
-        out_shape=jax.ShapeDtypeStruct(rows_shape, low),
-        compiler_params=params(),
-    )(resid, shared_y.reshape(rows_shape), y_back, route_rows)
-
-    output, dprompt, gattn = lax.optimization_barrier((output, dprompt, gattn))
-    dnorm_prompt, gattn = tail_sums(dprompt, gattn, group, holders, tok, parts)
+    dnorm_prompt, gattn, output, narrow = tail_sums(
+        dprompt,
+        gattn,
+        resid,
+        shared_y.reshape(rows_shape),
+        y_back,
+        route_rows,
+        group,
+        holders,
+        tok,
+        parts,
+    )
     at = 4 * width
-    pieces = [gattn[:, j : j + width] for j in range(0, at, width)] + [gattn[:, at:]]
+    pieces = [gattn[:, j : j + width] for j in range(0, at, width)]
     dnorm_prompt, pieces, gexpert_deep, gexpert_wide, gshared_wide, gshared_deep = (
         lax.optimization_barrier(
             (dnorm_prompt, pieces, gexpert_deep, gexpert_wide, gshared_wide, gshared_deep)
         )
     )
-    gquery, gkey, gvalue, gout, gsmall = (piece.astype(f32) for piece in pieces)
+    gquery, gkey, gvalue, gout = (piece.astype(f32) for piece in pieces)
     dnorm = dnorm_own + dnorm_prompt.astype(f32)
     own = tokens.astype(f32)
     inverse = inverse_rms(own)
@@ -1767,13 +1796,13 @@
     return (
         output,
         input_grad,
-        gsmall[:, 0],
+        narrow[0],
         gquery,
         gkey,
         gvalue,
         gout,
-        gsmall[:, 1],
-        gsmall[:, ROUTER_AT : ROUTER_AT + experts],
+        narrow[1],
+        narrow[ROUTER_AT : ROUTER_AT + experts].T,
         gshared_wide[0],
         gshared_wide[1],
         gshared_deep,

time: 730 us -> 728 us (level)
    pallas_call x1, Pallas kernels: 168 us -> 176 us  [tail_sums(): pl.pallas_call(functools.partial(tail_kernel, group, held, parts), in_spe...]
where the time goes in v7:
time: 728 us; the launch traced here: 724 us
  Pallas kernels  653 us (90%)
  starting transfers between devices  17.1 us (2%)
  other arithmetic  16.2 us (2%)
  local copies, waits for them, and re-layouts  14.7 us (2%)
  between operations  14.6 us (2%)
  waiting for transfers between devices  7.99 us (1%)
    pallas_call x1, Pallas kernels, expert_layer(): pl.pallas_call(functools.partial(expert_kernel, group), in_specs=[in_plac...  187 us
    pallas_call x1, Pallas kernels, tail_sums(): pl.pallas_call(functools.partial(tail_kernel, group, held, parts), in_spe...  176 us
    pallas_call x1, Pallas kernels, per_device(): pl.pallas_call(functools.partial(attend_back_kernel, experts, capacity),...  115 us
    pallas_call x1, Pallas kernels, open_gather(): pl.pallas_call(functools.partial(open_kernel, group, parts, holders // 2,...  74.3 us
    pallas_call x1, Pallas kernels, per_device(): pl.pallas_call(functools.partial(attend_kernel, experts, capacity), grid=...  56.8 us
    pallas_call x1, Pallas kernels, mlp(): pl.pallas_call(mlp_kernel, grid=(count // tile,), in_specs=[by_row(width)...  29.8 us
    all_to_all x1, starting transfers between devices, per_device(): cot_slots = exchange(cot_sent)  16.4 us
    pallas_call x1, Pallas kernels, mlp_weights(): pl.pallas_call(mlp_weights_kernel, grid=(ff // tile,), in_specs=[whole((c...  14.6 us
  transfers between devices with their start and end apart: 8, of which 2 were waited for; matrix products, arithmetic and copies ran while one was open for 1% of the time, Pallas kernels for 80%

profile of v7, /device:TPU:0, one launch (start us, length us, event | category | flops | bytes accessed | tf_op | source)
XLA Modules:
  0.0 723.9 jit_solution(17126582731179443758)
XLA Ops:
  10.0 2.7 pad_maximum_fusion
  12.7 74.3 %shard_map.289 = (bf16[3,1024,768]{2,1,0:T(8,128)(2,1)}, s32[8,3,2,256]{3,2,1,0:T(2,128)}, bf16[768,3200]{1,0:T(8,128)(2,1)}, bf16[2048,768]{1,0:T(8,128)(2,1)},...) custom-call(bf16[3,256,768]{2,1,0:T(8,128)(2,1)} %own_ref.3, s32[3,2,256]{2,1,0:T(2,128)} %bitcast.20, ...), custom_call_target="tpu_custom_call" | custom-call | tf_op jit(solution)/shard_map/pallas_call | solution.py:910
  87.8 16.4 %all-to-all-start = ((bf16[8,3,128,768]{3,2,1,0:T(8,128)(2,1)}), bf16[8,3,128,768]{3,2,1,0:T(8,128)(2,1)}, u32[]{:S(2)}, u32[]{:S(2)}) async-start(bf16[8,3,128,768]{3,2,1,0:T(8,128)(2,1)} %get-tuple-element.95), calls=%async_computation | async-start | bytes 9437184 | tf_op jit(solution)/shard_map/all_to_all | solution.py:1599
  105.1 1.7 constant_dynamic-slice_fusion
  106.8 1.2 fusion.9.bias_p
  108.0 56.8 %shard_map.290 = (bf16[8,3,128,768]{3,2,1,0:T(8,128)(2,1)}, bf16[3,256,768]{2,1,0:T(8,128)(2,1)}, f32[3,256,768]{2,1,0:T(8,128)}, bf16[3,256,768]{2,1,0:T(8,128)...) custom-call(bf16[3,256,768]{2,1,0:T(8,128)(2,1)} %own_ref.3, ...), custom_call_target="tpu_custom_call" | custom-call | flops 1 | bytes 1 | tf_op jit(solution)/shard_map/pallas_call | solution.py:1627
  164.8 29.8 %shard_map.291 = (f32[768,768]{1,0:T(8,128)}, bf16[768,768]{1,0:T(8,128)(2,1)}, bf16[768,2048]{1,0:T(8,128)(2,1)}, bf16[2,768,2048]{2,1,0:T(8,128)(2,1)}) custom-call(bf16[768,768]{1,0:T(8,128)(2,1)} %bitcast.26, bf16[768,768]{1,0:T(8,128)(2,1)} %bitcast.24, bf16[768,4096]{1,0:T(8,128)(2,1)} %get-tuple-element.85.wide_ref, ...), custom_call_target="tpu_custom_call" | custom-call | flops 1 | bytes 1 | tf_op jit(solution)/shard_map/pallas_call | solution.py:264
  194.6 14.6 %shard_map.292 = (bf16[2,768,2048]{2,1,0:T(8,128)(2,1)}, bf16[2048,768]{1,0:T(8,128)(2,1)}) custom-call(bf16[768,768]{1,0:T(8,128)(2,1)} %bitcast.27, bf16[768,768]{1,0:T(8,128)(2,1)} %bitcast.25, bf16[768,2048]{1,0:T(8,128)(2,1)} %get-tuple-element.89.hidden_ref, bf16[2,768,2048]{2,1,0:T(8,128)(2,1)} %get-tuple-element.90.dwide_ref), custom_call_target="tpu_custom_call" | custom-call | flops 1 | bytes 1 | tf_op jit(solution)/shard_map/pallas_call | solution.py:309
  209.5 5.8 all-gather.3.cloned.1.call-done.wide_ref
  216.8 186.5 %shard_map.293 = (bf16[8,3,128,768]{3,2,1,0:T(8,128)(2,1)}, bf16[8,3,128,768]{3,2,1,0:T(8,128)(2,1)}, bf16[2,768,2048]{2,1,0:T(8,128)(2,1)}, bf16[2048,768]{1,0:T(8,128)(2,1)}, f32[768,128]{1,0:T(8,128)}) custom-call(bf16[8,3,128,768]{3,2,1,0:T(8,128)(2,1)} %get-tuple-element.88.sent_ref, bf16[8,3,128,768]{3,2,1,0:T(8,128)(2,1)} %all-to-all-done.cot_hbm, ...), custom_call_target="tpu_custom_call" | custom-call | flops 1 | bytes 1 | tf_op jit(solution)/shard_map/pallas_call | solution.py:1469
  404.0 115.5 %shard_map.294 = (f32[3,256,768]{2,1,0:T(8,128)}, f32[3,256,768]{2,1,0:T(8,128)}, bf16[3,1024,768]{2,1,0:T(8,128)(2,1)}, bf16[768,3200]{1,0:T(8,128)(2,1)}, bf16[8,3,128,768]{3,2,1,0:T(8,128)(2,1)}) custom-call(bf16[3,256,768]{2,1,0:T(8,128)(2,1)} %own_ref.3, bf16[3,1024,768]{2,1,0:T(8,128)(2,1)} %get-tuple-element.75.prompt_ref, s32[3,2,256]{2,1,0:T(2,128)} %bitcast.22, ...), custom_call_target="tpu_custom_call" | custom-call | flops 1 | bytes 1 | tf_op jit(solution)/shard_map/pallas_call | solution.py:1688
  521.1 175.8 %shard_map.295 = (bf16[3,256,768]{2,1,0:T(8,128)(2,1)}, bf16[2,4,24,3200]{3,2,1,0:T(8,128)(2,1)}, bf16[3,256,768]{2,1,0:T(8,128)(2,1)}, f32[32,192]{1,0:T(8,128)S(1)}) custom-call(bf16[3,1024,768]{2,1,0:T(8,128)(2,1)} %get-tuple-element.103.part_ref, bf16[768,3200]{1,0:T(8,128)(2,1)} %get-tuple-element.107.grads_ref, ...), custom_call_target="tpu_custom_call" | custom-call | tf_op jit(solution)/shard_map/pallas_call | solution.py:1203
  698.1 2.3 fusion.13
  700.4 2.0 fusion.2
  702.5 0.9 convert_element_type.52
  703.3 0.9 convert_element_type.53
  705.1 0.9 convert_element_type.55
  705.9 1.3 convert_element_type.57
  707.2 1.3 bitcast_convert_fusion
  708.8 1.9 slice_bitcast_fusion
  710.9 2.0 fusion.12
  712.9 1.1 copy-done.5
  714.0 1.8 fusion.6
  715.9 1.0 copy.41
  (65 shorter events, 10.9 us)
Async XLA Ops:
  7.2 202.1 %all-gather.5.cloned.1.call-start = ((), (), s32[]{:S(2)}) async-start(), calls=%async_computation.6 | async-start | bytes 3932160 | tf_op jit(solution)/shard_map/all_gather | solution.py:1567
  87.0 128.3 %all-gather.3.cloned.1.call-start = ((), (), s32[]{:S(2)}) async-start(), calls=%async_computation.5 | async-start | bytes 7864320 | tf_op jit(solution)/shard_map/all_gather | solution.py:1568
  87.8 121.7 %all-to-all-start = ((bf16[8,3,128,768]{3,2,1,0:T(8,128)(2,1)}), bf16[8,3,128,768]{3,2,1,0:T(8,128)(2,1)}, u32[]{:S(2)}, u32[]{:S(2)}) async-start(bf16[8,3,128,768]{3,2,1,0:T(8,128)(2,1)} %get-tuple-element.95), calls=%async_computation | async-start | bytes 9437184 | tf_op jit(solution)/shard_map/all_to_all | solution.py:1599
  104.2 415.3 %reduce-scatter.5.cloned.1.call-start = ((), (), s32[]{:S(2)}) async-start(), calls=%async_computation.7 | async-start | bytes 3932160 | tf_op jit(solution)/shard_map/reduce_scatter | solution.py:1676
  215.4 304.2 %reduce-scatter.7.cloned.1.call-start = ((), (), s32[]{:S(2)}) async-start(), calls=%async_computation.8 | async-start | bytes 7864320 | tf_op jit(solution)/shard_map/reduce_scatter | solution.py:1676
  216.0 484.4 %reduce-scatter.9.cloned.1.call-start = ((), (), s32[]{:S(2)}) async-start(), calls=%async_computation.9 | async-start | bytes 3932160 | tf_op jit(solution)/shard_map/reduce_scatter | solution.py:1676
  403.4 297.0 %reduce-scatter.11.cloned.1.call-start = ((), (), s32[]{:S(2)}) async-start(), calls=%async_computation.10 | async-start | bytes 7864320 | tf_op jit(solution)/shard_map/reduce_scatter | solution.py:1676
  404.0 296.4 %all-reduce.4.cloned.1.call-start = ((), (), s32[]{:S(2)}) async-start(), calls=%async_computation.11 | async-start | bytes 4718592 | tf_op jit(solution)/shard_map/psum | solution.py:1764
  519.5 1.3 copy-start.1
  519.5 1.6 copy-start
  696.9 3.5 copy-start.2
  700.4 2.1 copy-start.10
  700.4 3.0 copy-start.9
  700.4 3.8 copy-start.8
  702.5 2.6 copy-start.7
  702.5 3.5 copy-start.13
  703.3 3.8 copy-start.12
  705.9 2.5 copy-start.6
  708.8 2.0 copy-start.3
  710.9 2.0 copy-start.4
  710.9 3.2 copy-start.5
  714.0 1.8 copy-start.11
Sparse Core Ops, SparseCore 0:
  87.2 55.6 all-gather.4
  145.3 70.0 all-gather.2
  218.4 43.8 reduce-scatter.4
  265.1 70.0 reduce-scatter.6
  403.5 67.2 reduce-scatter.8
  473.7 70.0 reduce-scatter.10
  546.2 102.0 all-reduce.3

commit v8 on v7

--- a/solution.py
+++ b/solution.py
@@ -864,8 +864,8 @@
     for k in range(1, group):
         routed(k).start()
     keep_routes.start()
+    chain.step(1)
     spreads[0].forward()
-    chain.step(1)
     spreads[1].forward()
     if group > 4:
         chain.step(2, range(1))

time: 728 us -> 725 us (level)
  no operation moved by 1% of the time
where the time goes in v8:
time: 725 us; the launch traced here: 721 us
  Pallas kernels  654 us (90%)
  other arithmetic  16.2 us (2%)
  local copies, waits for them, and re-layouts  14.6 us (2%)
  between operations  14.6 us (2%)
  starting transfers between devices  12.8 us (2%)
  waiting for transfers between devices  8.78 us (1%)
    pallas_call x1, Pallas kernels, expert_layer(): pl.pallas_call(functools.partial(expert_kernel, group), in_specs=[in_plac...  187 us
    pallas_call x1, Pallas kernels, tail_sums(): pl.pallas_call(functools.partial(tail_kernel, group, held, parts), in_spe...  176 us
    pallas_call x1, Pallas kernels, per_device(): pl.pallas_call(functools.partial(attend_back_kernel, experts, capacity),...  115 us
    pallas_call x1, Pallas kernels, open_gather(): pl.pallas_call(functools.partial(open_kernel, group, parts, holders // 2,...  74.3 us
    pallas_call x1, Pallas kernels, per_device(): pl.pallas_call(functools.partial(attend_kernel, experts, capacity), grid=...  57.1 us
    pallas_call x1, Pallas kernels, mlp(): pl.pallas_call(mlp_kernel, grid=(count // tile,), in_specs=[by_row(width)...  29.8 us
    pallas_call x1, Pallas kernels, mlp_weights(): pl.pallas_call(mlp_weights_kernel, grid=(ff // tile,), in_specs=[whole((c...  14.6 us
  transfers between devices with their start and end apart: 8, of which 2 were waited for; matrix products, arithmetic and copies ran while one was open for 1% of the time, Pallas kernels for 80%

profile of v8, /device:TPU:0, one launch (start us, length us, event | category | flops | bytes accessed | tf_op | source)
XLA Modules:
  0.0 720.6 jit_solution(7296799262324467796)
XLA Ops:
  10.0 2.7 pad_maximum_fusion
  12.7 74.3 %shard_map.289 = (bf16[3,1024,768]{2,1,0:T(8,128)(2,1)}, s32[8,3,2,256]{3,2,1,0:T(2,128)}, bf16[768,3200]{1,0:T(8,128)(2,1)}, bf16[2048,768]{1,0:T(8,128)(2,1)},...) custom-call(bf16[3,256,768]{2,1,0:T(8,128)(2,1)} %own_ref.3, s32[3,2,256]{2,1,0:T(2,128)} %bitcast.20, ...), custom_call_target="tpu_custom_call" | custom-call | tf_op jit(solution)/shard_map/pallas_call | solution.py:910
  87.8 12.1 %all-to-all-start = ((bf16[8,3,128,768]{3,2,1,0:T(8,128)(2,1)}), bf16[8,3,128,768]{3,2,1,0:T(8,128)(2,1)}, u32[]{:S(2)}, u32[]{:S(2)}) async-start(bf16[8,3,128,768]{3,2,1,0:T(8,128)(2,1)} %get-tuple-element.95), calls=%async_computation | async-start | bytes 9437184 | tf_op jit(solution)/shard_map/all_to_all | solution.py:1599
  100.8 1.7 constant_dynamic-slice_fusion
  102.5 1.2 fusion.9.bias_p
  103.7 57.1 %shard_map.290 = (bf16[8,3,128,768]{3,2,1,0:T(8,128)(2,1)}, bf16[3,256,768]{2,1,0:T(8,128)(2,1)}, f32[3,256,768]{2,1,0:T(8,128)}, bf16[3,256,768]{2,1,0:T(8,128)...) custom-call(bf16[3,256,768]{2,1,0:T(8,128)(2,1)} %own_ref.3, ...), custom_call_target="tpu_custom_call" | custom-call | flops 1 | bytes 1 | tf_op jit(solution)/shard_map/pallas_call | solution.py:1627
  160.7 29.8 %shard_map.291 = (f32[768,768]{1,0:T(8,128)}, bf16[768,768]{1,0:T(8,128)(2,1)}, bf16[768,2048]{1,0:T(8,128)(2,1)}, bf16[2,768,2048]{2,1,0:T(8,128)(2,1)}) custom-call(bf16[768,768]{1,0:T(8,128)(2,1)} %bitcast.26, bf16[768,768]{1,0:T(8,128)(2,1)} %bitcast.24, bf16[768,4096]{1,0:T(8,128)(2,1)} %get-tuple-element.85.wide_ref, ...), custom_call_target="tpu_custom_call" | custom-call | flops 1 | bytes 1 | tf_op jit(solution)/shard_map/pallas_call | solution.py:264
  190.5 14.6 %shard_map.292 = (bf16[2,768,2048]{2,1,0:T(8,128)(2,1)}, bf16[2048,768]{1,0:T(8,128)(2,1)}) custom-call(bf16[768,768]{1,0:T(8,128)(2,1)} %bitcast.27, bf16[768,768]{1,0:T(8,128)(2,1)} %bitcast.25, bf16[768,2048]{1,0:T(8,128)(2,1)} %get-tuple-element.89.hidden_ref, bf16[2,768,2048]{2,1,0:T(8,128)(2,1)} %get-tuple-element.90.dwide_ref), custom_call_target="tpu_custom_call" | custom-call | flops 1 | bytes 1 | tf_op jit(solution)/shard_map/pallas_call | solution.py:309
  205.2 6.8 all-gather.3.cloned.1.call-done.wide_ref
  213.5 186.5 %shard_map.293 = (bf16[8,3,128,768]{3,2,1,0:T(8,128)(2,1)}, bf16[8,3,128,768]{3,2,1,0:T(8,128)(2,1)}, bf16[2,768,2048]{2,1,0:T(8,128)(2,1)}, bf16[2048,768]{1,0:T(8,128)(2,1)}, f32[768,128]{1,0:T(8,128)}) custom-call(bf16[8,3,128,768]{3,2,1,0:T(8,128)(2,1)} %get-tuple-element.88.sent_ref, bf16[8,3,128,768]{3,2,1,0:T(8,128)(2,1)} %all-to-all-done.cot_hbm, ...), custom_call_target="tpu_custom_call" | custom-call | flops 1 | bytes 1 | tf_op jit(solution)/shard_map/pallas_call | solution.py:1469
  400.7 115.5 %shard_map.294 = (f32[3,256,768]{2,1,0:T(8,128)}, f32[3,256,768]{2,1,0:T(8,128)}, bf16[3,1024,768]{2,1,0:T(8,128)(2,1)}, bf16[768,3200]{1,0:T(8,128)(2,1)}, bf16[8,3,128,768]{3,2,1,0:T(8,128)(2,1)}) custom-call(bf16[3,256,768]{2,1,0:T(8,128)(2,1)} %own_ref.3, bf16[3,1024,768]{2,1,0:T(8,128)(2,1)} %get-tuple-element.75.prompt_ref, s32[3,2,256]{2,1,0:T(2,128)} %bitcast.22, ...), custom_call_target="tpu_custom_call" | custom-call | flops 1 | bytes 1 | tf_op jit(solution)/shard_map/pallas_call | solution.py:1688
  517.8 175.8 %shard_map.295 = (bf16[3,256,768]{2,1,0:T(8,128)(2,1)}, bf16[2,4,24,3200]{3,2,1,0:T(8,128)(2,1)}, bf16[3,256,768]{2,1,0:T(8,128)(2,1)}, f32[32,192]{1,0:T(8,128)S(1)}) custom-call(bf16[3,1024,768]{2,1,0:T(8,128)(2,1)} %get-tuple-element.103.part_ref, bf16[768,3200]{1,0:T(8,128)(2,1)} %get-tuple-element.107.grads_ref, ...), custom_call_target="tpu_custom_call" | custom-call | tf_op jit(solution)/shard_map/pallas_call | solution.py:1203
  694.8 2.3 fusion.13
  697.1 2.0 fusion.2
  699.2 0.9 convert_element_type.52
  700.0 0.9 convert_element_type.53
  700.9 0.9 convert_element_type.54
  702.6 1.3 convert_element_type.57
  703.8 1.3 bitcast_convert_fusion
  705.5 1.9 slice_bitcast_fusion
  707.5 2.0 fusion.12
  709.6 1.1 copy-done.5
  710.7 1.8 fusion.6
  712.5 1.0 copy.41
  (65 shorter events, 10.7 us)
Async XLA Ops:
  7.2 198.0 %all-gather.5.cloned.1.call-start = ((), (), s32[]{:S(2)}) async-start(), calls=%async_computation.6 | async-start | bytes 3932160 | tf_op jit(solution)/shard_map/all_gather | solution.py:1567
  87.0 125.0 %all-gather.3.cloned.1.call-start = ((), (), s32[]{:S(2)}) async-start(), calls=%async_computation.5 | async-start | bytes 7864320 | tf_op jit(solution)/shard_map/all_gather | solution.py:1568
  87.8 117.5 %all-to-all-start = ((bf16[8,3,128,768]{3,2,1,0:T(8,128)(2,1)}), bf16[8,3,128,768]{3,2,1,0:T(8,128)(2,1)}, u32[]{:S(2)}, u32[]{:S(2)}) async-start(bf16[8,3,128,768]{3,2,1,0:T(8,128)(2,1)} %get-tuple-element.95), calls=%async_computation | async-start | bytes 9437184 | tf_op jit(solution)/shard_map/all_to_all | solution.py:1599
  99.9 416.3 %reduce-scatter.5.cloned.1.call-start = ((), (), s32[]{:S(2)}) async-start(), calls=%async_computation.7 | async-start | bytes 3932160 | tf_op jit(solution)/shard_map/reduce_scatter | solution.py:1676
  212.1 304.1 %reduce-scatter.7.cloned.1.call-start = ((), (), s32[]{:S(2)}) async-start(), calls=%async_computation.8 | async-start | bytes 7864320 | tf_op jit(solution)/shard_map/reduce_scatter | solution.py:1676
  212.7 484.3 %reduce-scatter.9.cloned.1.call-start = ((), (), s32[]{:S(2)}) async-start(), calls=%async_computation.9 | async-start | bytes 3932160 | tf_op jit(solution)/shard_map/reduce_scatter | solution.py:1676
  400.1 297.0 %reduce-scatter.11.cloned.1.call-start = ((), (), s32[]{:S(2)}) async-start(), calls=%async_computation.10 | async-start | bytes 7864320 | tf_op jit(solution)/shard_map/reduce_scatter | solution.py:1676
  400.6 296.4 %all-reduce.4.cloned.1.call-start = ((), (), s32[]{:S(2)}) async-start(), calls=%async_computation.11 | async-start | bytes 4718592 | tf_op jit(solution)/shard_map/psum | solution.py:1764
  516.2 1.3 copy-start.1
  516.2 1.6 copy-start
  693.6 3.5 copy-start.2
  697.0 2.1 copy-start.10
  697.1 3.0 copy-start.9
  697.1 3.8 copy-start.8
  699.1 2.6 copy-start.7
  699.1 3.5 copy-start.13
  700.0 3.8 copy-start.12
  702.6 2.5 copy-start.6
  705.5 2.0 copy-start.3
  707.5 2.0 copy-start.4
  707.5 3.2 copy-start.5
  710.7 1.8 copy-start.11
Sparse Core Ops, SparseCore 0:
  87.2 52.3 all-gather.4
  142.0 70.0 all-gather.2
  215.1 43.8 reduce-scatter.4
  261.8 70.0 reduce-scatter.6
  400.2 67.3 reduce-scatter.8
  470.4 70.0 reduce-scatter.10
  542.9 102.0 all-reduce.3
